TPU v7x, 32 devices: a whole 2x2x4 slice. The times are simulated.
32 devices in a mesh: row: 4 (over z), col: 8 (over y, x, core).
Axes of the slice: x: 2, y: 2, z: 4, core: 2. Of those that a mesh axis runs over, the one named last changes fastest.
Arguments:
- slab_left: bfloat16 [16, 8, 2048, 32], P('row', 'col'), may hold values from -6 to 6
- slab_right: bfloat16 [16, 8, 2048, 32], P('row', 'col'), may hold values from -1 to 1
- slab_ranks: int32 [16, 8], P('row', 'col'), may hold values from 20 to 32
- panel_left: bfloat16 [16, 2048, 32], P('row', 'col'), may hold values from -6 to 6
- panel_right: bfloat16 [16, 2048, 32], P('row', 'col'), may hold values from -0.125 to 0.125
- panel_ranks: int32 [16], P('row'), may hold values from 20 to 32
- inverse_factor: bfloat16 [2048, 2048], P(None, 'col'), may hold values from -2 to 2, as said below
- sketch: bfloat16 [2048, 32], replicated, may hold values from -6 to 6
Outputs:
- new_left: bfloat16 [16, 8, 2048, 32], P('row', 'col')
- new_right: bfloat16 [16, 8, 2048, 32], P('row', 'col')
Inputs may be any that keep to these rules, and one draw needn't show every extreme that they name: `slab_ranks`: number of live columns of a slab tile's factors; columns from that index on are padding. `panel_ranks`: number of live columns of a panel tile's factors; columns from that index on are padding. `inverse_factor`: lower triangular: entries above the diagonal are zero, diagonal entries positive.
All inputs are finite; a program needn't handle non-finite values.
Results may differ from a plain program's by a relative error of at most 0.0073.
Values may be sent and summed in bfloat16 or wider, within the bound.
No kernel may reach another device: no remote copies, remote signals or barrier semaphores. Data moves between devices by JAX's collectives and lax.ppermute only.
A program may use at most 64 MiB of HBM per device.

v0:
```python
import functools
import math

import jax
import jax.numpy as jnp
from jax import lax
from jax.experimental import pallas as pl
from jax.experimental.pallas import tpu as pltpu
from jax.sharding import PartitionSpec as P


highest = lax.Precision.HIGHEST
stacked_precision = lax.Precision.HIGH
shift_rate = 0.01
tiny_shift = 1e-06
factor_scale = 0.5
LANES = 128
F32 = jnp.float32
BF16 = jnp.bfloat16
VMEM = pltpu.VMEM
SMEM = pltpu.SMEM


def spread(block, axis, owner):
    block = jnp.where(lax.axis_index(axis) == owner, block, jnp.zeros_like(block))
    return lax.psum(block, axis)


def product(first_matrix, second_matrix):
    return jnp.matmul(first_matrix, second_matrix, precision=highest)


def stacked_product(first_matrix, second_matrix):
    return jnp.matmul(first_matrix, second_matrix, precision=stacked_precision)


def flipped(matrix):
    return jnp.swapaxes(matrix, -1, -2)


def orthonormal(vectors):
    gram_matrix = product(flipped(vectors), vectors)
    shift_value = (
        shift_rate * jnp.trace(gram_matrix, axis1=-2, axis2=-1) / gram_matrix.shape[-1] + tiny_shift
    )
    identity = jnp.eye(gram_matrix.shape[-1], dtype=gram_matrix.dtype)
    lower_factor = jnp.linalg.cholesky(gram_matrix + shift_value[..., None, None] * identity)
    solved_rows = lax.linalg.triangular_solve(
        lower_factor, flipped(vectors), left_side=True, lower=True
    )
    return flipped(solved_rows)


def recompress(slab_factor, masked_right, row_factor, core_block, column_factor, sketch_float):
    target_shape = core_block.shape[:2] + slab_factor.shape[2:]
    column_wide = jnp.broadcast_to(column_factor[None], target_shape)
    row_core = product(row_factor, core_block)
    column_core = product(column_wide, flipped(core_block))
    forward_left = jnp.concatenate([slab_factor.astype(jnp.float32), -row_core], axis=-1)
    forward_right = jnp.concatenate([masked_right.astype(jnp.float32), column_wide], axis=-1)
    backward_left = jnp.concatenate([masked_right.astype(jnp.float32), -column_core], axis=-1)
    backward_right = jnp.concatenate([slab_factor.astype(jnp.float32), row_factor], axis=-1)

    def forward(vectors):
        return stacked_product(forward_left, stacked_product(flipped(forward_right), vectors))

    def backward(vectors):
        return stacked_product(backward_left, stacked_product(flipped(backward_right), vectors))

    basis_now = orthonormal(forward(sketch_float))
    basis_now = orthonormal(forward(backward(basis_now)))
    projected = backward(basis_now)
    factor_size = factor_scale * math.sqrt(slab_factor.shape[-2])
    return (basis_now * factor_size, projected / factor_size)


def plain_shards(
    slab_left, slab_right, slab_ranks, panel_left, panel_right, panel_ranks, inverse_factor, sketch
):
    rows_total = lax.axis_size("row")
    cols_total = lax.axis_size("col")
    my_row = lax.axis_index("row")
    my_col = lax.axis_index("col")
    tile_rows, piece_rows, rank_width = panel_left.shape
    column_tiles = slab_left.shape[1]
    tile_order = inverse_factor.shape[0]
    panel_keep = jnp.arange(rank_width, dtype=jnp.int32)[None, :] < panel_ranks[:, None]
    masked_panel = jnp.where(panel_keep[:, None, :], panel_right, jnp.zeros((), jnp.bfloat16))
    flat_right = jnp.swapaxes(masked_panel, 0, 1).reshape(piece_rows, tile_rows * rank_width)
    flat_left = jnp.swapaxes(panel_left, 0, 1).reshape(piece_rows, tile_rows * rank_width)
    solved_part = lax.psum_scatter(
        jnp.dot(inverse_factor, flat_right, preferred_element_type=jnp.float32),
        "col",
        scatter_dimension=0,
        tiled=True,
    ).astype(jnp.bfloat16)
    full_left, full_solved = (
        lax.all_gather(flat_left, "col", axis=0, tiled=True),
        lax.all_gather(solved_part, "col", axis=0, tiled=True),
    )
    full_left = full_left.reshape(tile_order, tile_rows, rank_width)
    full_solved = full_solved.reshape(tile_order, tile_rows, rank_width)
    first_pick = my_col // rows_total
    position = first_pick + 0
    picked_left = lax.dynamic_slice_in_dim(full_left, position, 1, 1)
    picked_solved = lax.dynamic_slice_in_dim(full_solved, position, 1, 1)
    send_left = picked_left.reshape(tile_order, column_tiles * rank_width)
    send_solved = picked_solved.reshape(tile_order, column_tiles * rank_width)
    root_row = my_col % rows_total
    column_left, column_solved = (
        spread(send_left, "row", root_row),
        spread(send_solved, "row", root_row),
    )
    row_factor = jnp.swapaxes(full_left, 0, 1)[:, None]
    row_solved = jnp.swapaxes(full_solved, 0, 1)
    column_factor = jnp.swapaxes(column_left.reshape(tile_order, column_tiles, rank_width), 0, 1)
    column_three = jnp.swapaxes(column_solved.reshape(tile_order, column_tiles, rank_width), 0, 1)
    core_block = jnp.einsum(
        "tbr,sbq->tsrq", row_solved, column_three, preferred_element_type=jnp.float32
    )
    slab_keep = jnp.arange(rank_width, dtype=jnp.int32) < slab_ranks[..., None]
    masked_right = jnp.where(slab_keep[:, :, None, :], slab_right, jnp.zeros((), jnp.bfloat16))
    fresh_left, fresh_right = recompress(
        slab_left, masked_right, row_factor, core_block, column_factor, sketch.astype(jnp.float32)
    )
    row_ids = jnp.arange(tile_rows, dtype=jnp.int32) * rows_total + my_row
    col_ids = jnp.arange(column_tiles, dtype=jnp.int32) * cols_total + my_col
    live_tile = (row_ids[:, None] > col_ids[None, :])[:, :, None, None]
    return (
        jnp.where(live_tile, fresh_left, 0.0).astype(jnp.bfloat16),
        jnp.where(live_tile, fresh_right, 0.0).astype(jnp.bfloat16),
    )


def nt(first, second):
    return lax.dot_general(first, second, (((1,), (1,)), ((), ())), preferred_element_type=F32)


def nn(first, second):
    return lax.dot_general(first, second, (((1,), (0,)), ((), ())), preferred_element_type=F32)


def split(value):
    high = value.astype(BF16)
    return high, (value - high.astype(F32)).astype(BF16)


def wide(value):
    return jnp.concatenate(split(value), axis=0)


def fold(value):
    half = value.shape[0] // 2
    return value[:half] + value[half:]


def dot_split(op, first, second_parts):
    stacked = wide(first)
    return fold(op(stacked, second_parts[0]) + op(stacked, second_parts[1]))


def grant(mebibytes):
    return pltpu.CompilerParams(vmem_limit_bytes=mebibytes << 20)


def solve_kernel(width, info, right_ref, inverse_ref, out_ref):
    right = right_ref[...]
    rows = lax.broadcasted_iota(jnp.int32, right.shape, 0)
    keep = jnp.zeros(right.shape, jnp.bool_)
    for tile in range(right.shape[0] // width):
        keep |= (rows >= tile * width) & (rows < tile * width + info[2 + tile])
    masked = jnp.where(keep, right, jnp.zeros((), right.dtype))
    out_ref[0] = nt(masked, inverse_ref[...])


def solve_part(info, right, inverse, odd, parts, width):
    lines, piece = right.shape
    return pl.pallas_call(
        functools.partial(solve_kernel, width),
        grid_spec=pltpu.PrefetchScalarGridSpec(
            num_scalar_prefetch=1,
            grid=(parts,),
            in_specs=[
                pl.BlockSpec((lines, piece), lambda step, info: (0, 0)),
                pl.BlockSpec((piece, piece), lambda step, info: (info[1] ^ (2 * step + odd), 0)),
            ],
            out_specs=pl.BlockSpec((1, lines, piece), lambda step, info: (step, 0, 0)),
        ),
        out_shape=jax.ShapeDtypeStruct((parts, lines, piece), F32),
        name="solve_odd" if odd else "solve_even",
        compiler_params=grant(4),
        cost_estimate=pl.CostEstimate(
            flops=2 * parts * lines * piece * piece,
            bytes_accessed=2 * parts * piece * piece + 4 * parts * lines * piece,
            transcendentals=0,
        ),
    )(info, right, inverse)


def pair_add_kernel(parts, mine_ref, other_ref, keep_ref, *send_refs):
    keep_ref[...] = mine_ref[0] + other_ref[0]
    for step in range(1, parts):
        send_refs[step - 1][...] = (mine_ref[step] + other_ref[step]).astype(
            send_refs[step - 1].dtype
        )


def in_vmem(count):
    return [pl.BlockSpec(memory_space=VMEM)] * count


def small_cost(bytes_accessed, flops=0):
    return pl.CostEstimate(flops=flops, bytes_accessed=bytes_accessed, transcendentals=0)


def pair_add(mine, other, send_type):
    parts = mine.shape[0]
    shape = mine.shape[1:]
    return pl.pallas_call(
        functools.partial(pair_add_kernel, parts),
        in_specs=in_vmem(2),
        out_specs=in_vmem(parts),
        out_shape=[jax.ShapeDtypeStruct(shape, F32)]
        + [jax.ShapeDtypeStruct(shape, send_type)] * (parts - 1),
        name="pair_add",
        compiler_params=grant(4),
        cost_estimate=small_cost(3 * mine.size * 4),
    )(mine, other)


def gather_add_kernel(count, head_lines, *refs):
    total = refs[0][...]
    for ref in refs[1:count]:
        total = total + ref[...].astype(F32)
    rounded = total.astype(BF16)
    refs[count][...] = rounded
    refs[count + 1][...] = rounded[:head_lines]


def gather_add(first, others, head_lines):
    count = 1 + len(others)
    return pl.pallas_call(
        functools.partial(gather_add_kernel, count, head_lines),
        in_specs=in_vmem(count),
        out_specs=in_vmem(2),
        out_shape=[
            jax.ShapeDtypeStruct(first.shape, BF16),
            jax.ShapeDtypeStruct((head_lines, first.shape[1]), BF16),
        ],
        name="gather_add",
        compiler_params=grant(4),
        cost_estimate=small_cost(first.size * 10),
    )(first, *others)


def core_kernel(rows_total, cols_total, width, info, own_ref, *refs):
    others = refs[: rows_total - 1]
    even_ref, odd_ref, stage = refs[rows_total - 1 :]
    my_row, my_col = info[0], info[1]
    for shift in range(rows_total):
        source = own_ref if shift == 0 else others[shift - 1]
        from_row = lax.rem(my_row - shift + rows_total, rows_total)
        for index in range(cols_total // rows_total):
            relative = my_col ^ (index * rows_total + from_row)
            place = (relative & 1) * (cols_total // 2) + lax.shift_right_logical(relative, 1)
            stage[place] = source[index * width : (index + 1) * width, :]
    piece = own_ref.shape[1]
    half = cols_total // 2
    own = own_ref[...]
    for part, ref in ((1, odd_ref), (0, even_ref)):
        block = stage[part * half : (part + 1) * half].reshape(half * width, piece)
        ref[...] = nt(block, own).reshape(ref.shape)


def core_parts(info, own, others, rows_total, cols_total, width):
    lines, piece = own.shape
    half = cols_total // 2
    shape = jax.ShapeDtypeStruct((half, width, lines), F32)
    return pl.pallas_call(
        functools.partial(core_kernel, rows_total, cols_total, width),
        in_specs=[pl.BlockSpec(memory_space=SMEM)] + in_vmem(rows_total),
        out_specs=in_vmem(2),
        out_shape=[shape, shape],
        scratch_shapes=[VMEM((cols_total, width, piece), BF16)],
        name="core_parts",
        compiler_params=grant(4),
        cost_estimate=small_cost(400000, 2 * lines * piece * cols_total * width),
    )(info, own, *others)


def message_kernel(rows_total, cols_total, width, info, own_ref, *refs):
    others = refs[: rows_total - 1]
    message_refs = refs[rows_total - 1 : -1]
    stage = refs[-1]
    my_row, my_col = info[0], info[1]
    lines = own_ref.shape[0]
    for shift in range(rows_total):
        source = own_ref if shift == 0 else others[shift - 1]
        from_row = lax.rem(my_row - shift + rows_total, rows_total)
        for index in range(cols_total // rows_total):
            stage[index * rows_total + from_row] = source[index * width : (index + 1) * width, :]
    for step, ref in enumerate(message_refs):
        target = my_col ^ (2 * step)
        ref[:width] = stage[target]
        ref[width : width + lines] = own_ref[...]
        ref[width + lines :] = stage[target ^ 1]


def messages(info, own, others, rows_total, cols_total, width):
    lines, piece = own.shape
    half = cols_total // 2
    return pl.pallas_call(
        functools.partial(message_kernel, rows_total, cols_total, width),
        in_specs=[pl.BlockSpec(memory_space=SMEM)] + in_vmem(rows_total),
        out_specs=in_vmem(half),
        out_shape=[jax.ShapeDtypeStruct((lines + 2 * width, piece), BF16)] * half,
        scratch_shapes=[VMEM((cols_total, width, piece), BF16)],
        name="messages",
        compiler_params=grant(4),
        cost_estimate=small_cost(half * (lines + 2 * width) * piece * 4),
    )(info, own, *others)


def bundle_kernel(count, width, *refs):
    out_ref = refs[count]
    for step in range(count):
        out_ref[step] = refs[step][width:]


def bundle(pieces, width):
    lines, piece = pieces[0].shape
    count = len(pieces)
    return pl.pallas_call(
        functools.partial(bundle_kernel, count, width),
        in_specs=in_vmem(count),
        out_specs=pl.BlockSpec(memory_space=VMEM),
        out_shape=jax.ShapeDtypeStruct((count, lines - width, piece), BF16),
        name="bundle",
        compiler_params=grant(4),
        cost_estimate=small_cost(count * (lines - width) * piece * 4),
    )(*pieces)


def piece_views(even_refs, odd_ref, width, lines):
    for step, ref in enumerate(even_refs):
        yield 2 * step, ref.at[width : width + lines], ref.at[:width]
    for step in range(len(even_refs)):
        yield 2 * step + 1, odd_ref.at[step, :lines], odd_ref.at[step, lines:]


def gram_kernel(half, width, info, left_ref, right_ref, sketch_ref, *refs):
    even_refs = refs[:half]
    odd_ref, row_gram_ref, column_gram_ref = refs[half:]
    lines = left_ref.shape[0]
    piece = odd_ref.shape[2]
    my_col = info[1]
    row_gram = jnp.zeros(row_gram_ref.shape, F32)
    column_gram = jnp.zeros(column_gram_ref.shape, F32)
    for relative, panel, column in piece_views(even_refs, odd_ref, width, lines):
        spot = pl.ds(pl.multiple_of((my_col ^ relative) * piece, LANES), piece)
        rows = jnp.concatenate([left_ref[:, spot], panel[...]], axis=0)
        row_gram = row_gram + nt(rows, rows)
        columns = jnp.concatenate([right_ref[:, spot], column[...]], axis=0)
        tall = jnp.concatenate([columns, sketch_ref[:, spot]], axis=0)
        column_gram = column_gram + nt(tall, columns)
    row_gram_ref[...] = row_gram
    column_gram_ref[...] = column_gram


def grams(info, left, right, sketch, even, odd, width):
    lines, order = left.shape
    half = len(even)
    return pl.pallas_call(
        functools.partial(gram_kernel, half, width),
        in_specs=[pl.BlockSpec(memory_space=SMEM)] + in_vmem(4 + half),
        out_specs=in_vmem(2),
        out_shape=[
            jax.ShapeDtypeStruct((2 * lines, 2 * lines), F32),
            jax.ShapeDtypeStruct((lines + 2 * width, lines + width), F32),
        ],
        name="grams",
        compiler_params=grant(16),
        cost_estimate=small_cost(2000000, 2 * order * lines * lines * 8),
    )(info, left, right, sketch, *even, odd)


def factor_and_apply(gram, shift, bands):
    width = gram.shape[0]
    blocks = width // 8
    lanes = lax.broadcasted_iota(jnp.int32, (8, LANES), 1)
    group = lanes - lax.rem(lanes, width)
    sub = lax.broadcasted_iota(jnp.int32, (8, LANES), 0)
    gram_rows = [gram[8 * b : 8 * b + 8] for b in range(blocks)]
    bands = [[band[8 * b : 8 * b + 8] for b in range(blocks)] for band in bands]
    rows = []
    for k in range(width):
        first = k // 8
        rows.append(
            {
                b: jnp.take_along_axis(gram_rows[b], group + k, axis=1)
                for b in range(first, blocks)
            }
        )
    for k in range(width):
        first, inner = divmod(k, 8)
        row = rows[k]
        pivot = row[first][inner : inner + 1] + shift[:1]
        scale = lax.rsqrt(pivot)
        scaled = {b: row[b] * scale for b in row}
        for i in range(k + 1, width):
            lead = scaled[i // 8][i % 8 : i % 8 + 1]
            for b in rows[i]:
                rows[i][b] = rows[i][b] - lead * scaled[b]
        below = dict(scaled)
        below[first] = jnp.where(sub > inner, scaled[first], 0.0)
        for band in bands:
            done = band[first][inner : inner + 1] * scale
            for b in range(first, blocks):
                band[b] = band[b] - below[b] * done
            band[first] = jnp.where(sub == inner, done, band[first])
    return [jnp.concatenate(band, axis=0) for band in bands]


def finish_kernel(half, width, rows_total, info, *refs):
    core_refs = refs[:half]
    row_gram_ref, column_gram_ref, left_ref, right_ref = refs[half : half + 4]
    even_refs = refs[half + 4 : 2 * half + 4]
    odd_ref, out_left_ref, out_right_ref = refs[2 * half + 4 :]
    my_row, my_col = info[0], info[1]
    lines, order = left_ref.shape
    tiles = lines // width
    piece = odd_ref.shape[2]
    lane = lax.broadcasted_iota(jnp.int32, (lines, lines), 1)
    line = lax.broadcasted_iota(jnp.int32, (lines, lines), 0)
    same = (lane // width) == (line // width)

    def diagonal(value):
        return jnp.where(same, value, 0.0)

    def stacked(value):
        return diagonal(jnp.concatenate([value] * tiles, axis=0))

    def blocks(value):
        return jnp.concatenate([stacked(value[:, :lines]), stacked(value[:, lines:])], axis=1)

    lane_row = lax.broadcasted_iota(jnp.int32, (1, lines), 1)
    line_col = lax.broadcasted_iota(jnp.int32, (lines, 1), 0)
    keep_lane = jnp.zeros((1, lines), jnp.bool_)
    keep_line = jnp.zeros((lines, 1), jnp.bool_)
    live_line = jnp.zeros((1, lines), jnp.bool_)
    for tile in range(tiles):
        low, high = tile * width, tile * width + info[2 + tile]
        keep_lane |= (lane_row >= low) & (lane_row < high)
        keep_line |= (line_col >= low) & (line_col < high)
        live = (tile * rows_total + my_row) > my_col
        live_line |= (lane_row >= low) & (lane_row < low + jnp.where(live, width, 0))

    row_gram = row_gram_ref[...]
    row_parts = split(
        jnp.concatenate(
            [
                jnp.concatenate(
                    [diagonal(row_gram[:lines, :lines]), diagonal(row_gram[:lines, lines:])], axis=1
                ),
                jnp.concatenate(
                    [diagonal(row_gram[lines:, :lines]), diagonal(row_gram[lines:, lines:])], axis=1
                ),
            ],
            axis=0,
        )
    )
    column_gram = column_gram_ref[...]
    right_right = jnp.where(same & keep_line & keep_lane, column_gram[:lines, :lines], 0.0)
    right_column = jnp.where(keep_line, column_gram[:lines, lines:], 0.0)
    column_column = column_gram[lines : lines + width, lines:]
    sketch_right = jnp.where(keep_lane, column_gram[lines + width :, :lines], 0.0)
    sketch_column = column_gram[lines + width :, lines:]

    core = core_refs[0][...]
    for ref in core_refs[1:]:
        core = core + ref[...]
    core_split = split(core)
    core_blocks = stacked(core)
    core_block_split = split(core_blocks)

    first = jnp.concatenate([sketch_right, -dot_split(nn, sketch_column, core_split)], axis=1)
    ones = jnp.where(same, 1.0, 0.0).astype(BF16)

    def traced(one, two):
        both = jnp.sum(one * two, axis=0, keepdims=True)
        both = both[:, :lines] + both[:, lines:]
        high, low = split(jnp.broadcast_to(both, (8, lines)))
        return (nn(high, ones) + nn(low, ones)) * (shift_rate / width) + tiny_shift

    image = dot_split(nn, first, row_parts)
    shift = traced(first, image)
    gram = dot_split(nt, first, split(blocks(image)))
    top, bottom = factor_and_apply(gram, shift, [image[:, :lines], image[:, lines:]])
    basis = jnp.concatenate([top, bottom], axis=1)

    cross = -diagonal(dot_split(nn, right_column, core_split))
    inner = dot_split(nn, column_column, core_split)
    core_lines = core.T
    corner = diagonal(dot_split(nn, core_lines, split(inner)))
    middle_parts = split(
        jnp.concatenate(
            [
                jnp.concatenate([right_right, cross], axis=1),
                jnp.concatenate([cross.T, corner], axis=1),
            ],
            axis=0,
        )
    )
    second = dot_split(nn, basis, middle_parts)
    image = dot_split(nn, second, row_parts)
    shift = traced(second, image)
    gram = dot_split(nt, second, split(blocks(image)))
    back = -dot_split(nt, image[:, lines:], core_block_split)
    left_top, left_bottom, right_top, right_bottom = factor_and_apply(
        gram, shift, [second[:, :lines], second[:, lines:], image[:, :lines], back]
    )
    factor_size = factor_scale * math.sqrt(order)
    live_scale = jnp.where(live_line, factor_size, 0.0)
    live_back = jnp.where(live_line, 1.0 / factor_size, 0.0)
    left_small = wide(
        jnp.concatenate([stacked(left_top * live_scale), stacked(left_bottom * live_scale)], axis=1)
    )
    right_small = wide(
        jnp.concatenate(
            [
                stacked(jnp.where(keep_lane, right_top * live_back, 0.0)),
                stacked(right_bottom * live_back),
            ],
            axis=1,
        )
    )
    for relative, panel, column in piece_views(even_refs, odd_ref, width, lines):
        spot = pl.ds(pl.multiple_of((my_col ^ relative) * piece, LANES), piece)
        rows = jnp.concatenate([left_ref[:, spot], panel[...]], axis=0)
        out_left_ref[:, spot] = fold(nn(left_small, rows)).astype(BF16)
        columns = jnp.concatenate([right_ref[:, spot]] + [column[...]] * tiles, axis=0)
        out_right_ref[:, spot] = fold(nn(right_small, columns)).astype(BF16)


def finish(info, cores, row_gram, column_gram, left, right, even, odd, rows_total, width):
    half = len(even)
    shape = jax.ShapeDtypeStruct(left.shape, BF16)
    return pl.pallas_call(
        functools.partial(finish_kernel, half, width, rows_total),
        in_specs=[pl.BlockSpec(memory_space=SMEM)] + in_vmem(2 * half + 5),
        out_specs=in_vmem(2),
        out_shape=[shape, shape],
        name="finish",
        compiler_params=grant(16),
        cost_estimate=small_cost(5000000, 10**9),
    )(info, *cores, row_gram, column_gram, left, right, *even, odd)


def flat_lines(block):
    return jnp.swapaxes(block, -1, -2).reshape(-1, block.shape[-2])


def fast_shards(
    slab_left, slab_right, slab_ranks, panel_left, panel_right, panel_ranks, inverse_factor, sketch
):
    rows_total = lax.axis_size("row")
    cols_total = lax.axis_size("col")
    width = panel_left.shape[-1]
    half = cols_total // 2
    place = jnp.stack([lax.axis_index("row"), lax.axis_index("col")]).astype(jnp.int32)
    panel_info = jnp.concatenate([place, panel_ranks])
    slab_info = jnp.concatenate([place, slab_ranks.reshape(-1)])
    left, right = flat_lines(slab_left), flat_lines(slab_right)
    panel, solve_right = flat_lines(panel_left), flat_lines(panel_right)
    sketch_lines = flat_lines(sketch)
    head = width * (cols_total // rows_total)

    def swap(block, step):
        return lax.ppermute(block, "col", [(i, i ^ step) for i in range(cols_total)])

    def turn(block, shift):
        pairs = [(i, (i + shift) % rows_total) for i in range(rows_total)]
        return lax.ppermute(block, "row", pairs)

    def across(blocks):
        return [swap(block, 2 * (step + 1)) for step, block in enumerate(blocks)]

    def along(block):
        return [turn(block, shift) for shift in range(1, rows_total)]

    odd = solve_part(panel_info, solve_right, inverse_factor, 1, half, width)
    other = swap(odd, 1)
    even = solve_part(panel_info, solve_right, inverse_factor, 0, half, width)
    kept, *sends = pair_add(even, other, BF16)
    received = across(sends)
    panel_others = along(panel[:head])
    solved, solved_head = gather_add(kept, received, head)
    solved_others = along(solved_head)
    own_message, *sends = messages(slab_info, panel, panel_others, rows_total, cols_total, width)
    even_pieces = [own_message] + across(sends)
    core_even, core_odd = core_parts(
        slab_info, solved, solved_others, rows_total, cols_total, width
    )
    core_other = swap(core_odd, 1)
    odd_pieces = swap(bundle(even_pieces, width), 1)
    core_kept, *sends = pair_add(core_even, core_other, F32)
    cores = [core_kept] + across(sends)
    row_gram, column_gram = grams(
        slab_info, left, right, sketch_lines, even_pieces, odd_pieces, width
    )
    fresh_left, fresh_right = finish(
        slab_info,
        cores,
        row_gram,
        column_gram,
        left,
        right,
        even_pieces,
        odd_pieces,
        rows_total,
        width,
    )

    def placed(block):
        tiles = slab_left.shape[:2] + (width, slab_left.shape[2])
        return jnp.swapaxes(block.reshape(tiles), -1, -2)

    return placed(fresh_left), placed(fresh_right)


def fast_fits(rows_total, cols_total, tile_rows, piece_rows, width, column_tiles):
    return (
        column_tiles == 1
        and tile_rows * width == LANES
        and width % 8 == 0
        and piece_rows % LANES == 0
        and cols_total & (cols_total - 1) == 0
        and cols_total >= 4
        and cols_total % rows_total == 0
        and rows_total > 1
        and cols_total <= tile_rows * rows_total
    )


def shards(*args):
    tile_rows, piece_rows, width = args[3].shape
    rows_total, cols_total = lax.axis_size("row"), lax.axis_size("col")
    fits = fast_fits(rows_total, cols_total, tile_rows, piece_rows, width, args[0].shape[1])
    return fast_shards(*args) if fits else plain_shards(*args)


def solution(mesh):
    placed = (
        P("row", "col", None, None),
        P("row", "col", None, None),
        P("row", "col"),
        P("row", "col", None),
        P("row", "col", None),
        P("row"),
        P(None, "col"),
        P(),
    )
    return jax.shard_map(
        shards,
        mesh=mesh,
        in_specs=placed,
        out_specs=(P("row", "col", None, None), P("row", "col", None, None)),
        check_vma=False,
    )
```

profile of v0, /device:TPU:0, one launch (start us, length us, event | category | flops | bytes accessed | tf_op | source)
XLA Modules:
  0.0 54.4 jit_solution(16322005193921757962)
XLA Ops:
  0.6 0.0 copy-start.8
  0.6 0.6 %copy-done.8 = s32[4]{0:T(128)S(1)} copy-done((s32[4]{0:T(128)S(1)}, s32[4]{0:T(128)}, u32[]{:S(2)}) %copy-start.8) | copy-done | bytes 40
  1.3 0.1 pad_add_fusion.2.info
  1.4 0.0 copy-start
  1.4 1.2 %copy-done = bf16[2048,256]{1,0:T(8,128)(2,1)S(1)} copy-done((bf16[2048,256]{1,0:T(8,128)(2,1)S(1)}, bf16[2048,256]{1,0:T(8,128)(2,1)}, u32[]{:S(2)}) %copy-start) | copy-done | bytes 1048600
  2.6 0.0 copy-start.2
  2.6 0.8 %copy-done.2 = bf16[4,256,32]{1,2,0:T(8,128)(2,1)S(1)} copy-done((bf16[4,256,32]{1,2,0:T(8,128)(2,1)S(1)}, bf16[4,256,32]{1,2,0:T(8,128)(2,1)}, u32[]{:S(2)}) %copy-start.2) | copy-done | bytes 65560
  3.4 0.0 copy-start.4
  3.4 0.0 copy-start.1
  3.4 1.4 %solve_odd.1 = f32[4,128,256]{2,1,0:T(8,128)S(1)} custom-call(s32[6]{0:T(128)S(1)} %pad_add_fusion.2.info, bf16[128,256]{1,0:T(8,128)(2,1)S(1)} %bitcast.27, bf16[2048,256]{1,0:T(8,128)(2,1)S(1)} %copy-done), custom_call_target="tpu_custom_call" | custom-call | flops 67108864 | bytes 1048576 | tf_op jit(solution)/shard_map/solve_odd/pallas_call | solution.py:178
  4.9 0.6 %collective-permute-start = (f32[4,128,256]{2,1,0:T(8,128)S(1)}, f32[4,128,256]{2,1,0:T(8,128)S(1)}, u32[]{:S(2)}, u32[]{:S(2)}) collective-permute-start(f32[4,128,256]{2,1,0:T(8,128)S(1)} %solve_odd.1), channel_id=1, source_target_pairs={{0,1},{1,0},{2,3},{3,2},{4,5},{5,4},{6,7},{7,6},{8,9},{9,8},{10,11... | collective-permute-start | bytes 1572872 | tf_op jit(solution)/shard_map/ppermute | solution.py:579
  5.4 0.0 copy-done.4
  5.4 0.0 copy-start.9
  5.4 2.6 %collective-permute-start.11 = (bf16[64,256]{1,0:T(8,128)(2,1)S(1)}, bf16[64,256]{1,0:T(8,128)(2,1)S(1)}, u32[]{:S(2)}, u32[]{:S(2)}) collective-permute-start(bf16[64,256]{1,0:T(8,128)(2,1)S(1)} %bitcast.36), channel_id=1, source_target_pairs={{0,8},{8,16},{16,24},{24,0},{1,9},{9,17},{17,25},{25,1},{2,10},{10... | collective-permute-start | bytes 98312 | tf_op jit(solution)/shard_map/ppermute | solution.py:583
  8.1 2.6 %collective-permute-start.12 = (bf16[64,256]{1,0:T(8,128)(2,1)S(1)}, bf16[64,256]{1,0:T(8,128)(2,1)S(1)}, u32[]{:S(2)}, u32[]{:S(2)}) collective-permute-start(bf16[64,256]{1,0:T(8,128)(2,1)S(1)} %bitcast.37), channel_id=1, source_target_pairs={{0,16},{8,24},{16,0},{24,8},{1,17},{9,25},{17,1},{25,9},{2,18},{10... | collective-permute-start | bytes 98312 | tf_op jit(solution)/shard_map/ppermute | solution.py:583
  10.7 1.3 %collective-permute-start.13 = (bf16[64,256]{1,0:T(8,128)(2,1)S(1)}, bf16[64,256]{1,0:T(8,128)(2,1)S(1)}, u32[]{:S(2)}, u32[]{:S(2)}) collective-permute-start(bf16[64,256]{1,0:T(8,128)(2,1)S(1)} %bitcast.38), channel_id=1, source_target_pairs={{0,24},{8,0},{16,8},{24,16},{1,25},{9,1},{17,9},{25,17},{2,26},{10... | collective-permute-start | bytes 98312 | tf_op jit(solution)/shard_map/ppermute | solution.py:583
  12.0 0.0 copy-done.9
  12.0 0.1 pad_add_fusion.info
  12.1 0.1 collective-permute-done.11.refs_0_
  12.2 1.1 %collective-permute-done.12.refs_1_ = bf16[64,256]{1,0:T(8,128)(2,1)S(1)} collective-permute-done((bf16[64,256]{1,0:T(8,128)(2,1)S(1)}, bf16[64,256]{1,0:T(8,128)(2,1)S(1)}, u32[]{:S(2)}, u32[]{:S(2)}) %collective-permute-start.12) | collective-permute-done | bytes 32800 | tf_op jit(solution)/shard_map/ppermute | solution.py:583
  13.3 1.3 %collective-permute-done.13.refs_2_ = bf16[64,256]{1,0:T(8,128)(2,1)S(1)} collective-permute-done((bf16[64,256]{1,0:T(8,128)(2,1)S(1)}, bf16[64,256]{1,0:T(8,128)(2,1)S(1)}, u32[]{:S(2)}, u32[]{:S(2)}) %collective-permute-start.13) | collective-permute-done | bytes 32800 | tf_op jit(solution)/shard_map/ppermute | solution.py:583
  14.6 0.6 %messages.1 = (bf16[192,256]{1,0:T(8,128)(2,1)S(1)}, bf16[192,256]{1,0:T(8,128)(2,1)S(1)}, bf16[192,256]{1,0:T(8,128)(2,1)S(1)}, bf16[192,256]{1,0:T(8,128)(2,1)S(1)}) custom-call(s32[6]{0:T(128)S(1)} %pad_add_fusion.info, bf16[128,256]{1,0:T(8,128)(2,1)S(1)} %bitcast.30, bf16[64,256]{1,0:T(8,128)(2,1)S(1)} %collective-permute-done.11.refs_0_, ...), custom_call_target="tpu_custom_call" | custom-call | bytes 786432 | tf_op jit(solution)/shard_map/messages/pallas_call | solution.py:312
  15.2 1.6 %collective-permute-start.14 = (bf16[192,256]{1,0:T(8,128)(2,1)S(1)}, bf16[192,256]{1,0:T(8,128)(2,1)S(1)}, u32[]{:S(2)}, u32[]{:S(2)}) collective-permute-start(bf16[192,256]{1,0:T(8,128)(2,1)S(1)} %get-tuple-element.35), channel_id=1, source_target_pairs={{0,2},{1,3},{2,0},{3,1},{4,6},{5,7},{6,4},{7,5},{8,10},{9,11},{10,... | collective-permute-start | bytes 294920 | tf_op jit(solution)/shard_map/ppermute | solution.py:579
  16.7 1.5 %collective-permute-start.15 = (bf16[192,256]{1,0:T(8,128)(2,1)S(1)}, bf16[192,256]{1,0:T(8,128)(2,1)S(1)}, u32[]{:S(2)}, u32[]{:S(2)}) collective-permute-start(bf16[192,256]{1,0:T(8,128)(2,1)S(1)} %get-tuple-element.36), channel_id=1, source_target_pairs={{0,4},{1,5},{2,6},{3,7},{4,0},{5,1},{6,2},{7,3},{8,12},{9,13},{10,... | collective-permute-start | bytes 294920 | tf_op jit(solution)/shard_map/ppermute | solution.py:579
  18.2 0.5 collective-permute-start.16
  18.7 2.0 %collective-permute-done.14.refs_1_.refs_9_ = bf16[192,256]{1,0:T(8,128)(2,1)S(1)} collective-permute-done((bf16[192,256]{1,0:T(8,128)(2,1)S(1)}, bf16[192,256]{1,0:T(8,128)(2,1)S(1)}, u32[]{:S(2)}, u32[]{:S(2)}) %collective-permute-start.14) | collective-permute-done | bytes 98336 | tf_op jit(solution)/shard_map/ppermute | solution.py:579
  20.7 1.5 %collective-permute-done.15.refs_2_.refs_10_ = bf16[192,256]{1,0:T(8,128)(2,1)S(1)} collective-permute-done((bf16[192,256]{1,0:T(8,128)(2,1)S(1)}, bf16[192,256]{1,0:T(8,128)(2,1)S(1)}, u32[]{:S(2)}, u32[]{:S(2)}) %collective-permute-start.15) | collective-permute-done | bytes 98336 | tf_op jit(solution)/shard_map/ppermute | solution.py:579
  22.2 1.5 %collective-permute-done.16.refs_3_.refs_11_ = bf16[192,256]{1,0:T(8,128)(2,1)S(1)} collective-permute-done((bf16[192,256]{1,0:T(8,128)(2,1)S(1)}, bf16[192,256]{1,0:T(8,128)(2,1)S(1)}, u32[]{:S(2)}, u32[]{:S(2)}) %collective-permute-start.16) | collective-permute-done | bytes 98336 | tf_op jit(solution)/shard_map/ppermute | solution.py:579
  23.8 0.0 copy-start.3
  23.8 0.1 collective-permute-start.17
  23.9 0.0 copy-done.1
  23.9 0.7 %copy-done.3 = bf16[4,256,32]{1,2,0:T(8,128)(2,1)S(1)} copy-done((bf16[4,256,32]{1,2,0:T(8,128)(2,1)S(1)}, bf16[4,256,32]{1,2,0:T(8,128)(2,1)}, u32[]{:S(2)}) %copy-start.3) | copy-done | bytes 65560
  24.6 1.4 %solve_even.1.mine_ref = f32[4,128,256]{2,1,0:T(8,128)S(1)} custom-call(s32[6]{0:T(128)S(1)} %pad_add_fusion.2.info, bf16[128,256]{1,0:T(8,128)(2,1)S(1)} %bitcast.28, bf16[2048,256]{1,0:T(8,128)(2,1)S(1)} %copy-done.1), custom_call_target="tpu_custom_call" | custom-call | flops 67108864 | bytes 1048576 | tf_op jit(solution)/shard_map/solve_even/pallas_call | solution.py:178
  26.0 0.0 collective-permute-done.other_ref
  26.0 0.0 copy-start.6
  26.0 0.0 copy-start.7
  26.0 0.1 pair_add.2
  26.1 0.6 %collective-permute-start.1 = (bf16[128,256]{1,0:T(8,128)(2,1)S(1)}, bf16[128,256]{1,0:T(8,128)(2,1)S(1)}, u32[]{:S(2)}, u32[]{:S(2)}) collective-permute-start(bf16[128,256]{1,0:T(8,128)(2,1)S(1)} %get-tuple-element.23), channel_id=1, source_target_pairs={{0,2},{1,3},{2,0},{3,1},{4,6},{5,7},{6,4},{7,5},{8,10},{9,11},{10,... | collective-permute-start | bytes 196616 | tf_op jit(solution)/shard_map/ppermute | solution.py:579
  26.7 0.5 collective-permute-start.2
  27.2 2.4 %collective-permute-start.3 = (bf16[128,256]{1,0:T(8,128)(2,1)S(1)}, bf16[128,256]{1,0:T(8,128)(2,1)S(1)}, u32[]{:S(2)}, u32[]{:S(2)}) collective-permute-start(bf16[128,256]{1,0:T(8,128)(2,1)S(1)} %get-tuple-element.25), channel_id=1, source_target_pairs={{0,6},{1,7},{2,4},{3,5},{4,2},{5,3},{6,0},{7,1},{8,14},{9,15},{10,... | collective-permute-start | bytes 196616 | tf_op jit(solution)/shard_map/ppermute | solution.py:579
  29.7 1.2 %collective-permute-done.1.refs_1_ = bf16[128,256]{1,0:T(8,128)(2,1)S(1)} collective-permute-done((bf16[128,256]{1,0:T(8,128)(2,1)S(1)}, bf16[128,256]{1,0:T(8,128)(2,1)S(1)}, u32[]{:S(2)}, u32[]{:S(2)}) %collective-permute-start.1) | collective-permute-done | bytes 65568 | tf_op jit(solution)/shard_map/ppermute | solution.py:579
  30.9 0.6 %collective-permute-done.2.refs_2_ = bf16[128,256]{1,0:T(8,128)(2,1)S(1)} collective-permute-done((bf16[128,256]{1,0:T(8,128)(2,1)S(1)}, bf16[128,256]{1,0:T(8,128)(2,1)S(1)}, u32[]{:S(2)}, u32[]{:S(2)}) %collective-permute-start.2) | collective-permute-done | bytes 65568 | tf_op jit(solution)/shard_map/ppermute | solution.py:579
  31.5 0.9 %collective-permute-done.3.refs_3_ = bf16[128,256]{1,0:T(8,128)(2,1)S(1)} collective-permute-done((bf16[128,256]{1,0:T(8,128)(2,1)S(1)}, bf16[128,256]{1,0:T(8,128)(2,1)S(1)}, u32[]{:S(2)}, u32[]{:S(2)}) %collective-permute-start.3) | collective-permute-done | bytes 65568 | tf_op jit(solution)/shard_map/ppermute | solution.py:579
  32.4 0.9 %collective-permute-start.4 = (bf16[64,256]{1,0:T(8,128)(2,1)S(1)}, bf16[64,256]{1,0:T(8,128)(2,1)S(1)}, u32[]{:S(2)}, u32[]{:S(2)}) collective-permute-start(bf16[64,256]{1,0:T(8,128)(2,1)S(1)} %get-tuple-element.27), channel_id=1, source_target_pairs={{0,8},{8,16},{16,24},{24,0},{1,9},{9,17},{17,25},{25,1},{2,10},{10... | collective-permute-start | bytes 98312 | tf_op jit(solution)/shard_map/ppermute | solution.py:583
  33.3 2.9 %collective-permute-start.5 = (bf16[64,256]{1,0:T(8,128)(2,1)S(1)}, bf16[64,256]{1,0:T(8,128)(2,1)S(1)}, u32[]{:S(2)}, u32[]{:S(2)}) collective-permute-start(bf16[64,256]{1,0:T(8,128)(2,1)S(1)} %get-tuple-element.27), channel_id=1, source_target_pairs={{0,16},{8,24},{16,0},{24,8},{1,17},{9,25},{17,1},{25,9},{2,18},{10... | collective-permute-start | bytes 98312 | tf_op jit(solution)/shard_map/ppermute | solution.py:583
  36.2 0.2 collective-permute-start.6
  36.4 1.9 %collective-permute-done.4.refs_0_ = bf16[64,256]{1,0:T(8,128)(2,1)S(1)} collective-permute-done((bf16[64,256]{1,0:T(8,128)(2,1)S(1)}, bf16[64,256]{1,0:T(8,128)(2,1)S(1)}, u32[]{:S(2)}, u32[]{:S(2)}) %collective-permute-start.4) | collective-permute-done | bytes 32800 | tf_op jit(solution)/shard_map/ppermute | solution.py:583
  38.3 0.5 collective-permute-done.5.refs_1_
  38.8 1.3 %collective-permute-done.6.refs_2_ = bf16[64,256]{1,0:T(8,128)(2,1)S(1)} collective-permute-done((bf16[64,256]{1,0:T(8,128)(2,1)S(1)}, bf16[64,256]{1,0:T(8,128)(2,1)S(1)}, u32[]{:S(2)}, u32[]{:S(2)}) %collective-permute-start.6) | collective-permute-done | bytes 32800 | tf_op jit(solution)/shard_map/ppermute | solution.py:583
  40.1 0.7 %core_parts.1 = (f32[4,32,128]{2,1,0:T(8,128)S(1)}, f32[4,32,128]{2,1,0:T(8,128)S(1)}) custom-call(s32[6]{0:T(128)S(1)} %pad_add_fusion.info, bf16[128,256]{1,0:T(8,128)(2,1)S(1)} %get-tuple-element.26.own_ref, bf16[64,256]{1,0:T(8,128)(2,1)S(1)} %collective-permute-done.4.refs_0_, bf16[64,256]{1,0:T(8,128)(2,1)S(1)} %collective-permute-done.5.refs_1_, ...), custom_call_target="tpu_custom_call" | custom-call | flops 16777216 | bytes 400000 | tf_op jit(solution)/shard_map/core_parts/pallas_call | solution.py:279
  40.8 0.1 collective-permute-start.7
  40.9 1.2 %collective-permute-done.7.other_ref = f32[4,32,128]{2,1,0:T(8,128)S(1)} collective-permute-done((f32[4,32,128]{2,1,0:T(8,128)S(1)}, f32[4,32,128]{2,1,0:T(8,128)S(1)}, u32[]{:S(2)}, u32[]{:S(2)}) %collective-permute-start.7) | collective-permute-done | bytes 65568 | tf_op jit(solution)/shard_map/ppermute | solution.py:579
  42.2 1.6 %collective-permute-start.8 = (f32[32,128]{1,0:T(8,128)S(1)}, f32[32,128]{1,0:T(8,128)S(1)}, u32[]{:S(2)}, u32[]{:S(2)}) collective-permute-start(f32[32,128]{1,0:T(8,128)S(1)} %get-tuple-element.31), channel_id=1, source_target_pairs={{0,2},{1,3},{2,0},{3,1},{4,6},{5,7},{6,4},{7,5},{8,10},{9,11},{10,... | collective-permute-start | bytes 49160 | tf_op jit(solution)/shard_map/ppermute | solution.py:579
  43.8 1.5 %collective-permute-start.9 = (f32[32,128]{1,0:T(8,128)S(1)}, f32[32,128]{1,0:T(8,128)S(1)}, u32[]{:S(2)}, u32[]{:S(2)}) collective-permute-start(f32[32,128]{1,0:T(8,128)S(1)} %get-tuple-element.32), channel_id=1, source_target_pairs={{0,4},{1,5},{2,6},{3,7},{4,0},{5,1},{6,2},{7,3},{8,12},{9,13},{10,... | collective-permute-start | bytes 49160 | tf_op jit(solution)/shard_map/ppermute | solution.py:579
  45.2 0.5 collective-permute-start.10
  45.7 0.0 collective-permute-done.17.refs_4_.refs_12_
  45.7 0.0 copy-done.6
  45.7 0.0 copy-done.7
  45.7 0.0 copy-done.5
  45.7 1.2 %grams.1 = (f32[256,256]{1,0:T(8,128)S(1)}, f32[192,160]{1,0:T(8,128)S(1)}) custom-call(s32[6]{0:T(128)S(1)} %pad_add_fusion.info, bf16[128,2048]{1,0:T(8,128)(2,1)S(1)} %bitcast.31, bf16[128,2048]{1,0:T(8,128)(2,1)S(1)} %bitcast.33, bf16[32,2048]{1,0:T(8,128)(2,1)S(1)} %bitcast.35, bf16[192,256]{1,0:T(8,128)(2,1)S(1)} %get-tuple-element.34.refs_0_.refs_8_, ...), custom_call_target="tpu_custom_call" | custom-call | flops 536870912 | bytes 2000000 | tf_op jit(solution)/shard_map/grams/pallas_call | solution.py:373
  47.0 0.0 collective-permute-done.8.refs_1_
  47.0 0.5 collective-permute-done.9.refs_2_
  47.5 2.4 %collective-permute-done.10.refs_3_ = f32[32,128]{1,0:T(8,128)S(1)} collective-permute-done((f32[32,128]{1,0:T(8,128)S(1)}, f32[32,128]{1,0:T(8,128)S(1)}, u32[]{:S(2)}, u32[]{:S(2)}) %collective-permute-start.10) | collective-permute-done | bytes 16416 | tf_op jit(solution)/shard_map/ppermute | solution.py:579
  49.9 4.5 %finish.1 = (bf16[128,2048]{1,0:T(8,128)(2,1)}, bf16[128,2048]{1,0:T(8,128)(2,1)}) custom-call(s32[6]{0:T(128)S(1)} %pad_add_fusion.info, f32[32,128]{1,0:T(8,128)S(1)} %get-tuple-element.30.refs_0_, f32[32,128]{1,0:T(8,128)S(1)} %collective-permute-done.8.refs_1_, f32[32,128]{1,0:T(8,128)S(1)} %collective-permute-done.9.refs_2_, ...), custom_call_target="tpu_custom_call" | custom-call | flops 1000000000 | bytes 5000000 | tf_op jit(solution)/shard_map/finish/pallas_call | solution.py:548
  (5 shorter events, 0.1 us)
Async XLA Ops:
  0.6 0.7 %copy-start.8 = (s32[4]{0:T(128)S(1)}, s32[4]{0:T(128)}, u32[]{:S(2)}) copy-start(s32[4]{0:T(128)} %param.13) | copy-start | bytes 52
  1.4 1.2 %copy-start = (bf16[2048,256]{1,0:T(8,128)(2,1)S(1)}, bf16[2048,256]{1,0:T(8,128)(2,1)}, u32[]{:S(2)}) copy-start(bf16[2048,256]{1,0:T(8,128)(2,1)} %inverse_ref.3) | copy-start | bytes 3145732
  2.6 0.8 %copy-start.2 = (bf16[4,256,32]{1,2,0:T(8,128)(2,1)S(1)}, bf16[4,256,32]{1,2,0:T(8,128)(2,1)}, u32[]{:S(2)}) copy-start(bf16[4,256,32]{1,2,0:T(8,128)(2,1)} %param.12) | copy-start | bytes 196612
  3.4 2.0 %copy-start.4 = (bf16[4,256,32]{1,2,0:T(8,128)(2,1)S(1)}, bf16[4,256,32]{1,2,0:T(8,128)(2,1)}, u32[]{:S(2)}) copy-start(bf16[4,256,32]{1,2,0:T(8,128)(2,1)} %param.11) | copy-start | bytes 196612
  3.4 20.4 %copy-start.1 = (bf16[2048,256]{1,0:T(8,128)(2,1)S(1)}, bf16[2048,256]{1,0:T(8,128)(2,1)}, u32[]{:S(2)}) copy-start(bf16[2048,256]{1,0:T(8,128)(2,1)} %inverse_ref.3) | copy-start | bytes 3145732
  4.9 21.1 %collective-permute-start = (f32[4,128,256]{2,1,0:T(8,128)S(1)}, f32[4,128,256]{2,1,0:T(8,128)S(1)}, u32[]{:S(2)}, u32[]{:S(2)}) collective-permute-start(f32[4,128,256]{2,1,0:T(8,128)S(1)} %solve_odd.1), channel_id=1, source_target_pairs={{0,1},{1,0},{2,3},{3,2},{4,5},{5,4},{6,7},{7,6},{8,9},{9,8},{10,11... | collective-permute-start | bytes 1572872 | tf_op jit(solution)/shard_map/ppermute | solution.py:579
  5.4 6.6 %copy-start.9 = (s32[4,1]{0,1:T(1,128)S(1)}, s32[4,1]{0,1:T(1,128)}, u32[]{:S(2)}) copy-start(s32[4,1]{0,1:T(1,128)} %param.10) | copy-start | bytes 52
  5.4 6.7 %collective-permute-start.11 = (bf16[64,256]{1,0:T(8,128)(2,1)S(1)}, bf16[64,256]{1,0:T(8,128)(2,1)S(1)}, u32[]{:S(2)}, u32[]{:S(2)}) collective-permute-start(bf16[64,256]{1,0:T(8,128)(2,1)S(1)} %bitcast.36), channel_id=1, source_target_pairs={{0,8},{8,16},{16,24},{24,0},{1,9},{9,17},{17,25},{25,1},{2,10},{10... | collective-permute-start | bytes 98312 | tf_op jit(solution)/shard_map/ppermute | solution.py:583
  8.1 5.2 %collective-permute-start.12 = (bf16[64,256]{1,0:T(8,128)(2,1)S(1)}, bf16[64,256]{1,0:T(8,128)(2,1)S(1)}, u32[]{:S(2)}, u32[]{:S(2)}) collective-permute-start(bf16[64,256]{1,0:T(8,128)(2,1)S(1)} %bitcast.37), channel_id=1, source_target_pairs={{0,16},{8,24},{16,0},{24,8},{1,17},{9,25},{17,1},{25,9},{2,18},{10... | collective-permute-start | bytes 98312 | tf_op jit(solution)/shard_map/ppermute | solution.py:583
  10.7 3.9 %collective-permute-start.13 = (bf16[64,256]{1,0:T(8,128)(2,1)S(1)}, bf16[64,256]{1,0:T(8,128)(2,1)S(1)}, u32[]{:S(2)}, u32[]{:S(2)}) collective-permute-start(bf16[64,256]{1,0:T(8,128)(2,1)S(1)} %bitcast.38), channel_id=1, source_target_pairs={{0,24},{8,0},{16,8},{24,16},{1,25},{9,1},{17,9},{25,17},{2,26},{10... | collective-permute-start | bytes 98312 | tf_op jit(solution)/shard_map/ppermute | solution.py:583
  15.2 5.5 %collective-permute-start.14 = (bf16[192,256]{1,0:T(8,128)(2,1)S(1)}, bf16[192,256]{1,0:T(8,128)(2,1)S(1)}, u32[]{:S(2)}, u32[]{:S(2)}) collective-permute-start(bf16[192,256]{1,0:T(8,128)(2,1)S(1)} %get-tuple-element.35), channel_id=1, source_target_pairs={{0,2},{1,3},{2,0},{3,1},{4,6},{5,7},{6,4},{7,5},{8,10},{9,11},{10,... | collective-permute-start | bytes 294920 | tf_op jit(solution)/shard_map/ppermute | solution.py:579
  16.7 5.5 %collective-permute-start.15 = (bf16[192,256]{1,0:T(8,128)(2,1)S(1)}, bf16[192,256]{1,0:T(8,128)(2,1)S(1)}, u32[]{:S(2)}, u32[]{:S(2)}) collective-permute-start(bf16[192,256]{1,0:T(8,128)(2,1)S(1)} %get-tuple-element.36), channel_id=1, source_target_pairs={{0,4},{1,5},{2,6},{3,7},{4,0},{5,1},{6,2},{7,3},{8,12},{9,13},{10,... | collective-permute-start | bytes 294920 | tf_op jit(solution)/shard_map/ppermute | solution.py:579
  18.2 5.5 %collective-permute-start.16 = (bf16[192,256]{1,0:T(8,128)(2,1)S(1)}, bf16[192,256]{1,0:T(8,128)(2,1)S(1)}, u32[]{:S(2)}, u32[]{:S(2)}) collective-permute-start(bf16[192,256]{1,0:T(8,128)(2,1)S(1)} %get-tuple-element.37), channel_id=1, source_target_pairs={{0,6},{1,7},{2,4},{3,5},{4,2},{5,3},{6,0},{7,1},{8,14},{9,15},{10,... | collective-permute-start | bytes 294920 | tf_op jit(solution)/shard_map/ppermute | solution.py:579
  23.8 0.8 %copy-start.3 = (bf16[4,256,32]{1,2,0:T(8,128)(2,1)S(1)}, bf16[4,256,32]{1,2,0:T(8,128)(2,1)}, u32[]{:S(2)}) copy-start(bf16[4,256,32]{1,2,0:T(8,128)(2,1)} %param.12) | copy-start | bytes 196612
  23.8 21.9 %collective-permute-start.17 = (bf16[4,160,256]{2,1,0:T(8,128)(2,1)S(1)}, bf16[4,160,256]{2,1,0:T(8,128)(2,1)S(1)}, u32[]{:S(2)}, u32[]{:S(2)}) collective-permute-start(bf16[4,160,256]{2,1,0:T(8,128)(2,1)S(1)} %bundle.1), channel_id=1, source_target_pairs={{0,1},{1,0},{2,3},{3,2},{4,5},{5,4},{6,7},{7,6},{8,9},{9,8},{10,11... | collective-permute-start | bytes 983048 | tf_op jit(solution)/shard_map/ppermute | solution.py:579
  26.0 19.7 %copy-start.6 = (bf16[4,1,2048,32]{2,3,1,0:T(8,128)(2,1)S(1)}, bf16[4,1,2048,32]{2,3,1,0:T(8,128)(2,1)}, u32[]{:S(2)}) copy-start(bf16[4,1,2048,32]{2,3,1,0:T(8,128)(2,1)} %param.9) | copy-start | bytes 1572868
  26.0 19.7 %copy-start.7 = (bf16[2048,32]{0,1:T(8,128)(2,1)S(1)}, bf16[2048,32]{0,1:T(8,128)(2,1)}, u32[]{:S(2)}) copy-start(bf16[2048,32]{0,1:T(8,128)(2,1)} %param.15) | copy-start | bytes 393220
  26.1 19.6 %copy-start.5 = (bf16[4,1,2048,32]{2,3,1,0:T(8,128)(2,1)S(1)}, bf16[4,1,2048,32]{2,3,1,0:T(8,128)(2,1)}, u32[]{:S(2)}) copy-start(bf16[4,1,2048,32]{2,3,1,0:T(8,128)(2,1)} %param.8) | copy-start | bytes 1572868
  26.1 4.8 %collective-permute-start.1 = (bf16[128,256]{1,0:T(8,128)(2,1)S(1)}, bf16[128,256]{1,0:T(8,128)(2,1)S(1)}, u32[]{:S(2)}, u32[]{:S(2)}) collective-permute-start(bf16[128,256]{1,0:T(8,128)(2,1)S(1)} %get-tuple-element.23), channel_id=1, source_target_pairs={{0,2},{1,3},{2,0},{3,1},{4,6},{5,7},{6,4},{7,5},{8,10},{9,11},{10,... | collective-permute-start | bytes 196616 | tf_op jit(solution)/shard_map/ppermute | solution.py:579
  26.7 4.8 %collective-permute-start.2 = (bf16[128,256]{1,0:T(8,128)(2,1)S(1)}, bf16[128,256]{1,0:T(8,128)(2,1)S(1)}, u32[]{:S(2)}, u32[]{:S(2)}) collective-permute-start(bf16[128,256]{1,0:T(8,128)(2,1)S(1)} %get-tuple-element.24), channel_id=1, source_target_pairs={{0,4},{1,5},{2,6},{3,7},{4,0},{5,1},{6,2},{7,3},{8,12},{9,13},{10,... | collective-permute-start | bytes 196616 | tf_op jit(solution)/shard_map/ppermute | solution.py:579
  27.2 5.2 %collective-permute-start.3 = (bf16[128,256]{1,0:T(8,128)(2,1)S(1)}, bf16[128,256]{1,0:T(8,128)(2,1)S(1)}, u32[]{:S(2)}, u32[]{:S(2)}) collective-permute-start(bf16[128,256]{1,0:T(8,128)(2,1)S(1)} %get-tuple-element.25), channel_id=1, source_target_pairs={{0,6},{1,7},{2,4},{3,5},{4,2},{5,3},{6,0},{7,1},{8,14},{9,15},{10,... | collective-permute-start | bytes 196616 | tf_op jit(solution)/shard_map/ppermute | solution.py:579
  32.4 5.9 %collective-permute-start.4 = (bf16[64,256]{1,0:T(8,128)(2,1)S(1)}, bf16[64,256]{1,0:T(8,128)(2,1)S(1)}, u32[]{:S(2)}, u32[]{:S(2)}) collective-permute-start(bf16[64,256]{1,0:T(8,128)(2,1)S(1)} %get-tuple-element.27), channel_id=1, source_target_pairs={{0,8},{8,16},{16,24},{24,0},{1,9},{9,17},{17,25},{25,1},{2,10},{10... | collective-permute-start | bytes 98312 | tf_op jit(solution)/shard_map/ppermute | solution.py:583
  33.3 5.5 %collective-permute-start.5 = (bf16[64,256]{1,0:T(8,128)(2,1)S(1)}, bf16[64,256]{1,0:T(8,128)(2,1)S(1)}, u32[]{:S(2)}, u32[]{:S(2)}) collective-permute-start(bf16[64,256]{1,0:T(8,128)(2,1)S(1)} %get-tuple-element.27), channel_id=1, source_target_pairs={{0,16},{8,24},{16,0},{24,8},{1,17},{9,25},{17,1},{25,9},{2,18},{10... | collective-permute-start | bytes 98312 | tf_op jit(solution)/shard_map/ppermute | solution.py:583
  36.2 3.9 %collective-permute-start.6 = (bf16[64,256]{1,0:T(8,128)(2,1)S(1)}, bf16[64,256]{1,0:T(8,128)(2,1)S(1)}, u32[]{:S(2)}, u32[]{:S(2)}) collective-permute-start(bf16[64,256]{1,0:T(8,128)(2,1)S(1)} %get-tuple-element.27), channel_id=1, source_target_pairs={{0,24},{8,0},{16,8},{24,16},{1,25},{9,1},{17,9},{25,17},{2,26},{10... | collective-permute-start | bytes 98312 | tf_op jit(solution)/shard_map/ppermute | solution.py:583
  40.8 1.3 %collective-permute-start.7 = (f32[4,32,128]{2,1,0:T(8,128)S(1)}, f32[4,32,128]{2,1,0:T(8,128)S(1)}, u32[]{:S(2)}, u32[]{:S(2)}) collective-permute-start(f32[4,32,128]{2,1,0:T(8,128)S(1)} %get-tuple-element.29), channel_id=1, source_target_pairs={{0,1},{1,0},{2,3},{3,2},{4,5},{5,4},{6,7},{7,6},{8,9},{9,8},{10,11... | collective-permute-start | bytes 196616 | tf_op jit(solution)/shard_map/ppermute | solution.py:579
  42.2 4.8 %collective-permute-start.8 = (f32[32,128]{1,0:T(8,128)S(1)}, f32[32,128]{1,0:T(8,128)S(1)}, u32[]{:S(2)}, u32[]{:S(2)}) collective-permute-start(f32[32,128]{1,0:T(8,128)S(1)} %get-tuple-element.31), channel_id=1, source_target_pairs={{0,2},{1,3},{2,0},{3,1},{4,6},{5,7},{6,4},{7,5},{8,10},{9,11},{10,... | collective-permute-start | bytes 49160 | tf_op jit(solution)/shard_map/ppermute | solution.py:579
  43.8 3.7 %collective-permute-start.9 = (f32[32,128]{1,0:T(8,128)S(1)}, f32[32,128]{1,0:T(8,128)S(1)}, u32[]{:S(2)}, u32[]{:S(2)}) collective-permute-start(f32[32,128]{1,0:T(8,128)S(1)} %get-tuple-element.32), channel_id=1, source_target_pairs={{0,4},{1,5},{2,6},{3,7},{4,0},{5,1},{6,2},{7,3},{8,12},{9,13},{10,... | collective-permute-start | bytes 49160 | tf_op jit(solution)/shard_map/ppermute | solution.py:579
  45.2 4.6 %collective-permute-start.10 = (f32[32,128]{1,0:T(8,128)S(1)}, f32[32,128]{1,0:T(8,128)S(1)}, u32[]{:S(2)}, u32[]{:S(2)}) collective-permute-start(f32[32,128]{1,0:T(8,128)S(1)} %get-tuple-element.33), channel_id=1, source_target_pairs={{0,6},{1,7},{2,4},{3,5},{4,2},{5,3},{6,0},{7,1},{8,14},{9,15},{10,... | collective-permute-start | bytes 49160 | tf_op jit(solution)/shard_map/ppermute | solution.py:579
where the time goes:
time: 54.7 us; the launch traced here: 54.4 us
  starting transfers between devices  21.9 us (40%)
  waiting for transfers between devices  18.1 us (33%)
  Pallas kernels  10 us (18%)
  local copies, waits for them, and re-layouts  3.47 us (6%)
  between operations  0.79 us (1%)
    ppermute x12, waiting for transfers between devices, swap(): lax.ppermute(block, 'col', [(i, i ^ step) for i in range(cols_total)])  11.9 us
    ppermute x12, starting transfers between devices, swap(): lax.ppermute(block, 'col', [(i, i ^ step) for i in range(cols_total)])  11.4 us
    ppermute x6, starting transfers between devices, turn(): return lax.ppermute(block, 'row', pairs)  10.5 us
    ppermute x6, waiting for transfers between devices, turn(): return lax.ppermute(block, 'row', pairs)  6.22 us
    pallas_call x1, Pallas kernels, finish(): pl.pallas_call(functools.partial(finish_kernel, half, width, rows_total),...  4.54 us
    unnamed x20, local copies, waits for them, and re-layouts  3.47 us
    pallas_call x2, Pallas kernels, solve_part(): pl.pallas_call(functools.partial(solve_kernel, width), grid_spec=pltpu.Pr...  2.8 us
    pallas_call x1, Pallas kernels, grams(): pl.pallas_call(functools.partial(gram_kernel, half, width), in_specs=[pl....  1.22 us
  transfers between devices with their start and end apart: 18, of which 15 were waited for; matrix products, arithmetic and copies ran while one was open for 0% of the time, Pallas kernels for 7%

commit v1 on v0

--- a/solution.py
+++ b/solution.py
@@ -18,7 +18,6 @@
 F32 = jnp.float32
 BF16 = jnp.bfloat16
 VMEM = pltpu.VMEM
-SMEM = pltpu.SMEM
 
 
 def spread(block, axis, owner):
@@ -163,225 +162,261 @@
     return pltpu.CompilerParams(vmem_limit_bytes=mebibytes << 20)
 
 
-def solve_kernel(width, info, right_ref, inverse_ref, out_ref):
+def line_mask(tile_lines, ranks):
+    width = tile_lines // ranks.shape[0]
+    keep = (jnp.arange(width, dtype=jnp.int32)[None, :] < ranks[:, None]).astype(F32).reshape(-1)
+    return (
+        jnp.broadcast_to(keep[:, None], (tile_lines, LANES)),
+        jnp.broadcast_to(keep[None, :], (8, tile_lines)),
+    )
+
+
+def in_vmem(count):
+    return [pl.BlockSpec(memory_space=VMEM)] * count
+
+
+def small_cost(bytes_accessed, flops=0):
+    return pl.CostEstimate(flops=flops, bytes_accessed=bytes_accessed, transcendentals=0)
+
+
+def solve_kernel(odd, right_hbm, inverse_hbm, out_ref, right_ref, inverse_ref, sems):
+    parts = out_ref.shape[0]
+    piece = right_ref.shape[1]
+    my_col = lax.axis_index("col")
+    first = pltpu.make_async_copy(right_hbm, right_ref, sems.at[parts])
+    first.start()
+    copies = []
+    for step in range(parts):
+        block = my_col ^ (2 * step + odd)
+        copy = pltpu.make_async_copy(
+            inverse_hbm.at[pl.ds(pl.multiple_of(block * piece, piece), piece)],
+            inverse_ref.at[step],
+            sems.at[step],
+        )
+        copy.start()
+        copies.append(copy)
+    first.wait()
     right = right_ref[...]
-    rows = lax.broadcasted_iota(jnp.int32, right.shape, 0)
-    keep = jnp.zeros(right.shape, jnp.bool_)
-    for tile in range(right.shape[0] // width):
-        keep |= (rows >= tile * width) & (rows < tile * width + info[2 + tile])
-    masked = jnp.where(keep, right, jnp.zeros((), right.dtype))
-    out_ref[0] = nt(masked, inverse_ref[...])
-
-
-def solve_part(info, right, inverse, odd, parts, width):
+    for step, copy in enumerate(copies):
+        copy.wait()
+        out_ref[step] = nt(right, inverse_ref[step])
+
+
+def solve_part(right, inverse, odd, parts):
     lines, piece = right.shape
     return pl.pallas_call(
-        functools.partial(solve_kernel, width),
-        grid_spec=pltpu.PrefetchScalarGridSpec(
-            num_scalar_prefetch=1,
-            grid=(parts,),
-            in_specs=[
-                pl.BlockSpec((lines, piece), lambda step, info: (0, 0)),
-                pl.BlockSpec((piece, piece), lambda step, info: (info[1] ^ (2 * step + odd), 0)),
-            ],
-            out_specs=pl.BlockSpec((1, lines, piece), lambda step, info: (step, 0, 0)),
-        ),
+        functools.partial(solve_kernel, odd),
+        in_specs=[pl.BlockSpec(memory_space=pltpu.HBM)] * 2,
+        out_specs=pl.BlockSpec(memory_space=VMEM),
         out_shape=jax.ShapeDtypeStruct((parts, lines, piece), F32),
+        scratch_shapes=[
+            VMEM((lines, piece), BF16),
+            VMEM((parts, piece, piece), BF16),
+            pltpu.SemaphoreType.DMA((parts + 1,)),
+        ],
         name="solve_odd" if odd else "solve_even",
         compiler_params=grant(4),
-        cost_estimate=pl.CostEstimate(
-            flops=2 * parts * lines * piece * piece,
-            bytes_accessed=2 * parts * piece * piece + 4 * parts * lines * piece,
-            transcendentals=0,
+        cost_estimate=small_cost(
+            2 * parts * piece * piece + 4 * parts * lines * piece,
+            2 * parts * lines * piece * piece,
         ),
-    )(info, right, inverse)
-
-
-def pair_add_kernel(parts, mine_ref, other_ref, keep_ref, *send_refs):
+    )(right, inverse)
+
+
+def pair_add_kernel(mine_ref, other_ref, keep_ref, *send_refs):
     keep_ref[...] = mine_ref[0] + other_ref[0]
-    for step in range(1, parts):
-        send_refs[step - 1][...] = (mine_ref[step] + other_ref[step]).astype(
-            send_refs[step - 1].dtype
-        )
-
-
-def in_vmem(count):
-    return [pl.BlockSpec(memory_space=VMEM)] * count
-
-
-def small_cost(bytes_accessed, flops=0):
-    return pl.CostEstimate(flops=flops, bytes_accessed=bytes_accessed, transcendentals=0)
-
-
-def pair_add(mine, other, send_type):
-    parts = mine.shape[0]
-    shape = mine.shape[1:]
+    for step, ref in enumerate(send_refs):
+        ref[...] = (mine_ref[step + 1] + other_ref[step + 1]).astype(BF16)
+
+
+def pair_add(mine, other):
+    parts, lines, piece = mine.shape
     return pl.pallas_call(
-        functools.partial(pair_add_kernel, parts),
+        pair_add_kernel,
         in_specs=in_vmem(2),
         out_specs=in_vmem(parts),
-        out_shape=[jax.ShapeDtypeStruct(shape, F32)]
-        + [jax.ShapeDtypeStruct(shape, send_type)] * (parts - 1),
+        out_shape=[jax.ShapeDtypeStruct((lines, piece), F32)]
+        + [jax.ShapeDtypeStruct((lines, piece), BF16)] * (parts - 1),
         name="pair_add",
         compiler_params=grant(4),
         cost_estimate=small_cost(3 * mine.size * 4),
     )(mine, other)
 
 
-def gather_add_kernel(count, head_lines, *refs):
-    total = refs[0][...]
-    for ref in refs[1:count]:
+def gather_add_kernel(head, first_ref, panel_ref, mask_ref, *refs):
+    *others, solved_ref, head_ref = refs
+    total = first_ref[...]
+    for ref in others:
         total = total + ref[...].astype(F32)
-    rounded = total.astype(BF16)
-    refs[count][...] = rounded
-    refs[count + 1][...] = rounded[:head_lines]
-
-
-def gather_add(first, others, head_lines):
-    count = 1 + len(others)
+    keep = jnp.concatenate([mask_ref[...]] * (total.shape[1] // LANES), axis=1)
+    rounded = jnp.where(keep > 0.0, total, 0.0).astype(BF16)
+    solved_ref[...] = rounded
+    head_ref[:head] = rounded[:head]
+    head_ref[head:] = panel_ref[:head]
+
+
+def gather_add(first, panel, mask, others, head):
     return pl.pallas_call(
-        functools.partial(gather_add_kernel, count, head_lines),
-        in_specs=in_vmem(count),
+        functools.partial(gather_add_kernel, head),
+        in_specs=in_vmem(3 + len(others)),
         out_specs=in_vmem(2),
         out_shape=[
             jax.ShapeDtypeStruct(first.shape, BF16),
-            jax.ShapeDtypeStruct((head_lines, first.shape[1]), BF16),
+            jax.ShapeDtypeStruct((2 * head, first.shape[1]), BF16),
         ],
         name="gather_add",
         compiler_params=grant(4),
         cost_estimate=small_cost(first.size * 10),
-    )(first, *others)
-
-
-def core_kernel(rows_total, cols_total, width, info, own_ref, *refs):
+    )(first, panel, mask, *others)
+
+
+def bundle_kernel(*refs):
+    *pieces, out_ref = refs
+    for step, ref in enumerate(pieces):
+        out_ref[step] = ref[...]
+
+
+def bundle(pieces):
+    count = len(pieces)
+    return pl.pallas_call(
+        bundle_kernel,
+        in_specs=in_vmem(count),
+        out_specs=pl.BlockSpec(memory_space=VMEM),
+        out_shape=jax.ShapeDtypeStruct((count,) + pieces[0].shape, BF16),
+        name="bundle",
+        compiler_params=grant(4),
+        cost_estimate=small_cost(count * pieces[0].size * 4),
+    )(*pieces)
+
+
+def both_halves(value):
+    return jnp.concatenate(split(value), axis=1)
+
+
+def from_halves(value):
+    half = value.shape[1] // 2
+    return value[:, :half].astype(F32) + value[:, half:].astype(F32)
+
+
+def core_kernel(rows_total, cols_total, width, own_ref, panel_ref, *refs):
     others = refs[: rows_total - 1]
-    even_ref, odd_ref, stage = refs[rows_total - 1 :]
-    my_row, my_col = info[0], info[1]
+    even_ref, even_panel_ref, odd_ref, solved_stage, panel_stage = refs[rows_total - 1 :]
+    my_row, my_col = lax.axis_index("row"), lax.axis_index("col")
+    half = cols_total // 2
+    per_row = cols_total // rows_total
+    head = per_row * width
     for shift in range(rows_total):
-        source = own_ref if shift == 0 else others[shift - 1]
-        from_row = lax.rem(my_row - shift + rows_total, rows_total)
-        for index in range(cols_total // rows_total):
+        from_row = my_row ^ shift
+        for index in range(per_row):
             relative = my_col ^ (index * rows_total + from_row)
-            place = (relative & 1) * (cols_total // 2) + lax.shift_right_logical(relative, 1)
-            stage[place] = source[index * width : (index + 1) * width, :]
+            place = (relative & 1) * half + lax.shift_right_logical(relative, 1)
+            lines = slice(index * width, (index + 1) * width)
+            if shift == 0:
+                solved_stage[place] = own_ref[lines, :]
+                panel_stage[place] = panel_ref[lines, :]
+            else:
+                source = others[shift - 1]
+                solved_stage[place] = source[lines, :]
+                panel_stage[place] = source[head + index * width : head + (index + 1) * width, :]
     piece = own_ref.shape[1]
-    half = cols_total // 2
     own = own_ref[...]
-    for part, ref in ((1, odd_ref), (0, even_ref)):
-        block = stage[part * half : (part + 1) * half].reshape(half * width, piece)
-        ref[...] = nt(block, own).reshape(ref.shape)
-
-
-def core_parts(info, own, others, rows_total, cols_total, width):
+    odd_core = nt(solved_stage[half:].reshape(half * width, piece), own)
+    for step in range(half):
+        odd_ref[step, :width] = both_halves(odd_core[step * width : (step + 1) * width])
+        odd_ref[step, width:] = panel_stage[half + step]
+    even_ref[...] = nt(solved_stage[:half].reshape(half * width, piece), own).reshape(
+        even_ref.shape
+    )
+    even_panel_ref[...] = panel_stage[:half]
+
+
+def core_parts(own, panel, others, rows_total, cols_total, width):
     lines, piece = own.shape
     half = cols_total // 2
-    shape = jax.ShapeDtypeStruct((half, width, lines), F32)
     return pl.pallas_call(
         functools.partial(core_kernel, rows_total, cols_total, width),
-        in_specs=[pl.BlockSpec(memory_space=SMEM)] + in_vmem(rows_total),
-        out_specs=in_vmem(2),
-        out_shape=[shape, shape],
-        scratch_shapes=[VMEM((cols_total, width, piece), BF16)],
+        in_specs=in_vmem(1 + rows_total),
+        out_specs=in_vmem(3),
+        out_shape=[
+            jax.ShapeDtypeStruct((half, width, lines), F32),
+            jax.ShapeDtypeStruct((half, width, piece), BF16),
+            jax.ShapeDtypeStruct((half, 2 * width, piece), BF16),
+        ],
+        scratch_shapes=[VMEM((cols_total, width, piece), BF16)] * 2,
         name="core_parts",
         compiler_params=grant(4),
         cost_estimate=small_cost(400000, 2 * lines * piece * cols_total * width),
-    )(info, own, *others)
-
-
-def message_kernel(rows_total, cols_total, width, info, own_ref, *refs):
-    others = refs[: rows_total - 1]
-    message_refs = refs[rows_total - 1 : -1]
-    stage = refs[-1]
-    my_row, my_col = info[0], info[1]
-    lines = own_ref.shape[0]
-    for shift in range(rows_total):
-        source = own_ref if shift == 0 else others[shift - 1]
-        from_row = lax.rem(my_row - shift + rows_total, rows_total)
-        for index in range(cols_total // rows_total):
-            stage[index * rows_total + from_row] = source[index * width : (index + 1) * width, :]
-    for step, ref in enumerate(message_refs):
-        target = my_col ^ (2 * step)
-        ref[:width] = stage[target]
-        ref[width : width + lines] = own_ref[...]
-        ref[width + lines :] = stage[target ^ 1]
-
-
-def messages(info, own, others, rows_total, cols_total, width):
-    lines, piece = own.shape
-    half = cols_total // 2
+    )(own, panel, *others)
+
+
+def core_add_kernel(mine_ref, panel_ref, other_ref, keep_ref, keep_panel_ref, *send_refs):
+    width = mine_ref.shape[1]
+    for step in range(mine_ref.shape[0]):
+        total = mine_ref[step] + from_halves(other_ref[step, :width])
+        if step == 0:
+            keep_ref[...] = total
+            keep_panel_ref[:width] = panel_ref[0]
+            keep_panel_ref[width:] = other_ref[0, width:]
+        else:
+            ref = send_refs[step - 1]
+            ref[:width] = both_halves(total)
+            ref[width : 2 * width] = panel_ref[step]
+            ref[2 * width :] = other_ref[step, width:]
+
+
+def core_add(mine, panel, other):
+    half, width, lines = mine.shape
+    piece = panel.shape[2]
     return pl.pallas_call(
-        functools.partial(message_kernel, rows_total, cols_total, width),
-        in_specs=[pl.BlockSpec(memory_space=SMEM)] + in_vmem(rows_total),
-        out_specs=in_vmem(half),
-        out_shape=[jax.ShapeDtypeStruct((lines + 2 * width, piece), BF16)] * half,
-        scratch_shapes=[VMEM((cols_total, width, piece), BF16)],
-        name="messages",
+        core_add_kernel,
+        in_specs=in_vmem(3),
+        out_specs=in_vmem(1 + half),
+        out_shape=[
+            jax.ShapeDtypeStruct((width, lines), F32),
+            jax.ShapeDtypeStruct((2 * width, piece), BF16),
+        ]
+        + [jax.ShapeDtypeStruct((3 * width, piece), BF16)] * (half - 1),
+        name="core_add",
         compiler_params=grant(4),
-        cost_estimate=small_cost(half * (lines + 2 * width) * piece * 4),
-    )(info, own, *others)
-
-
-def bundle_kernel(count, width, *refs):
-    out_ref = refs[count]
-    for step in range(count):
-        out_ref[step] = refs[step][width:]
-
-
-def bundle(pieces, width):
-    lines, piece = pieces[0].shape
-    count = len(pieces)
+        cost_estimate=small_cost(1000000),
+    )(mine, panel, other)
+
+
+def piece_spot(relative, piece):
+    block = lax.axis_index("col") ^ relative
+    return pl.ds(pl.multiple_of(block * piece, LANES), piece)
+
+
+def gram_kernel(left_ref, right_ref, sketch_ref, even_ref, odd_ref, row_ref, column_ref):
+    half, _, piece = even_ref.shape
+    row_gram = jnp.zeros(row_ref.shape, F32)
+    column_gram = jnp.zeros(column_ref.shape, F32)
+    for relative in range(2 * half):
+        spot = piece_spot(relative, piece)
+        source = odd_ref if relative & 1 else even_ref
+        rows = jnp.concatenate([left_ref[:, spot], source[relative // 2]], axis=0)
+        row_gram = row_gram + nt(rows, rows)
+        right = right_ref[:, spot]
+        tall = jnp.concatenate([right, sketch_ref[:, spot]], axis=0)
+        column_gram = column_gram + nt(tall, right)
+    row_ref[...] = row_gram
+    column_ref[...] = column_gram
+
+
+def grams(left, right, sketch, even, odd):
+    lines, order = left.shape
     return pl.pallas_call(
-        functools.partial(bundle_kernel, count, width),
-        in_specs=in_vmem(count),
-        out_specs=pl.BlockSpec(memory_space=VMEM),
-        out_shape=jax.ShapeDtypeStruct((count, lines - width, piece), BF16),
-        name="bundle",
-        compiler_params=grant(4),
-        cost_estimate=small_cost(count * (lines - width) * piece * 4),
-    )(*pieces)
-
-
-def piece_views(even_refs, odd_ref, width, lines):
-    for step, ref in enumerate(even_refs):
-        yield 2 * step, ref.at[width : width + lines], ref.at[:width]
-    for step in range(len(even_refs)):
-        yield 2 * step + 1, odd_ref.at[step, :lines], odd_ref.at[step, lines:]
-
-
-def gram_kernel(half, width, info, left_ref, right_ref, sketch_ref, *refs):
-    even_refs = refs[:half]
-    odd_ref, row_gram_ref, column_gram_ref = refs[half:]
-    lines = left_ref.shape[0]
-    piece = odd_ref.shape[2]
-    my_col = info[1]
-    row_gram = jnp.zeros(row_gram_ref.shape, F32)
-    column_gram = jnp.zeros(column_gram_ref.shape, F32)
-    for relative, panel, column in piece_views(even_refs, odd_ref, width, lines):
-        spot = pl.ds(pl.multiple_of((my_col ^ relative) * piece, LANES), piece)
-        rows = jnp.concatenate([left_ref[:, spot], panel[...]], axis=0)
-        row_gram = row_gram + nt(rows, rows)
-        columns = jnp.concatenate([right_ref[:, spot], column[...]], axis=0)
-        tall = jnp.concatenate([columns, sketch_ref[:, spot]], axis=0)
-        column_gram = column_gram + nt(tall, columns)
-    row_gram_ref[...] = row_gram
-    column_gram_ref[...] = column_gram
-
-
-def grams(info, left, right, sketch, even, odd, width):
-    lines, order = left.shape
-    half = len(even)
-    return pl.pallas_call(
-        functools.partial(gram_kernel, half, width),
-        in_specs=[pl.BlockSpec(memory_space=SMEM)] + in_vmem(4 + half),
+        gram_kernel,
+        in_specs=in_vmem(5),
         out_specs=in_vmem(2),
         out_shape=[
             jax.ShapeDtypeStruct((2 * lines, 2 * lines), F32),
-            jax.ShapeDtypeStruct((lines + 2 * width, lines + width), F32),
+            jax.ShapeDtypeStruct((lines + sketch.shape[0], lines), F32),
         ],
         name="grams",
         compiler_params=grant(16),
         cost_estimate=small_cost(2000000, 2 * order * lines * lines * 8),
-    )(info, left, right, sketch, *even, odd)
+    )(left, right, sketch, even, odd)
 
 
 def factor_and_apply(gram, shift, bands):
@@ -421,12 +456,23 @@
     return [jnp.concatenate(band, axis=0) for band in bands]
 
 
-def finish_kernel(half, width, rows_total, info, *refs):
-    core_refs = refs[:half]
-    row_gram_ref, column_gram_ref, left_ref, right_ref = refs[half : half + 4]
-    even_refs = refs[half + 4 : 2 * half + 4]
-    odd_ref, out_left_ref, out_right_ref = refs[2 * half + 4 :]
-    my_row, my_col = info[0], info[1]
+def finish_kernel(half, width, rows_total, *refs):
+    core_ref, column_ref = refs[:2]
+    core_refs = refs[2 : half + 1]
+    (
+        row_gram_ref,
+        column_gram_ref,
+        left_ref,
+        right_ref,
+        sketch_ref,
+        even_ref,
+        odd_ref,
+        keep_line_ref,
+        keep_lane_ref,
+        out_left_ref,
+        out_right_ref,
+    ) = refs[half + 1 :]
+    my_row, my_col = lax.axis_index("row"), lax.axis_index("col")
     lines, order = left_ref.shape
     tiles = lines // width
     piece = odd_ref.shape[2]
@@ -443,17 +489,32 @@
     def blocks(value):
         return jnp.concatenate([stacked(value[:, :lines]), stacked(value[:, lines:])], axis=1)
 
+    def column_piece(relative):
+        step, side = divmod(relative, 2)
+        if step == 0:
+            return column_ref[side * width : (side + 1) * width]
+        return core_refs[step - 1][(1 + side) * width : (2 + side) * width]
+
+    keep_line = keep_line_ref[...] > 0.0
+    keep_lane = keep_lane_ref[:1] > 0.0
     lane_row = lax.broadcasted_iota(jnp.int32, (1, lines), 1)
-    line_col = lax.broadcasted_iota(jnp.int32, (lines, 1), 0)
-    keep_lane = jnp.zeros((1, lines), jnp.bool_)
-    keep_line = jnp.zeros((lines, 1), jnp.bool_)
     live_line = jnp.zeros((1, lines), jnp.bool_)
     for tile in range(tiles):
-        low, high = tile * width, tile * width + info[2 + tile]
-        keep_lane |= (lane_row >= low) & (lane_row < high)
-        keep_line |= (line_col >= low) & (line_col < high)
+        low = tile * width
         live = (tile * rows_total + my_row) > my_col
         live_line |= (lane_row >= low) & (lane_row < low + jnp.where(live, width, 0))
+
+    right_column = jnp.zeros((lines, width), F32)
+    column_column = jnp.zeros((width, width), F32)
+    sketch_column = jnp.zeros((width, width), F32)
+    for relative in range(2 * half):
+        spot = piece_spot(relative, piece)
+        column = column_piece(relative)
+        tall = nt(jnp.concatenate([right_ref[:, spot], column, sketch_ref[:, spot]], axis=0), column)
+        right_column = right_column + tall[:lines]
+        column_column = column_column + tall[lines : lines + width]
+        sketch_column = sketch_column + tall[lines + width :]
+    right_column = jnp.where(keep_line[:, :width], right_column, 0.0)
 
     row_gram = row_gram_ref[...]
     row_parts = split(
@@ -470,15 +531,12 @@
         )
     )
     column_gram = column_gram_ref[...]
-    right_right = jnp.where(same & keep_line & keep_lane, column_gram[:lines, :lines], 0.0)
-    right_column = jnp.where(keep_line, column_gram[:lines, lines:], 0.0)
-    column_column = column_gram[lines : lines + width, lines:]
-    sketch_right = jnp.where(keep_lane, column_gram[lines + width :, :lines], 0.0)
-    sketch_column = column_gram[lines + width :, lines:]
-
-    core = core_refs[0][...]
-    for ref in core_refs[1:]:
-        core = core + ref[...]
+    right_right = jnp.where(same & keep_line & keep_lane, column_gram[:lines], 0.0)
+    sketch_right = jnp.where(keep_lane, column_gram[lines:], 0.0)
+
+    core = core_ref[...]
+    for ref in core_refs:
+        core = core + from_halves(ref[:width])
     core_split = split(core)
     core_blocks = stacked(core)
     core_block_split = split(core_blocks)
@@ -534,26 +592,29 @@
             axis=1,
         )
     )
-    for relative, panel, column in piece_views(even_refs, odd_ref, width, lines):
-        spot = pl.ds(pl.multiple_of((my_col ^ relative) * piece, LANES), piece)
-        rows = jnp.concatenate([left_ref[:, spot], panel[...]], axis=0)
+    for relative in range(2 * half):
+        spot = piece_spot(relative, piece)
+        source = odd_ref if relative & 1 else even_ref
+        rows = jnp.concatenate([left_ref[:, spot], source[relative // 2]], axis=0)
         out_left_ref[:, spot] = fold(nn(left_small, rows)).astype(BF16)
-        columns = jnp.concatenate([right_ref[:, spot]] + [column[...]] * tiles, axis=0)
+        columns = jnp.concatenate([right_ref[:, spot]] + [column_piece(relative)] * tiles, axis=0)
         out_right_ref[:, spot] = fold(nn(right_small, columns)).astype(BF16)
 
 
-def finish(info, cores, row_gram, column_gram, left, right, even, odd, rows_total, width):
-    half = len(even)
+def finish(core, column, cores, others, rows_total, width):
+    half = len(cores) + 1
+    left = others[2]
     shape = jax.ShapeDtypeStruct(left.shape, BF16)
+    operands = (core, column, *cores, *others)
     return pl.pallas_call(
         functools.partial(finish_kernel, half, width, rows_total),
-        in_specs=[pl.BlockSpec(memory_space=SMEM)] + in_vmem(2 * half + 5),
+        in_specs=in_vmem(len(operands)),
         out_specs=in_vmem(2),
         out_shape=[shape, shape],
         name="finish",
         compiler_params=grant(16),
         cost_estimate=small_cost(5000000, 10**9),
-    )(info, *cores, row_gram, column_gram, left, right, *even, odd)
+    )(*operands)
 
 
 def flat_lines(block):
@@ -567,9 +628,6 @@
     cols_total = lax.axis_size("col")
     width = panel_left.shape[-1]
     half = cols_total // 2
-    place = jnp.stack([lax.axis_index("row"), lax.axis_index("col")]).astype(jnp.int32)
-    panel_info = jnp.concatenate([place, panel_ranks])
-    slab_info = jnp.concatenate([place, slab_ranks.reshape(-1)])
     left, right = flat_lines(slab_left), flat_lines(slab_right)
     panel, solve_right = flat_lines(panel_left), flat_lines(panel_right)
     sketch_lines = flat_lines(sketch)
@@ -579,7 +637,7 @@
         return lax.ppermute(block, "col", [(i, i ^ step) for i in range(cols_total)])
 
     def turn(block, shift):
-        pairs = [(i, (i + shift) % rows_total) for i in range(rows_total)]
+        pairs = [(i, i ^ shift) for i in range(rows_total)]
         return lax.ppermute(block, "row", pairs)
 
     def across(blocks):
@@ -588,35 +646,41 @@
     def along(block):
         return [turn(block, shift) for shift in range(1, rows_total)]
 
-    odd = solve_part(panel_info, solve_right, inverse_factor, 1, half, width)
+    panel_keep, _ = line_mask(panel.shape[0], panel_ranks)
+    slab_line, slab_lane = line_mask(panel.shape[0], slab_ranks.reshape(-1))
+    solve_right = pltpu.with_memory_space_constraint(solve_right, pltpu.HBM)
+    inverse_factor = pltpu.with_memory_space_constraint(inverse_factor, pltpu.HBM)
+    odd = solve_part(solve_right, inverse_factor, 1, half)
     other = swap(odd, 1)
-    even = solve_part(panel_info, solve_right, inverse_factor, 0, half, width)
-    kept, *sends = pair_add(even, other, BF16)
+    even = solve_part(solve_right, inverse_factor, 0, half)
+    kept, *sends = pair_add(even, other)
     received = across(sends)
-    panel_others = along(panel[:head])
-    solved, solved_head = gather_add(kept, received, head)
+    solved, solved_head = gather_add(kept, panel, panel_keep, received, head)
     solved_others = along(solved_head)
-    own_message, *sends = messages(slab_info, panel, panel_others, rows_total, cols_total, width)
-    even_pieces = [own_message] + across(sends)
-    core_even, core_odd = core_parts(
-        slab_info, solved, solved_others, rows_total, cols_total, width
-    )
-    core_other = swap(core_odd, 1)
-    odd_pieces = swap(bundle(even_pieces, width), 1)
-    core_kept, *sends = pair_add(core_even, core_other, F32)
-    cores = [core_kept] + across(sends)
-    row_gram, column_gram = grams(
-        slab_info, left, right, sketch_lines, even_pieces, odd_pieces, width
-    )
+    even_panel = bundle([panel] + across([panel] * (half - 1)))
+    odd_panel = swap(even_panel, 1)
+    row_gram, column_gram = grams(left, right, sketch_lines, even_panel, odd_panel)
+    core_even, even_column, odd_message = core_parts(
+        solved, panel, solved_others, rows_total, cols_total, width
+    )
+    other = swap(odd_message, 1)
+    core, column, *sends = core_add(core_even, even_column, other)
+    cores = across(sends)
     fresh_left, fresh_right = finish(
-        slab_info,
+        core,
+        column,
         cores,
-        row_gram,
-        column_gram,
-        left,
-        right,
-        even_pieces,
-        odd_pieces,
+        (
+            row_gram,
+            column_gram,
+            left,
+            right,
+            sketch_lines,
+            even_panel,
+            odd_panel,
+            slab_line,
+            slab_lane,
+        ),
         rows_total,
         width,
     )
@@ -636,6 +700,7 @@
         and piece_rows % LANES == 0
         and cols_total & (cols_total - 1) == 0
         and cols_total >= 4
+        and rows_total & (rows_total - 1) == 0
         and cols_total % rows_total == 0
         and rows_total > 1
         and cols_total <= tile_rows * rows_total

time: 54.7 us -> 40.7 us (0.74)
  waiting for transfers between devices: 18.1 us -> 12.9 us
  starting transfers between devices: 21.9 us -> 17.2 us
  local copies, waits for them, and re-layouts: 3.47 us -> 0.35 us
  Pallas kernels: 10 us -> 9.23 us
    ppermute x6 -> x3, starting transfers between devices: 10.5 us -> 4.45 us  [turn(): return lax.ppermute(block, 'row', pairs)]
    ppermute x12, waiting for transfers between devices: 11.9 us -> 7.14 us  [swap(): lax.ppermute(block, 'col', [(i, i ^ step) for i in range(cols_total)])]
    unnamed x20 -> x12, local copies, waits for them, and re-layouts: 3.47 us -> 0.03 us
    ppermute x12, starting transfers between devices: 11.4 us -> 12.7 us  [swap(): lax.ppermute(block, 'col', [(i, i ^ step) for i in range(cols_total)])]
    ppermute x6 -> x3, waiting for transfers between devices: 6.22 us -> 5.73 us  [turn(): return lax.ppermute(block, 'row', pairs)]
    pallas_call x8 -> x7, Pallas kernels: 4.75 us -> 4.52 us  [the longest x2 3.7 us: solve_part(): pl.pallas_call(functools.partial(solve_kernel, odd), in_specs=[pl.BlockSp...]
  transfers between devices with their start and end apart: 18 -> 15, of which waited for: 15 -> 8; matrix products, arithmetic and copies ran while one was open for 0% -> 1% of each run, Pallas kernels for 7% -> 7%
where the time goes in v1:
time: 40.7 us; the launch traced here: 40.6 us
  starting transfers between devices  17.2 us (42%)
  waiting for transfers between devices  12.9 us (32%)
  Pallas kernels  9.23 us (23%)
  between operations  0.79 us (2%)
    ppermute x12, starting transfers between devices, swap(): lax.ppermute(block, 'col', [(i, i ^ step) for i in range(cols_total)])  12.7 us
    ppermute x12, waiting for transfers between devices, swap(): lax.ppermute(block, 'col', [(i, i ^ step) for i in range(cols_total)])  7.14 us
    ppermute x3, waiting for transfers between devices, turn(): return lax.ppermute(block, 'row', pairs)  5.73 us
    pallas_call x1, Pallas kernels, finish(): pl.pallas_call(functools.partial(finish_kernel, half, width, rows_total),...  4.53 us
    ppermute x3, starting transfers between devices, turn(): return lax.ppermute(block, 'row', pairs)  4.45 us
    pallas_call x2, Pallas kernels, solve_part(): pl.pallas_call(functools.partial(solve_kernel, odd), in_specs=[pl.BlockSp...  3.7 us
  transfers between devices with their start and end apart: 15, of which 8 were waited for; matrix products, arithmetic and copies ran while one was open for 1% of the time, Pallas kernels for 7%

profile of v1, /device:TPU:0, one launch (start us, length us, event | category | flops | bytes accessed | tf_op | source)
XLA Modules:
  0.0 40.6 jit_solution(2608601714150970105)
XLA Ops:
  0.6 1.9 %solve_odd.1 = f32[4,128,256]{2,1,0:T(8,128)S(1)} custom-call(bf16[128,256]{1,0:T(8,128)(2,1)} %bitcast.36, bf16[2048,256]{1,0:T(8,128)(2,1)} %inverse_hbm.3), custom_call_target="tpu_custom_call" | custom-call | flops 67108864 | bytes 1048576 | tf_op jit(solution)/shard_map/solve_odd/pallas_call | solution.py:207
  2.5 0.6 %collective-permute-start = (f32[4,128,256]{2,1,0:T(8,128)S(1)}, f32[4,128,256]{2,1,0:T(8,128)S(1)}, u32[]{:S(2)}, u32[]{:S(2)}) collective-permute-start(f32[4,128,256]{2,1,0:T(8,128)S(1)} %solve_odd.1), channel_id=1, source_target_pairs={{0,1},{1,0},{2,3},{3,2},{4,5},{5,4},{6,7},{7,6},{8,9},{9,8},{10,11... | collective-permute-start | bytes 1572872 | tf_op jit(solution)/shard_map/ppermute | solution.py:637
  3.0 1.8 %solve_even.1.mine_ref = f32[4,128,256]{2,1,0:T(8,128)S(1)} custom-call(bf16[128,256]{1,0:T(8,128)(2,1)} %bitcast.37, bf16[2048,256]{1,0:T(8,128)(2,1)} %inverse_hbm.3), custom_call_target="tpu_custom_call" | custom-call | flops 67108864 | bytes 1048576 | tf_op jit(solution)/shard_map/solve_even/pallas_call | solution.py:207
  4.9 0.0 copy-start
  4.9 0.0 collective-permute-done.other_ref
  4.9 0.1 pair_add.1
  5.0 2.6 %collective-permute-start.1 = (bf16[128,256]{1,0:T(8,128)(2,1)S(1)}, bf16[128,256]{1,0:T(8,128)(2,1)S(1)}, u32[]{:S(2)}, u32[]{:S(2)}) collective-permute-start(bf16[128,256]{1,0:T(8,128)(2,1)S(1)} %get-tuple-element.21), channel_id=1, source_target_pairs={{0,2},{1,3},{2,0},{3,1},{4,6},{5,7},{6,4},{7,5},{8,10},{9,11},{10,... | collective-permute-start | bytes 196616 | tf_op jit(solution)/shard_map/ppermute | solution.py:637
  7.5 0.0 copy-done
  7.6 0.7 %collective-permute-start.11 = (bf16[128,256]{1,0:T(8,128)(2,1)S(1)}, bf16[128,256]{1,0:T(8,128)(2,1)S(1)}, u32[]{:S(2)}, u32[]{:S(2)}) collective-permute-start(bf16[128,256]{1,0:T(8,128)(2,1)S(1)} %bitcast.24), channel_id=1, source_target_pairs={{0,2},{1,3},{2,0},{3,1},{4,6},{5,7},{6,4},{7,5},{8,10},{9,11},{10,... | collective-permute-start | bytes 196616 | tf_op jit(solution)/shard_map/ppermute | solution.py:637
  8.2 1.5 %collective-permute-start.12 = (bf16[128,256]{1,0:T(8,128)(2,1)S(1)}, bf16[128,256]{1,0:T(8,128)(2,1)S(1)}, u32[]{:S(2)}, u32[]{:S(2)}) collective-permute-start(bf16[128,256]{1,0:T(8,128)(2,1)S(1)} %bitcast.25), channel_id=1, source_target_pairs={{0,4},{1,5},{2,6},{3,7},{4,0},{5,1},{6,2},{7,3},{8,12},{9,13},{10,... | collective-permute-start | bytes 196616 | tf_op jit(solution)/shard_map/ppermute | solution.py:637
  9.8 1.3 %collective-permute-start.13 = (bf16[128,256]{1,0:T(8,128)(2,1)S(1)}, bf16[128,256]{1,0:T(8,128)(2,1)S(1)}, u32[]{:S(2)}, u32[]{:S(2)}) collective-permute-start(bf16[128,256]{1,0:T(8,128)(2,1)S(1)} %bitcast.26), channel_id=1, source_target_pairs={{0,6},{1,7},{2,4},{3,5},{4,2},{5,3},{6,0},{7,1},{8,14},{9,15},{10,... | collective-permute-start | bytes 196616 | tf_op jit(solution)/shard_map/ppermute | solution.py:637
  11.0 0.0 copy-start.4
  11.0 1.5 %collective-permute-start.2 = (bf16[128,256]{1,0:T(8,128)(2,1)S(1)}, bf16[128,256]{1,0:T(8,128)(2,1)S(1)}, u32[]{:S(2)}, u32[]{:S(2)}) collective-permute-start(bf16[128,256]{1,0:T(8,128)(2,1)S(1)} %get-tuple-element.22), channel_id=1, source_target_pairs={{0,4},{1,5},{2,6},{3,7},{4,0},{5,1},{6,2},{7,3},{8,12},{9,13},{10,... | collective-permute-start | bytes 196616 | tf_op jit(solution)/shard_map/ppermute | solution.py:637
  12.6 0.0 collective-permute-done.1.refs_0_
  12.6 0.9 %collective-permute-start.3 = (bf16[128,256]{1,0:T(8,128)(2,1)S(1)}, bf16[128,256]{1,0:T(8,128)(2,1)S(1)}, u32[]{:S(2)}, u32[]{:S(2)}) collective-permute-start(bf16[128,256]{1,0:T(8,128)(2,1)S(1)} %get-tuple-element.23), channel_id=1, source_target_pairs={{0,6},{1,7},{2,4},{3,5},{4,2},{5,3},{6,0},{7,1},{8,14},{9,15},{10,... | collective-permute-start | bytes 196616 | tf_op jit(solution)/shard_map/ppermute | solution.py:637
  13.5 0.0 copy-done.4
  13.5 0.1 fusion
  13.5 0.1 reshape.77
  13.6 2.9 %collective-permute-done.2.refs_1_ = bf16[128,256]{1,0:T(8,128)(2,1)S(1)} collective-permute-done((bf16[128,256]{1,0:T(8,128)(2,1)S(1)}, bf16[128,256]{1,0:T(8,128)(2,1)S(1)}, u32[]{:S(2)}, u32[]{:S(2)}) %collective-permute-start.2) | collective-permute-done | bytes 65568 | tf_op jit(solution)/shard_map/ppermute | solution.py:637
  16.5 1.2 %collective-permute-done.3.refs_2_ = bf16[128,256]{1,0:T(8,128)(2,1)S(1)} collective-permute-done((bf16[128,256]{1,0:T(8,128)(2,1)S(1)}, bf16[128,256]{1,0:T(8,128)(2,1)S(1)}, u32[]{:S(2)}, u32[]{:S(2)}) %collective-permute-start.3) | collective-permute-done | bytes 65568 | tf_op jit(solution)/shard_map/ppermute | solution.py:637
  17.7 0.1 broadcast_in_dim.6.mask_ref
  17.8 0.0 copy-start.5
  17.8 0.0 copy-start.3
  17.9 0.0 copy-start.1
  17.9 0.0 copy-start.2
  17.9 1.6 %collective-permute-start.4 = (bf16[128,256]{1,0:T(8,128)(2,1)S(1)}, bf16[128,256]{1,0:T(8,128)(2,1)S(1)}, u32[]{:S(2)}, u32[]{:S(2)}) collective-permute-start(bf16[128,256]{1,0:T(8,128)(2,1)S(1)} %get-tuple-element.25), channel_id=1, source_target_pairs={{0,8},{8,0},{16,24},{24,16},{1,9},{9,1},{17,25},{25,17},{2,10},{10... | collective-permute-start | bytes 196616 | tf_op jit(solution)/shard_map/ppermute | solution.py:641
  19.5 2.6 %collective-permute-start.5 = (bf16[128,256]{1,0:T(8,128)(2,1)S(1)}, bf16[128,256]{1,0:T(8,128)(2,1)S(1)}, u32[]{:S(2)}, u32[]{:S(2)}) collective-permute-start(bf16[128,256]{1,0:T(8,128)(2,1)S(1)} %get-tuple-element.25), channel_id=1, source_target_pairs={{0,16},{8,24},{16,0},{24,8},{1,17},{9,25},{17,1},{25,9},{2,18},{10... | collective-permute-start | bytes 196616 | tf_op jit(solution)/shard_map/ppermute | solution.py:641
  22.1 0.0 collective-permute-done.11.refs_1_
  22.1 0.2 collective-permute-start.6
  22.4 0.0 collective-permute-done.12.refs_2_
  22.4 0.0 collective-permute-done.13.refs_3_
  22.4 0.1 collective-permute-start.14
  22.5 0.0 collective-permute-done.4.refs_0_
  22.5 3.6 %collective-permute-done.5.refs_1_ = bf16[128,256]{1,0:T(8,128)(2,1)S(1)} collective-permute-done((bf16[128,256]{1,0:T(8,128)(2,1)S(1)}, bf16[128,256]{1,0:T(8,128)(2,1)S(1)}, u32[]{:S(2)}, u32[]{:S(2)}) %collective-permute-start.5) | collective-permute-done | bytes 65568 | tf_op jit(solution)/shard_map/ppermute | solution.py:641
  26.1 2.1 %collective-permute-done.6.refs_2_ = bf16[128,256]{1,0:T(8,128)(2,1)S(1)} collective-permute-done((bf16[128,256]{1,0:T(8,128)(2,1)S(1)}, bf16[128,256]{1,0:T(8,128)(2,1)S(1)}, u32[]{:S(2)}, u32[]{:S(2)}) %collective-permute-start.6) | collective-permute-done | bytes 65568 | tf_op jit(solution)/shard_map/ppermute | solution.py:641
  28.2 0.2 core_parts.1
  28.4 0.1 collective-permute-start.7
  28.5 0.0 copy-done.5
  28.5 0.1 fusion.1
  28.6 0.1 reshape.78
  28.6 1.2 %collective-permute-done.7.other_ref = bf16[4,64,256]{2,1,0:T(8,128)(2,1)S(1)} collective-permute-done((bf16[4,64,256]{2,1,0:T(8,128)(2,1)S(1)}, bf16[4,64,256]{2,1,0:T(8,128)(2,1)S(1)}, u32[]{:S(2)}, u32[]{:S(2)}) %collective-permute-start.7) | collective-permute-done | bytes 131104 | tf_op jit(solution)/shard_map/ppermute | solution.py:637
  29.8 1.4 %collective-permute-start.10 = (bf16[96,256]{1,0:T(8,128)(2,1)S(1)}, bf16[96,256]{1,0:T(8,128)(2,1)S(1)}, u32[]{:S(2)}, u32[]{:S(2)}) collective-permute-start(bf16[96,256]{1,0:T(8,128)(2,1)S(1)} %get-tuple-element.33), channel_id=1, source_target_pairs={{0,6},{1,7},{2,4},{3,5},{4,2},{5,3},{6,0},{7,1},{8,14},{9,15},{10,... | collective-permute-start | bytes 147464 | tf_op jit(solution)/shard_map/ppermute | solution.py:637
  31.2 0.7 %collective-permute-start.8 = (bf16[96,256]{1,0:T(8,128)(2,1)S(1)}, bf16[96,256]{1,0:T(8,128)(2,1)S(1)}, u32[]{:S(2)}, u32[]{:S(2)}) collective-permute-start(bf16[96,256]{1,0:T(8,128)(2,1)S(1)} %get-tuple-element.31), channel_id=1, source_target_pairs={{0,2},{1,3},{2,0},{3,1},{4,6},{5,7},{6,4},{7,5},{8,10},{9,11},{10,... | collective-permute-start | bytes 147464 | tf_op jit(solution)/shard_map/ppermute | solution.py:637
  31.9 1.5 %collective-permute-start.9 = (bf16[96,256]{1,0:T(8,128)(2,1)S(1)}, bf16[96,256]{1,0:T(8,128)(2,1)S(1)}, u32[]{:S(2)}, u32[]{:S(2)}) collective-permute-start(bf16[96,256]{1,0:T(8,128)(2,1)S(1)} %get-tuple-element.32), channel_id=1, source_target_pairs={{0,4},{1,5},{2,6},{3,7},{4,0},{5,1},{6,2},{7,3},{8,12},{9,13},{10,... | collective-permute-start | bytes 147464 | tf_op jit(solution)/shard_map/ppermute | solution.py:637
  33.4 0.0 collective-permute-done.14.odd_ref.refs_11_
  33.4 0.0 copy-done.3
  33.4 0.0 copy-done.1
  33.4 0.0 copy-done.2
  33.4 0.7 %grams.1 = (f32[256,256]{1,0:T(8,128)S(1)}, f32[160,128]{1,0:T(8,128)S(1)}) custom-call(bf16[128,2048]{1,0:T(8,128)(2,1)S(1)} %bitcast.30, bf16[128,2048]{1,0:T(8,128)(2,1)S(1)} %bitcast.32, bf16[32,2048]{1,0:T(8,128)(2,1)S(1)} %bitcast.34, bf16[4,128,256]{2,1,0:T(8,128)(2,1)S(1)} %bundle.1.even_ref.refs_10_, ...), custom_call_target="tpu_custom_call" | custom-call | flops 536870912 | bytes 2000000 | tf_op jit(solution)/shard_map/grams/pallas_call | solution.py:408
  34.1 1.0 %collective-permute-done.10.refs_4_ = bf16[96,256]{1,0:T(8,128)(2,1)S(1)} collective-permute-done((bf16[96,256]{1,0:T(8,128)(2,1)S(1)}, bf16[96,256]{1,0:T(8,128)(2,1)S(1)}, u32[]{:S(2)}, u32[]{:S(2)}) %collective-permute-start.10) | collective-permute-done | bytes 49184 | tf_op jit(solution)/shard_map/ppermute | solution.py:637
  35.1 0.2 collective-permute-done.8.refs_2_
  35.3 0.7 %collective-permute-done.9.refs_3_ = bf16[96,256]{1,0:T(8,128)(2,1)S(1)} collective-permute-done((bf16[96,256]{1,0:T(8,128)(2,1)S(1)}, bf16[96,256]{1,0:T(8,128)(2,1)S(1)}, u32[]{:S(2)}, u32[]{:S(2)}) %collective-permute-start.9) | collective-permute-done | bytes 49184 | tf_op jit(solution)/shard_map/ppermute | solution.py:637
  36.0 0.1 broadcast_in_dim.7.refs_12_
  36.0 4.5 %finish.1 = (bf16[128,2048]{1,0:T(8,128)(2,1)}, bf16[128,2048]{1,0:T(8,128)(2,1)}) custom-call(f32[32,128]{1,0:T(8,128)S(1)} %get-tuple-element.29.refs_0_, bf16[64,256]{1,0:T(8,128)(2,1)S(1)} %get-tuple-element.30.refs_1_, bf16[96,256]{1,0:T(8,128)(2,1)S(1)} %collective-permute-done.8.refs_2_, bf16[96,256]{1,0:T(8,128)(2,1)S(1)} %collective-permute-done.9.refs_3_, ...), custom_call_target="tpu_custom_call" | custom-call | flops 1000000000 | bytes 5000000 | tf_op jit(solution)/shard_map/finish/pallas_call | solution.py:609
  (4 shorter events, 0.1 us)
Async XLA Ops:
  2.5 2.4 %collective-permute-start = (f32[4,128,256]{2,1,0:T(8,128)S(1)}, f32[4,128,256]{2,1,0:T(8,128)S(1)}, u32[]{:S(2)}, u32[]{:S(2)}) collective-permute-start(f32[4,128,256]{2,1,0:T(8,128)S(1)} %solve_odd.1), channel_id=1, source_target_pairs={{0,1},{1,0},{2,3},{3,2},{4,5},{5,4},{6,7},{7,6},{8,9},{9,8},{10,11... | collective-permute-start | bytes 1572872 | tf_op jit(solution)/shard_map/ppermute | solution.py:637
  4.9 2.6 %copy-start = (bf16[4,256,32]{1,2,0:T(8,128)(2,1)S(1)}, bf16[4,256,32]{1,2,0:T(8,128)(2,1)}, u32[]{:S(2)}) copy-start(bf16[4,256,32]{1,2,0:T(8,128)(2,1)} %param.11) | copy-start | bytes 196612
  5.0 7.6 %collective-permute-start.1 = (bf16[128,256]{1,0:T(8,128)(2,1)S(1)}, bf16[128,256]{1,0:T(8,128)(2,1)S(1)}, u32[]{:S(2)}, u32[]{:S(2)}) collective-permute-start(bf16[128,256]{1,0:T(8,128)(2,1)S(1)} %get-tuple-element.21), channel_id=1, source_target_pairs={{0,2},{1,3},{2,0},{3,1},{4,6},{5,7},{6,4},{7,5},{8,10},{9,11},{10,... | collective-permute-start | bytes 196616 | tf_op jit(solution)/shard_map/ppermute | solution.py:637
  7.6 14.6 %collective-permute-start.11 = (bf16[128,256]{1,0:T(8,128)(2,1)S(1)}, bf16[128,256]{1,0:T(8,128)(2,1)S(1)}, u32[]{:S(2)}, u32[]{:S(2)}) collective-permute-start(bf16[128,256]{1,0:T(8,128)(2,1)S(1)} %bitcast.24), channel_id=1, source_target_pairs={{0,2},{1,3},{2,0},{3,1},{4,6},{5,7},{6,4},{7,5},{8,10},{9,11},{10,... | collective-permute-start | bytes 196616 | tf_op jit(solution)/shard_map/ppermute | solution.py:637
  8.2 14.1 %collective-permute-start.12 = (bf16[128,256]{1,0:T(8,128)(2,1)S(1)}, bf16[128,256]{1,0:T(8,128)(2,1)S(1)}, u32[]{:S(2)}, u32[]{:S(2)}) collective-permute-start(bf16[128,256]{1,0:T(8,128)(2,1)S(1)} %bitcast.25), channel_id=1, source_target_pairs={{0,4},{1,5},{2,6},{3,7},{4,0},{5,1},{6,2},{7,3},{8,12},{9,13},{10,... | collective-permute-start | bytes 196616 | tf_op jit(solution)/shard_map/ppermute | solution.py:637
  9.8 12.6 %collective-permute-start.13 = (bf16[128,256]{1,0:T(8,128)(2,1)S(1)}, bf16[128,256]{1,0:T(8,128)(2,1)S(1)}, u32[]{:S(2)}, u32[]{:S(2)}) collective-permute-start(bf16[128,256]{1,0:T(8,128)(2,1)S(1)} %bitcast.26), channel_id=1, source_target_pairs={{0,6},{1,7},{2,4},{3,5},{4,2},{5,3},{6,0},{7,1},{8,14},{9,15},{10,... | collective-permute-start | bytes 196616 | tf_op jit(solution)/shard_map/ppermute | solution.py:637
  11.0 2.4 %copy-start.4 = (s32[4]{0:T(128)S(1)}, s32[4]{0:T(128)}, u32[]{:S(2)}) copy-start(s32[4]{0:T(128)} %param.13) | copy-start | bytes 52
  11.0 5.5 %collective-permute-start.2 = (bf16[128,256]{1,0:T(8,128)(2,1)S(1)}, bf16[128,256]{1,0:T(8,128)(2,1)S(1)}, u32[]{:S(2)}, u32[]{:S(2)}) collective-permute-start(bf16[128,256]{1,0:T(8,128)(2,1)S(1)} %get-tuple-element.22), channel_id=1, source_target_pairs={{0,4},{1,5},{2,6},{3,7},{4,0},{5,1},{6,2},{7,3},{8,12},{9,13},{10,... | collective-permute-start | bytes 196616 | tf_op jit(solution)/shard_map/ppermute | solution.py:637
  12.6 5.2 %collective-permute-start.3 = (bf16[128,256]{1,0:T(8,128)(2,1)S(1)}, bf16[128,256]{1,0:T(8,128)(2,1)S(1)}, u32[]{:S(2)}, u32[]{:S(2)}) collective-permute-start(bf16[128,256]{1,0:T(8,128)(2,1)S(1)} %get-tuple-element.23), channel_id=1, source_target_pairs={{0,6},{1,7},{2,4},{3,5},{4,2},{5,3},{6,0},{7,1},{8,14},{9,15},{10,... | collective-permute-start | bytes 196616 | tf_op jit(solution)/shard_map/ppermute | solution.py:637
  17.8 10.7 %copy-start.5 = (s32[4,1]{0,1:T(1,128)S(1)}, s32[4,1]{0,1:T(1,128)}, u32[]{:S(2)}) copy-start(s32[4,1]{0,1:T(1,128)} %param.10) | copy-start | bytes 52
  17.8 15.6 %copy-start.3 = (bf16[2048,32]{0,1:T(8,128)(2,1)S(1)}, bf16[2048,32]{0,1:T(8,128)(2,1)}, u32[]{:S(2)}) copy-start(bf16[2048,32]{0,1:T(8,128)(2,1)} %param.15) | copy-start | bytes 393220
  17.9 15.5 %copy-start.1 = (bf16[4,1,2048,32]{2,3,1,0:T(8,128)(2,1)S(1)}, bf16[4,1,2048,32]{2,3,1,0:T(8,128)(2,1)}, u32[]{:S(2)}) copy-start(bf16[4,1,2048,32]{2,3,1,0:T(8,128)(2,1)} %param.8) | copy-start | bytes 1572868
  17.9 15.5 %copy-start.2 = (bf16[4,1,2048,32]{2,3,1,0:T(8,128)(2,1)S(1)}, bf16[4,1,2048,32]{2,3,1,0:T(8,128)(2,1)}, u32[]{:S(2)}) copy-start(bf16[4,1,2048,32]{2,3,1,0:T(8,128)(2,1)} %param.9) | copy-start | bytes 1572868
  17.9 4.6 %collective-permute-start.4 = (bf16[128,256]{1,0:T(8,128)(2,1)S(1)}, bf16[128,256]{1,0:T(8,128)(2,1)S(1)}, u32[]{:S(2)}, u32[]{:S(2)}) collective-permute-start(bf16[128,256]{1,0:T(8,128)(2,1)S(1)} %get-tuple-element.25), channel_id=1, source_target_pairs={{0,8},{8,0},{16,24},{24,16},{1,9},{9,1},{17,25},{25,17},{2,10},{10... | collective-permute-start | bytes 196616 | tf_op jit(solution)/shard_map/ppermute | solution.py:641
  19.5 6.6 %collective-permute-start.5 = (bf16[128,256]{1,0:T(8,128)(2,1)S(1)}, bf16[128,256]{1,0:T(8,128)(2,1)S(1)}, u32[]{:S(2)}, u32[]{:S(2)}) collective-permute-start(bf16[128,256]{1,0:T(8,128)(2,1)S(1)} %get-tuple-element.25), channel_id=1, source_target_pairs={{0,16},{8,24},{16,0},{24,8},{1,17},{9,25},{17,1},{25,9},{2,18},{10... | collective-permute-start | bytes 196616 | tf_op jit(solution)/shard_map/ppermute | solution.py:641
  22.1 6.1 %collective-permute-start.6 = (bf16[128,256]{1,0:T(8,128)(2,1)S(1)}, bf16[128,256]{1,0:T(8,128)(2,1)S(1)}, u32[]{:S(2)}, u32[]{:S(2)}) collective-permute-start(bf16[128,256]{1,0:T(8,128)(2,1)S(1)} %get-tuple-element.25), channel_id=1, source_target_pairs={{0,24},{8,16},{16,8},{24,0},{1,25},{9,17},{17,9},{25,1},{2,26},{10... | collective-permute-start | bytes 196616 | tf_op jit(solution)/shard_map/ppermute | solution.py:641
  22.4 11.0 %collective-permute-start.14 = (bf16[4,128,256]{2,1,0:T(8,128)(2,1)S(1)}, bf16[4,128,256]{2,1,0:T(8,128)(2,1)S(1)}, u32[]{:S(2)}, u32[]{:S(2)}) collective-permute-start(bf16[4,128,256]{2,1,0:T(8,128)(2,1)S(1)} %bundle.1.even_ref.refs_10_), channel_id=1, source_target_pairs={{0,1},{1,0},{2,3},{3,2},{4,5},{5,4},{6,7},{7,6},{8,9},{9,8},{10,11... | collective-permute-start | bytes 786440 | tf_op jit(solution)/shard_map/ppermute | solution.py:637
  28.4 1.4 %collective-permute-start.7 = (bf16[4,64,256]{2,1,0:T(8,128)(2,1)S(1)}, bf16[4,64,256]{2,1,0:T(8,128)(2,1)S(1)}, u32[]{:S(2)}, u32[]{:S(2)}) collective-permute-start(bf16[4,64,256]{2,1,0:T(8,128)(2,1)S(1)} %get-tuple-element.28), channel_id=1, source_target_pairs={{0,1},{1,0},{2,3},{3,2},{4,5},{5,4},{6,7},{7,6},{8,9},{9,8},{10,11... | collective-permute-start | bytes 393224 | tf_op jit(solution)/shard_map/ppermute | solution.py:637
  29.8 5.3 %collective-permute-start.10 = (bf16[96,256]{1,0:T(8,128)(2,1)S(1)}, bf16[96,256]{1,0:T(8,128)(2,1)S(1)}, u32[]{:S(2)}, u32[]{:S(2)}) collective-permute-start(bf16[96,256]{1,0:T(8,128)(2,1)S(1)} %get-tuple-element.33), channel_id=1, source_target_pairs={{0,6},{1,7},{2,4},{3,5},{4,2},{5,3},{6,0},{7,1},{8,14},{9,15},{10,... | collective-permute-start | bytes 147464 | tf_op jit(solution)/shard_map/ppermute | solution.py:637
  31.2 4.1 %collective-permute-start.8 = (bf16[96,256]{1,0:T(8,128)(2,1)S(1)}, bf16[96,256]{1,0:T(8,128)(2,1)S(1)}, u32[]{:S(2)}, u32[]{:S(2)}) collective-permute-start(bf16[96,256]{1,0:T(8,128)(2,1)S(1)} %get-tuple-element.31), channel_id=1, source_target_pairs={{0,2},{1,3},{2,0},{3,1},{4,6},{5,7},{6,4},{7,5},{8,10},{9,11},{10,... | collective-permute-start | bytes 147464 | tf_op jit(solution)/shard_map/ppermute | solution.py:637
  31.9 4.1 %collective-permute-start.9 = (bf16[96,256]{1,0:T(8,128)(2,1)S(1)}, bf16[96,256]{1,0:T(8,128)(2,1)S(1)}, u32[]{:S(2)}, u32[]{:S(2)}) collective-permute-start(bf16[96,256]{1,0:T(8,128)(2,1)S(1)} %get-tuple-element.32), channel_id=1, source_target_pairs={{0,4},{1,5},{2,6},{3,7},{4,0},{5,1},{6,2},{7,3},{8,12},{9,13},{10,... | collective-permute-start | bytes 147464 | tf_op jit(solution)/shard_map/ppermute | solution.py:637

commit v2 on v1

--- a/solution.py
+++ b/solution.py
@@ -387,98 +387,146 @@
     return pl.ds(pl.multiple_of(block * piece, LANES), piece)
 
 
-def gram_kernel(left_ref, right_ref, sketch_ref, even_ref, odd_ref, row_ref, column_ref):
-    half, _, piece = even_ref.shape
-    row_gram = jnp.zeros(row_ref.shape, F32)
-    column_gram = jnp.zeros(column_ref.shape, F32)
-    for relative in range(2 * half):
-        spot = piece_spot(relative, piece)
-        source = odd_ref if relative & 1 else even_ref
-        rows = jnp.concatenate([left_ref[:, spot], source[relative // 2]], axis=0)
-        row_gram = row_gram + nt(rows, rows)
-        right = right_ref[:, spot]
-        tall = jnp.concatenate([right, sketch_ref[:, spot]], axis=0)
-        column_gram = column_gram + nt(tall, right)
-    row_ref[...] = row_gram
-    column_ref[...] = column_gram
-
-
-def grams(left, right, sketch, even, odd):
+def pieces_wide(ref, count, piece):
+    return jnp.concatenate([ref[:, piece_spot(k, piece)] for k in range(count)], axis=1)
+
+
+def same_tile(lines, width):
+    lane = lax.broadcasted_iota(jnp.int32, (lines, lines), 1)
+    line = lax.broadcasted_iota(jnp.int32, (lines, lines), 0)
+    return (lane // width) == (line // width)
+
+
+def gram_kernel(width, *refs):
+    left_ref, right_ref, sketch_ref, even_ref, odd_ref, keep_line_ref, keep_lane_ref = refs[:7]
+    row_high_ref, row_low_ref, right_gram_ref, sketch_right_ref = refs[7:]
+    half, lines, piece = even_ref.shape
+    count = 2 * half
+    same = same_tile(lines, width)
+    panel = jnp.concatenate(
+        [(odd_ref if k & 1 else even_ref)[k // 2] for k in range(count)], axis=1
+    )
+    left = pieces_wide(left_ref, count, piece)
+    for i, one in enumerate((left, panel)):
+        for j, two in enumerate((left, panel)):
+            high, low = split(jnp.where(same, nt(one, two), 0.0))
+            row_high_ref[i * lines : (i + 1) * lines, j * lines : (j + 1) * lines] = high
+            row_low_ref[i * lines : (i + 1) * lines, j * lines : (j + 1) * lines] = low
+    right = right_ref[...]
+    keep_line = keep_line_ref[...] > 0.0
+    keep_lane = keep_lane_ref[:1] > 0.0
+    right_gram_ref[...] = jnp.where(same & keep_line & keep_lane, nt(right, right), 0.0)
+    sketch_right_ref[...] = jnp.where(keep_lane, nt(sketch_ref[...], right), 0.0)
+
+
+def grams(left, right, sketch, even, odd, keep_line, keep_lane, width):
     lines, order = left.shape
+    square = jax.ShapeDtypeStruct((2 * lines, 2 * lines), BF16)
     return pl.pallas_call(
-        gram_kernel,
-        in_specs=in_vmem(5),
-        out_specs=in_vmem(2),
+        functools.partial(gram_kernel, width),
+        in_specs=in_vmem(7),
+        out_specs=in_vmem(4),
         out_shape=[
-            jax.ShapeDtypeStruct((2 * lines, 2 * lines), F32),
-            jax.ShapeDtypeStruct((lines + sketch.shape[0], lines), F32),
+            square,
+            square,
+            jax.ShapeDtypeStruct((lines, lines), F32),
+            jax.ShapeDtypeStruct((sketch.shape[0], lines), F32),
         ],
         name="grams",
         compiler_params=grant(16),
         cost_estimate=small_cost(2000000, 2 * order * lines * lines * 8),
-    )(left, right, sketch, even, odd)
+    )(left, right, sketch, even, odd, keep_line, keep_lane)
 
 
 def factor_and_apply(gram, shift, bands):
     width = gram.shape[0]
-    blocks = width // 8
+    count = width // 8
+    chunk = count // 2
     lanes = lax.broadcasted_iota(jnp.int32, (8, LANES), 1)
-    group = lanes - lax.rem(lanes, width)
+    inner_lane = lax.rem(lanes, width)
+    group = lanes - inner_lane
     sub = lax.broadcasted_iota(jnp.int32, (8, LANES), 0)
-    gram_rows = [gram[8 * b : 8 * b + 8] for b in range(blocks)]
-    bands = [[band[8 * b : 8 * b + 8] for b in range(blocks)] for band in bands]
-    rows = []
-    for k in range(width):
-        first = k // 8
-        rows.append(
+    inverse_shift = 1.0 / shift
+    matrix = [
+        gram[8 * b : 8 * b + 8] * inverse_shift + jnp.where(inner_lane == sub + 8 * b, 1.0, 0.0)
+        for b in range(count)
+    ]
+    bands = [matrix] + [[band[8 * b : 8 * b + 8] for b in range(count)] for band in bands]
+
+    def pick(vector, row):
+        return vector[row : row + 1]
+
+    for start in range(0, count, chunk):
+        first_column = 8 * start
+        columns = [
             {
-                b: jnp.take_along_axis(gram_rows[b], group + k, axis=1)
-                for b in range(first, blocks)
+                b: jnp.take_along_axis(matrix[b], group + first_column + k, axis=1)
+                for b in range(start + k // 8, count)
             }
-        )
-    for k in range(width):
-        first, inner = divmod(k, 8)
-        row = rows[k]
-        pivot = row[first][inner : inner + 1] + shift[:1]
-        scale = lax.rsqrt(pivot)
-        scaled = {b: row[b] * scale for b in row}
-        for i in range(k + 1, width):
-            lead = scaled[i // 8][i % 8 : i % 8 + 1]
-            for b in rows[i]:
-                rows[i][b] = rows[i][b] - lead * scaled[b]
-        below = dict(scaled)
-        below[first] = jnp.where(sub > inner, scaled[first], 0.0)
-        for band in bands:
-            done = band[first][inner : inner + 1] * scale
-            for b in range(first, blocks):
-                band[b] = band[b] - below[b] * done
-            band[first] = jnp.where(sub == inner, done, band[first])
-    return [jnp.concatenate(band, axis=0) for band in bands]
+            for k in range(8 * chunk)
+        ]
+        last_half = start + chunk == count
+        for k in range(0, 8 * chunk, 2):
+            b, row = start + k // 8, k % 8
+            one, two = columns[k], columns[k + 1]
+            corner = pick(one[b], row)
+            side = pick(one[b], row + 1)
+            other = pick(two[b], row + 1)
+            scale_one = lax.rsqrt(corner)
+            scale_two = (corner * scale_one) * lax.rsqrt(corner * other - side * side)
+            side = side * scale_one
+            one = {c: one[c] * scale_one for c in one}
+            two = {c: (two[c] - side * one[c]) * scale_two for c in two}
+            for i in range(k + 2, 8 * chunk):
+                c, place = start + i // 8, i % 8
+                lead_one, lead_two = pick(one[c], place), pick(two[c], place)
+                for d in columns[i]:
+                    columns[i][d] = columns[i][d] - lead_one * one[d] - lead_two * two[d]
+            below_one = dict(one)
+            below_two = dict(two)
+            below_one[b] = jnp.where(sub > row, one[b], 0.0)
+            below_two[b] = jnp.where(sub > row + 1, two[b], 0.0)
+            for number, band in enumerate(bands):
+                if number == 0 and last_half:
+                    continue
+                done_one = pick(band[b], row) * scale_one
+                done_two = (pick(band[b], row + 1) - side * done_one) * scale_two
+                for c in range(b, count):
+                    band[c] = band[c] - below_one[c] * done_one - below_two[c] * done_two
+                if number > 0:
+                    band[b] = jnp.where(
+                        sub == row, done_one, jnp.where(sub == row + 1, done_two, band[b])
+                    )
+    scale = lax.rsqrt(shift)
+    return [jnp.concatenate([part * scale for part in band], axis=0) for band in bands[1:]]
 
 
 def finish_kernel(half, width, rows_total, *refs):
     core_ref, column_ref = refs[:2]
     core_refs = refs[2 : half + 1]
     (
-        row_gram_ref,
-        column_gram_ref,
+        row_high_ref,
+        row_low_ref,
+        right_gram_ref,
+        sketch_right_ref,
         left_ref,
         right_ref,
         sketch_ref,
         even_ref,
         odd_ref,
-        keep_line_ref,
         keep_lane_ref,
+        out_left_hbm,
+        out_right_hbm,
         out_left_ref,
         out_right_ref,
+        sems,
     ) = refs[half + 1 :]
     my_row, my_col = lax.axis_index("row"), lax.axis_index("col")
     lines, order = left_ref.shape
     tiles = lines // width
     piece = odd_ref.shape[2]
-    lane = lax.broadcasted_iota(jnp.int32, (lines, lines), 1)
-    line = lax.broadcasted_iota(jnp.int32, (lines, lines), 0)
-    same = (lane // width) == (line // width)
+    count = 2 * half
+    same = same_tile(lines, width)
 
     def diagonal(value):
         return jnp.where(same, value, 0.0)
@@ -495,7 +543,6 @@
             return column_ref[side * width : (side + 1) * width]
         return core_refs[step - 1][(1 + side) * width : (2 + side) * width]
 
-    keep_line = keep_line_ref[...] > 0.0
     keep_lane = keep_lane_ref[:1] > 0.0
     lane_row = lax.broadcasted_iota(jnp.int32, (1, lines), 1)
     live_line = jnp.zeros((1, lines), jnp.bool_)
@@ -504,35 +551,9 @@
         live = (tile * rows_total + my_row) > my_col
         live_line |= (lane_row >= low) & (lane_row < low + jnp.where(live, width, 0))
 
-    right_column = jnp.zeros((lines, width), F32)
-    column_column = jnp.zeros((width, width), F32)
-    sketch_column = jnp.zeros((width, width), F32)
-    for relative in range(2 * half):
-        spot = piece_spot(relative, piece)
-        column = column_piece(relative)
-        tall = nt(jnp.concatenate([right_ref[:, spot], column, sketch_ref[:, spot]], axis=0), column)
-        right_column = right_column + tall[:lines]
-        column_column = column_column + tall[lines : lines + width]
-        sketch_column = sketch_column + tall[lines + width :]
-    right_column = jnp.where(keep_line[:, :width], right_column, 0.0)
-
-    row_gram = row_gram_ref[...]
-    row_parts = split(
-        jnp.concatenate(
-            [
-                jnp.concatenate(
-                    [diagonal(row_gram[:lines, :lines]), diagonal(row_gram[:lines, lines:])], axis=1
-                ),
-                jnp.concatenate(
-                    [diagonal(row_gram[lines:, :lines]), diagonal(row_gram[lines:, lines:])], axis=1
-                ),
-            ],
-            axis=0,
-        )
-    )
-    column_gram = column_gram_ref[...]
-    right_right = jnp.where(same & keep_line & keep_lane, column_gram[:lines], 0.0)
-    sketch_right = jnp.where(keep_lane, column_gram[lines:], 0.0)
+    columns = jnp.concatenate([column_piece(k) for k in range(count)], axis=1)
+    sketch_column = nt(pieces_wide(sketch_ref, count, piece), columns)
+    row_parts = (row_high_ref[...], row_low_ref[...])
 
     core = core_ref[...]
     for ref in core_refs:
@@ -541,7 +562,7 @@
     core_blocks = stacked(core)
     core_block_split = split(core_blocks)
 
-    first = jnp.concatenate([sketch_right, -dot_split(nn, sketch_column, core_split)], axis=1)
+    first = jnp.concatenate([sketch_right_ref[...], -dot_split(nn, sketch_column, core_split)], axis=1)
     ones = jnp.where(same, 1.0, 0.0).astype(BF16)
 
     def traced(one, two):
@@ -553,24 +574,27 @@
     image = dot_split(nn, first, row_parts)
     shift = traced(first, image)
     gram = dot_split(nt, first, split(blocks(image)))
+    tall = jnp.concatenate([pieces_wide(right_ref, count, piece), columns], axis=0)
+    column_wide = nt(columns, tall)
+    column_right = jnp.where(keep_lane, column_wide[:, :lines], 0.0)
+    core_lines = core.T
+    cross = -diagonal(dot_split(nn, core_lines, split(column_right)))
+    inner = dot_split(nn, column_wide[:, lines:], core_split)
+    corner = diagonal(dot_split(nn, core_lines, split(inner)))
+    middle = jnp.concatenate(
+        [
+            jnp.concatenate([right_gram_ref[...], cross.T], axis=1),
+            jnp.concatenate([cross, corner], axis=1),
+        ],
+        axis=0,
+    )
+    middle_parts = split(middle)
+    beyond_parts = split(dot_split(nn, middle, row_parts))
     top, bottom = factor_and_apply(gram, shift, [image[:, :lines], image[:, lines:]])
     basis = jnp.concatenate([top, bottom], axis=1)
 
-    cross = -diagonal(dot_split(nn, right_column, core_split))
-    inner = dot_split(nn, column_column, core_split)
-    core_lines = core.T
-    corner = diagonal(dot_split(nn, core_lines, split(inner)))
-    middle_parts = split(
-        jnp.concatenate(
-            [
-                jnp.concatenate([right_right, cross], axis=1),
-                jnp.concatenate([cross.T, corner], axis=1),
-            ],
-            axis=0,
-        )
-    )
     second = dot_split(nn, basis, middle_parts)
-    image = dot_split(nn, second, row_parts)
+    image = dot_split(nn, basis, beyond_parts)
     shift = traced(second, image)
     gram = dot_split(nt, second, split(blocks(image)))
     back = -dot_split(nt, image[:, lines:], core_block_split)
@@ -580,37 +604,51 @@
     factor_size = factor_scale * math.sqrt(order)
     live_scale = jnp.where(live_line, factor_size, 0.0)
     live_back = jnp.where(live_line, 1.0 / factor_size, 0.0)
-    left_small = wide(
-        jnp.concatenate([stacked(left_top * live_scale), stacked(left_bottom * live_scale)], axis=1)
-    )
-    right_small = wide(
-        jnp.concatenate(
-            [
-                stacked(jnp.where(keep_lane, right_top * live_back, 0.0)),
-                stacked(right_bottom * live_back),
-            ],
-            axis=1,
+    left_small = jnp.concatenate(
+        [stacked(left_top * live_scale), stacked(left_bottom * live_scale)], axis=1
+    ).astype(BF16)
+    right_small = jnp.concatenate(
+        [
+            stacked(jnp.where(keep_lane, right_top * live_back, 0.0)),
+            stacked(right_bottom * live_back),
+        ],
+        axis=1,
+    ).astype(BF16)
+    copies = []
+    for relative in range(count):
+        spot = piece_spot(relative, piece)
+        rows = jnp.concatenate(
+            [left_ref[:, spot], (odd_ref if relative & 1 else even_ref)[relative // 2]], axis=0
         )
-    )
-    for relative in range(2 * half):
-        spot = piece_spot(relative, piece)
-        source = odd_ref if relative & 1 else even_ref
-        rows = jnp.concatenate([left_ref[:, spot], source[relative // 2]], axis=0)
-        out_left_ref[:, spot] = fold(nn(left_small, rows)).astype(BF16)
-        columns = jnp.concatenate([right_ref[:, spot]] + [column_piece(relative)] * tiles, axis=0)
-        out_right_ref[:, spot] = fold(nn(right_small, columns)).astype(BF16)
+        out_left_ref[relative] = nn(left_small, rows).astype(BF16)
+        tall = jnp.concatenate([right_ref[:, spot]] + [column_piece(relative)] * tiles, axis=0)
+        out_right_ref[relative] = nn(right_small, tall).astype(BF16)
+        for side, (ref, hbm) in enumerate(
+            ((out_left_ref, out_left_hbm), (out_right_ref, out_right_hbm))
+        ):
+            copy = pltpu.make_async_copy(ref.at[relative], hbm.at[:, spot], sems.at[relative, side])
+            copy.start()
+            copies.append(copy)
+    for copy in copies:
+        copy.wait()
 
 
 def finish(core, column, cores, others, rows_total, width):
     half = len(cores) + 1
-    left = others[2]
+    left, panel = others[4], others[7]
+    lines, piece = panel.shape[1:]
     shape = jax.ShapeDtypeStruct(left.shape, BF16)
     operands = (core, column, *cores, *others)
     return pl.pallas_call(
         functools.partial(finish_kernel, half, width, rows_total),
         in_specs=in_vmem(len(operands)),
-        out_specs=in_vmem(2),
+        out_specs=[pl.BlockSpec(memory_space=pltpu.HBM)] * 2,
         out_shape=[shape, shape],
+        scratch_shapes=[
+            VMEM((2 * half, lines, piece), BF16),
+            VMEM((2 * half, lines, piece), BF16),
+            pltpu.SemaphoreType.DMA((2 * half, 2)),
+        ],
         name="finish",
         compiler_params=grant(16),
         cost_estimate=small_cost(5000000, 10**9),
@@ -659,7 +697,9 @@
     solved_others = along(solved_head)
     even_panel = bundle([panel] + across([panel] * (half - 1)))
     odd_panel = swap(even_panel, 1)
-    row_gram, column_gram = grams(left, right, sketch_lines, even_panel, odd_panel)
+    gram_parts = grams(
+        left, right, sketch_lines, even_panel, odd_panel, slab_line, slab_lane, width
+    )
     core_even, even_column, odd_message = core_parts(
         solved, panel, solved_others, rows_total, cols_total, width
     )
@@ -670,17 +710,7 @@
         core,
         column,
         cores,
-        (
-            row_gram,
-            column_gram,
-            left,
-            right,
-            sketch_lines,
-            even_panel,
-            odd_panel,
-            slab_line,
-            slab_lane,
-        ),
+        (*gram_parts, left, right, sketch_lines, even_panel, odd_panel, slab_lane),
         rows_total,
         width,
     )

time: 40.7 us -> 40 us (0.983)
    pallas_call x1, Pallas kernels: 4.53 us -> 3.92 us  [finish(): pl.pallas_call(functools.partial(finish_kernel, half, width, rows_total),...]
  transfers between devices with their start and end apart: 15 -> 15, of which waited for: 8 -> 8; matrix products, arithmetic and copies ran while one was open for 1% -> 1% of each run, Pallas kernels for 7% -> 8%
where the time goes in v2:
time: 40 us; the launch traced here: 39.9 us
  starting transfers between devices  17.2 us (43%)
  waiting for transfers between devices  12.5 us (31%)
  Pallas kernels  8.93 us (22%)
  between operations  0.79 us (2%)
    ppermute x12, starting transfers between devices, swap(): lax.ppermute(block, 'col', [(i, i ^ step) for i in range(cols_total)])  12.7 us
    ppermute x12, waiting for transfers between devices, swap(): lax.ppermute(block, 'col', [(i, i ^ step) for i in range(cols_total)])  6.75 us
    ppermute x3, waiting for transfers between devices, turn(): return lax.ppermute(block, 'row', pairs)  5.73 us
    ppermute x3, starting transfers between devices, turn(): return lax.ppermute(block, 'row', pairs)  4.45 us
    pallas_call x1, Pallas kernels, finish(): pl.pallas_call(functools.partial(finish_kernel, half, width, rows_total),...  3.92 us
    pallas_call x2, Pallas kernels, solve_part(): pl.pallas_call(functools.partial(solve_kernel, odd), in_specs=[pl.BlockSp...  3.7 us
    pallas_call x1, Pallas kernels, grams(): pl.pallas_call(functools.partial(gram_kernel, width), in_specs=in_vmem(7)...  0.99 us
  transfers between devices with their start and end apart: 15, of which 8 were waited for; matrix products, arithmetic and copies ran while one was open for 1% of the time, Pallas kernels for 8%

profile of v2, /device:TPU:0, one launch (start us, length us, event | category | flops | bytes accessed | tf_op | source)
XLA Modules:
  0.0 39.9 jit_solution(2744479295737689536)
XLA Ops:
  0.6 1.9 %solve_odd.1 = f32[4,128,256]{2,1,0:T(8,128)S(1)} custom-call(bf16[128,256]{1,0:T(8,128)(2,1)} %bitcast.36, bf16[2048,256]{1,0:T(8,128)(2,1)} %inverse_hbm.3), custom_call_target="tpu_custom_call" | custom-call | flops 67108864 | bytes 1048576 | tf_op jit(solution)/shard_map/solve_odd/pallas_call | solution.py:207
  2.5 0.6 %collective-permute-start = (f32[4,128,256]{2,1,0:T(8,128)S(1)}, f32[4,128,256]{2,1,0:T(8,128)S(1)}, u32[]{:S(2)}, u32[]{:S(2)}) collective-permute-start(f32[4,128,256]{2,1,0:T(8,128)S(1)} %solve_odd.1), channel_id=1, source_target_pairs={{0,1},{1,0},{2,3},{3,2},{4,5},{5,4},{6,7},{7,6},{8,9},{9,8},{10,11... | collective-permute-start | bytes 1572872 | tf_op jit(solution)/shard_map/ppermute | solution.py:675
  3.0 1.8 %solve_even.1.mine_ref = f32[4,128,256]{2,1,0:T(8,128)S(1)} custom-call(bf16[128,256]{1,0:T(8,128)(2,1)} %bitcast.37, bf16[2048,256]{1,0:T(8,128)(2,1)} %inverse_hbm.3), custom_call_target="tpu_custom_call" | custom-call | flops 67108864 | bytes 1048576 | tf_op jit(solution)/shard_map/solve_even/pallas_call | solution.py:207
  4.9 0.0 copy-start
  4.9 0.0 collective-permute-done.other_ref
  4.9 0.1 pair_add.1
  5.0 2.6 %collective-permute-start.1 = (bf16[128,256]{1,0:T(8,128)(2,1)S(1)}, bf16[128,256]{1,0:T(8,128)(2,1)S(1)}, u32[]{:S(2)}, u32[]{:S(2)}) collective-permute-start(bf16[128,256]{1,0:T(8,128)(2,1)S(1)} %get-tuple-element.23), channel_id=1, source_target_pairs={{0,2},{1,3},{2,0},{3,1},{4,6},{5,7},{6,4},{7,5},{8,10},{9,11},{10,... | collective-permute-start | bytes 196616 | tf_op jit(solution)/shard_map/ppermute | solution.py:675
  7.5 0.0 copy-done
  7.6 0.7 %collective-permute-start.11 = (bf16[128,256]{1,0:T(8,128)(2,1)S(1)}, bf16[128,256]{1,0:T(8,128)(2,1)S(1)}, u32[]{:S(2)}, u32[]{:S(2)}) collective-permute-start(bf16[128,256]{1,0:T(8,128)(2,1)S(1)} %bitcast.24), channel_id=1, source_target_pairs={{0,2},{1,3},{2,0},{3,1},{4,6},{5,7},{6,4},{7,5},{8,10},{9,11},{10,... | collective-permute-start | bytes 196616 | tf_op jit(solution)/shard_map/ppermute | solution.py:675
  8.2 1.5 %collective-permute-start.12 = (bf16[128,256]{1,0:T(8,128)(2,1)S(1)}, bf16[128,256]{1,0:T(8,128)(2,1)S(1)}, u32[]{:S(2)}, u32[]{:S(2)}) collective-permute-start(bf16[128,256]{1,0:T(8,128)(2,1)S(1)} %bitcast.25), channel_id=1, source_target_pairs={{0,4},{1,5},{2,6},{3,7},{4,0},{5,1},{6,2},{7,3},{8,12},{9,13},{10,... | collective-permute-start | bytes 196616 | tf_op jit(solution)/shard_map/ppermute | solution.py:675
  9.8 1.3 %collective-permute-start.13 = (bf16[128,256]{1,0:T(8,128)(2,1)S(1)}, bf16[128,256]{1,0:T(8,128)(2,1)S(1)}, u32[]{:S(2)}, u32[]{:S(2)}) collective-permute-start(bf16[128,256]{1,0:T(8,128)(2,1)S(1)} %bitcast.26), channel_id=1, source_target_pairs={{0,6},{1,7},{2,4},{3,5},{4,2},{5,3},{6,0},{7,1},{8,14},{9,15},{10,... | collective-permute-start | bytes 196616 | tf_op jit(solution)/shard_map/ppermute | solution.py:675
  11.0 0.0 copy-start.4
  11.0 1.5 %collective-permute-start.2 = (bf16[128,256]{1,0:T(8,128)(2,1)S(1)}, bf16[128,256]{1,0:T(8,128)(2,1)S(1)}, u32[]{:S(2)}, u32[]{:S(2)}) collective-permute-start(bf16[128,256]{1,0:T(8,128)(2,1)S(1)} %get-tuple-element.24), channel_id=1, source_target_pairs={{0,4},{1,5},{2,6},{3,7},{4,0},{5,1},{6,2},{7,3},{8,12},{9,13},{10,... | collective-permute-start | bytes 196616 | tf_op jit(solution)/shard_map/ppermute | solution.py:675
  12.6 0.0 collective-permute-done.1.refs_0_
  12.6 0.9 %collective-permute-start.3 = (bf16[128,256]{1,0:T(8,128)(2,1)S(1)}, bf16[128,256]{1,0:T(8,128)(2,1)S(1)}, u32[]{:S(2)}, u32[]{:S(2)}) collective-permute-start(bf16[128,256]{1,0:T(8,128)(2,1)S(1)} %get-tuple-element.25), channel_id=1, source_target_pairs={{0,6},{1,7},{2,4},{3,5},{4,2},{5,3},{6,0},{7,1},{8,14},{9,15},{10,... | collective-permute-start | bytes 196616 | tf_op jit(solution)/shard_map/ppermute | solution.py:675
  13.5 0.0 copy-done.4
  13.5 0.1 fusion
  13.5 0.1 reshape.77
  13.6 2.9 %collective-permute-done.2.refs_1_ = bf16[128,256]{1,0:T(8,128)(2,1)S(1)} collective-permute-done((bf16[128,256]{1,0:T(8,128)(2,1)S(1)}, bf16[128,256]{1,0:T(8,128)(2,1)S(1)}, u32[]{:S(2)}, u32[]{:S(2)}) %collective-permute-start.2) | collective-permute-done | bytes 65568 | tf_op jit(solution)/shard_map/ppermute | solution.py:675
  16.5 1.2 %collective-permute-done.3.refs_2_ = bf16[128,256]{1,0:T(8,128)(2,1)S(1)} collective-permute-done((bf16[128,256]{1,0:T(8,128)(2,1)S(1)}, bf16[128,256]{1,0:T(8,128)(2,1)S(1)}, u32[]{:S(2)}, u32[]{:S(2)}) %collective-permute-start.3) | collective-permute-done | bytes 65568 | tf_op jit(solution)/shard_map/ppermute | solution.py:675
  17.7 0.1 broadcast_in_dim.6.mask_ref
  17.8 0.0 copy-start.5
  17.9 0.0 copy-start.1
  17.9 0.0 copy-start.2
  17.9 1.6 %collective-permute-start.4 = (bf16[128,256]{1,0:T(8,128)(2,1)S(1)}, bf16[128,256]{1,0:T(8,128)(2,1)S(1)}, u32[]{:S(2)}, u32[]{:S(2)}) collective-permute-start(bf16[128,256]{1,0:T(8,128)(2,1)S(1)} %get-tuple-element.27), channel_id=1, source_target_pairs={{0,8},{8,0},{16,24},{24,16},{1,9},{9,1},{17,25},{25,17},{2,10},{10... | collective-permute-start | bytes 196616 | tf_op jit(solution)/shard_map/ppermute | solution.py:679
  19.5 2.6 %collective-permute-start.5 = (bf16[128,256]{1,0:T(8,128)(2,1)S(1)}, bf16[128,256]{1,0:T(8,128)(2,1)S(1)}, u32[]{:S(2)}, u32[]{:S(2)}) collective-permute-start(bf16[128,256]{1,0:T(8,128)(2,1)S(1)} %get-tuple-element.27), channel_id=1, source_target_pairs={{0,16},{8,24},{16,0},{24,8},{1,17},{9,25},{17,1},{25,9},{2,18},{10... | collective-permute-start | bytes 196616 | tf_op jit(solution)/shard_map/ppermute | solution.py:679
  22.1 0.0 collective-permute-done.11.refs_1_
  22.1 0.2 collective-permute-start.6
  22.3 0.0 collective-permute-done.12.refs_2_
  22.4 0.0 collective-permute-done.13.refs_3_
  22.4 0.1 collective-permute-start.14
  22.5 0.0 collective-permute-done.4.refs_0_
  22.5 3.6 %collective-permute-done.5.refs_1_ = bf16[128,256]{1,0:T(8,128)(2,1)S(1)} collective-permute-done((bf16[128,256]{1,0:T(8,128)(2,1)S(1)}, bf16[128,256]{1,0:T(8,128)(2,1)S(1)}, u32[]{:S(2)}, u32[]{:S(2)}) %collective-permute-start.5) | collective-permute-done | bytes 65568 | tf_op jit(solution)/shard_map/ppermute | solution.py:679
  26.1 2.1 %collective-permute-done.6.refs_2_ = bf16[128,256]{1,0:T(8,128)(2,1)S(1)} collective-permute-done((bf16[128,256]{1,0:T(8,128)(2,1)S(1)}, bf16[128,256]{1,0:T(8,128)(2,1)S(1)}, u32[]{:S(2)}, u32[]{:S(2)}) %collective-permute-start.6) | collective-permute-done | bytes 65568 | tf_op jit(solution)/shard_map/ppermute | solution.py:679
  28.2 0.2 core_parts.1
  28.4 0.1 collective-permute-start.7
  28.5 0.0 copy-done.5
  28.5 0.1 fusion.1
  28.5 0.1 reshape.78
  28.6 1.2 %collective-permute-done.7.other_ref = bf16[4,64,256]{2,1,0:T(8,128)(2,1)S(1)} collective-permute-done((bf16[4,64,256]{2,1,0:T(8,128)(2,1)S(1)}, bf16[4,64,256]{2,1,0:T(8,128)(2,1)S(1)}, u32[]{:S(2)}, u32[]{:S(2)}) %collective-permute-start.7) | collective-permute-done | bytes 131104 | tf_op jit(solution)/shard_map/ppermute | solution.py:675
  29.8 0.0 copy-start.3
  29.8 1.4 %collective-permute-start.10 = (bf16[96,256]{1,0:T(8,128)(2,1)S(1)}, bf16[96,256]{1,0:T(8,128)(2,1)S(1)}, u32[]{:S(2)}, u32[]{:S(2)}) collective-permute-start(bf16[96,256]{1,0:T(8,128)(2,1)S(1)} %get-tuple-element.35), channel_id=1, source_target_pairs={{0,6},{1,7},{2,4},{3,5},{4,2},{5,3},{6,0},{7,1},{8,14},{9,15},{10,... | collective-permute-start | bytes 147464 | tf_op jit(solution)/shard_map/ppermute | solution.py:675
  31.2 0.7 %collective-permute-start.8 = (bf16[96,256]{1,0:T(8,128)(2,1)S(1)}, bf16[96,256]{1,0:T(8,128)(2,1)S(1)}, u32[]{:S(2)}, u32[]{:S(2)}) collective-permute-start(bf16[96,256]{1,0:T(8,128)(2,1)S(1)} %get-tuple-element.33), channel_id=1, source_target_pairs={{0,2},{1,3},{2,0},{3,1},{4,6},{5,7},{6,4},{7,5},{8,10},{9,11},{10,... | collective-permute-start | bytes 147464 | tf_op jit(solution)/shard_map/ppermute | solution.py:675
  31.9 1.5 %collective-permute-start.9 = (bf16[96,256]{1,0:T(8,128)(2,1)S(1)}, bf16[96,256]{1,0:T(8,128)(2,1)S(1)}, u32[]{:S(2)}, u32[]{:S(2)}) collective-permute-start(bf16[96,256]{1,0:T(8,128)(2,1)S(1)} %get-tuple-element.34), channel_id=1, source_target_pairs={{0,4},{1,5},{2,6},{3,7},{4,0},{5,1},{6,2},{7,3},{8,12},{9,13},{10,... | collective-permute-start | bytes 147464 | tf_op jit(solution)/shard_map/ppermute | solution.py:675
  33.4 0.0 collective-permute-done.14.refs_4_.refs_13_
  33.4 0.1 broadcast_in_dim.7.refs_5_
  33.5 0.0 copy-done.1
  33.5 0.0 copy-done.2
  33.5 0.0 copy-done.3
  33.5 1.0 %grams.1 = (bf16[256,256]{1,0:T(8,128)(2,1)S(1)}, bf16[256,256]{1,0:T(8,128)(2,1)S(1)}, f32[128,128]{1,0:T(8,128)S(1)}, f32[32,128]{1,0:T(8,128)S(1)}) custom-call(bf16[128,2048]{1,0:T(8,128)(2,1)S(1)} %bitcast.30, bf16[128,2048]{1,0:T(8,128)(2,1)S(1)} %bitcast.32, bf16[32,2048]{1,0:T(8,128)(2,1)S(1)} %bitcast.34, ...), custom_call_target="tpu_custom_call" | custom-call | flops 536870912 | bytes 2000000 | tf_op jit(solution)/shard_map/grams/pallas_call | solution.py:425
  34.5 0.6 %collective-permute-done.10.refs_4_ = bf16[96,256]{1,0:T(8,128)(2,1)S(1)} collective-permute-done((bf16[96,256]{1,0:T(8,128)(2,1)S(1)}, bf16[96,256]{1,0:T(8,128)(2,1)S(1)}, u32[]{:S(2)}, u32[]{:S(2)}) %collective-permute-start.10) | collective-permute-done | bytes 49184 | tf_op jit(solution)/shard_map/ppermute | solution.py:675
  35.1 0.2 collective-permute-done.8.refs_2_
  35.3 0.7 %collective-permute-done.9.refs_3_ = bf16[96,256]{1,0:T(8,128)(2,1)S(1)} collective-permute-done((bf16[96,256]{1,0:T(8,128)(2,1)S(1)}, bf16[96,256]{1,0:T(8,128)(2,1)S(1)}, u32[]{:S(2)}, u32[]{:S(2)}) %collective-permute-start.9) | collective-permute-done | bytes 49184 | tf_op jit(solution)/shard_map/ppermute | solution.py:675
  35.9 3.9 %finish.1 = (bf16[128,2048]{1,0:T(8,128)(2,1)}, bf16[128,2048]{1,0:T(8,128)(2,1)}) custom-call(f32[32,128]{1,0:T(8,128)S(1)} %get-tuple-element.31.refs_0_, bf16[64,256]{1,0:T(8,128)(2,1)S(1)} %get-tuple-element.32.refs_1_, bf16[96,256]{1,0:T(8,128)(2,1)S(1)} %collective-permute-done.8.refs_2_, bf16[96,256]{1,0:T(8,128)(2,1)S(1)} %collective-permute-done.9.refs_3_, ...), custom_call_target="tpu_custom_call" | custom-call | flops 1000000000 | bytes 5000000 | tf_op jit(solution)/shard_map/finish/pallas_call | solution.py:642
  (4 shorter events, 0.1 us)
Async XLA Ops:
  2.5 2.4 %collective-permute-start = (f32[4,128,256]{2,1,0:T(8,128)S(1)}, f32[4,128,256]{2,1,0:T(8,128)S(1)}, u32[]{:S(2)}, u32[]{:S(2)}) collective-permute-start(f32[4,128,256]{2,1,0:T(8,128)S(1)} %solve_odd.1), channel_id=1, source_target_pairs={{0,1},{1,0},{2,3},{3,2},{4,5},{5,4},{6,7},{7,6},{8,9},{9,8},{10,11... | collective-permute-start | bytes 1572872 | tf_op jit(solution)/shard_map/ppermute | solution.py:675
  4.9 2.6 %copy-start = (bf16[4,256,32]{1,2,0:T(8,128)(2,1)S(1)}, bf16[4,256,32]{1,2,0:T(8,128)(2,1)}, u32[]{:S(2)}) copy-start(bf16[4,256,32]{1,2,0:T(8,128)(2,1)} %param.11) | copy-start | bytes 196612
  5.0 7.6 %collective-permute-start.1 = (bf16[128,256]{1,0:T(8,128)(2,1)S(1)}, bf16[128,256]{1,0:T(8,128)(2,1)S(1)}, u32[]{:S(2)}, u32[]{:S(2)}) collective-permute-start(bf16[128,256]{1,0:T(8,128)(2,1)S(1)} %get-tuple-element.23), channel_id=1, source_target_pairs={{0,2},{1,3},{2,0},{3,1},{4,6},{5,7},{6,4},{7,5},{8,10},{9,11},{10,... | collective-permute-start | bytes 196616 | tf_op jit(solution)/shard_map/ppermute | solution.py:675
  7.6 14.6 %collective-permute-start.11 = (bf16[128,256]{1,0:T(8,128)(2,1)S(1)}, bf16[128,256]{1,0:T(8,128)(2,1)S(1)}, u32[]{:S(2)}, u32[]{:S(2)}) collective-permute-start(bf16[128,256]{1,0:T(8,128)(2,1)S(1)} %bitcast.24), channel_id=1, source_target_pairs={{0,2},{1,3},{2,0},{3,1},{4,6},{5,7},{6,4},{7,5},{8,10},{9,11},{10,... | collective-permute-start | bytes 196616 | tf_op jit(solution)/shard_map/ppermute | solution.py:675
  8.2 14.1 %collective-permute-start.12 = (bf16[128,256]{1,0:T(8,128)(2,1)S(1)}, bf16[128,256]{1,0:T(8,128)(2,1)S(1)}, u32[]{:S(2)}, u32[]{:S(2)}) collective-permute-start(bf16[128,256]{1,0:T(8,128)(2,1)S(1)} %bitcast.25), channel_id=1, source_target_pairs={{0,4},{1,5},{2,6},{3,7},{4,0},{5,1},{6,2},{7,3},{8,12},{9,13},{10,... | collective-permute-start | bytes 196616 | tf_op jit(solution)/shard_map/ppermute | solution.py:675
  9.8 12.6 %collective-permute-start.13 = (bf16[128,256]{1,0:T(8,128)(2,1)S(1)}, bf16[128,256]{1,0:T(8,128)(2,1)S(1)}, u32[]{:S(2)}, u32[]{:S(2)}) collective-permute-start(bf16[128,256]{1,0:T(8,128)(2,1)S(1)} %bitcast.26), channel_id=1, source_target_pairs={{0,6},{1,7},{2,4},{3,5},{4,2},{5,3},{6,0},{7,1},{8,14},{9,15},{10,... | collective-permute-start | bytes 196616 | tf_op jit(solution)/shard_map/ppermute | solution.py:675
  11.0 2.4 %copy-start.4 = (s32[4]{0:T(128)S(1)}, s32[4]{0:T(128)}, u32[]{:S(2)}) copy-start(s32[4]{0:T(128)} %param.13) | copy-start | bytes 52
  11.0 5.5 %collective-permute-start.2 = (bf16[128,256]{1,0:T(8,128)(2,1)S(1)}, bf16[128,256]{1,0:T(8,128)(2,1)S(1)}, u32[]{:S(2)}, u32[]{:S(2)}) collective-permute-start(bf16[128,256]{1,0:T(8,128)(2,1)S(1)} %get-tuple-element.24), channel_id=1, source_target_pairs={{0,4},{1,5},{2,6},{3,7},{4,0},{5,1},{6,2},{7,3},{8,12},{9,13},{10,... | collective-permute-start | bytes 196616 | tf_op jit(solution)/shard_map/ppermute | solution.py:675
  12.6 5.2 %collective-permute-start.3 = (bf16[128,256]{1,0:T(8,128)(2,1)S(1)}, bf16[128,256]{1,0:T(8,128)(2,1)S(1)}, u32[]{:S(2)}, u32[]{:S(2)}) collective-permute-start(bf16[128,256]{1,0:T(8,128)(2,1)S(1)} %get-tuple-element.25), channel_id=1, source_target_pairs={{0,6},{1,7},{2,4},{3,5},{4,2},{5,3},{6,0},{7,1},{8,14},{9,15},{10,... | collective-permute-start | bytes 196616 | tf_op jit(solution)/shard_map/ppermute | solution.py:675
  17.8 10.7 %copy-start.5 = (s32[4,1]{0,1:T(1,128)S(1)}, s32[4,1]{0,1:T(1,128)}, u32[]{:S(2)}) copy-start(s32[4,1]{0,1:T(1,128)} %param.10) | copy-start | bytes 52
  17.9 15.6 %copy-start.1 = (bf16[4,1,2048,32]{2,3,1,0:T(8,128)(2,1)S(1)}, bf16[4,1,2048,32]{2,3,1,0:T(8,128)(2,1)}, u32[]{:S(2)}) copy-start(bf16[4,1,2048,32]{2,3,1,0:T(8,128)(2,1)} %param.8) | copy-start | bytes 1572868
  17.9 15.6 %copy-start.2 = (bf16[4,1,2048,32]{2,3,1,0:T(8,128)(2,1)S(1)}, bf16[4,1,2048,32]{2,3,1,0:T(8,128)(2,1)}, u32[]{:S(2)}) copy-start(bf16[4,1,2048,32]{2,3,1,0:T(8,128)(2,1)} %param.9) | copy-start | bytes 1572868
  17.9 4.6 %collective-permute-start.4 = (bf16[128,256]{1,0:T(8,128)(2,1)S(1)}, bf16[128,256]{1,0:T(8,128)(2,1)S(1)}, u32[]{:S(2)}, u32[]{:S(2)}) collective-permute-start(bf16[128,256]{1,0:T(8,128)(2,1)S(1)} %get-tuple-element.27), channel_id=1, source_target_pairs={{0,8},{8,0},{16,24},{24,16},{1,9},{9,1},{17,25},{25,17},{2,10},{10... | collective-permute-start | bytes 196616 | tf_op jit(solution)/shard_map/ppermute | solution.py:679
  19.5 6.6 %collective-permute-start.5 = (bf16[128,256]{1,0:T(8,128)(2,1)S(1)}, bf16[128,256]{1,0:T(8,128)(2,1)S(1)}, u32[]{:S(2)}, u32[]{:S(2)}) collective-permute-start(bf16[128,256]{1,0:T(8,128)(2,1)S(1)} %get-tuple-element.27), channel_id=1, source_target_pairs={{0,16},{8,24},{16,0},{24,8},{1,17},{9,25},{17,1},{25,9},{2,18},{10... | collective-permute-start | bytes 196616 | tf_op jit(solution)/shard_map/ppermute | solution.py:679
  22.1 6.1 %collective-permute-start.6 = (bf16[128,256]{1,0:T(8,128)(2,1)S(1)}, bf16[128,256]{1,0:T(8,128)(2,1)S(1)}, u32[]{:S(2)}, u32[]{:S(2)}) collective-permute-start(bf16[128,256]{1,0:T(8,128)(2,1)S(1)} %get-tuple-element.27), channel_id=1, source_target_pairs={{0,24},{8,16},{16,8},{24,0},{1,25},{9,17},{17,9},{25,1},{2,26},{10... | collective-permute-start | bytes 196616 | tf_op jit(solution)/shard_map/ppermute | solution.py:679
  22.4 11.0 %collective-permute-start.14 = (bf16[4,128,256]{2,1,0:T(8,128)(2,1)S(1)}, bf16[4,128,256]{2,1,0:T(8,128)(2,1)S(1)}, u32[]{:S(2)}, u32[]{:S(2)}) collective-permute-start(bf16[4,128,256]{2,1,0:T(8,128)(2,1)S(1)} %bundle.1.refs_3_.refs_12_), channel_id=1, source_target_pairs={{0,1},{1,0},{2,3},{3,2},{4,5},{5,4},{6,7},{7,6},{8,9},{9,8},{10,11... | collective-permute-start | bytes 786440 | tf_op jit(solution)/shard_map/ppermute | solution.py:675
  28.4 1.4 %collective-permute-start.7 = (bf16[4,64,256]{2,1,0:T(8,128)(2,1)S(1)}, bf16[4,64,256]{2,1,0:T(8,128)(2,1)S(1)}, u32[]{:S(2)}, u32[]{:S(2)}) collective-permute-start(bf16[4,64,256]{2,1,0:T(8,128)(2,1)S(1)} %get-tuple-element.30), channel_id=1, source_target_pairs={{0,1},{1,0},{2,3},{3,2},{4,5},{5,4},{6,7},{7,6},{8,9},{9,8},{10,11... | collective-permute-start | bytes 393224 | tf_op jit(solution)/shard_map/ppermute | solution.py:675
  29.8 3.7 %copy-start.3 = (bf16[2048,32]{0,1:T(8,128)(2,1)S(1)}, bf16[2048,32]{0,1:T(8,128)(2,1)}, u32[]{:S(2)}) copy-start(bf16[2048,32]{0,1:T(8,128)(2,1)} %param.15) | copy-start | bytes 393220
  29.8 5.3 %collective-permute-start.10 = (bf16[96,256]{1,0:T(8,128)(2,1)S(1)}, bf16[96,256]{1,0:T(8,128)(2,1)S(1)}, u32[]{:S(2)}, u32[]{:S(2)}) collective-permute-start(bf16[96,256]{1,0:T(8,128)(2,1)S(1)} %get-tuple-element.35), channel_id=1, source_target_pairs={{0,6},{1,7},{2,4},{3,5},{4,2},{5,3},{6,0},{7,1},{8,14},{9,15},{10,... | collective-permute-start | bytes 147464 | tf_op jit(solution)/shard_map/ppermute | solution.py:675
  31.2 4.1 %collective-permute-start.8 = (bf16[96,256]{1,0:T(8,128)(2,1)S(1)}, bf16[96,256]{1,0:T(8,128)(2,1)S(1)}, u32[]{:S(2)}, u32[]{:S(2)}) collective-permute-start(bf16[96,256]{1,0:T(8,128)(2,1)S(1)} %get-tuple-element.33), channel_id=1, source_target_pairs={{0,2},{1,3},{2,0},{3,1},{4,6},{5,7},{6,4},{7,5},{8,10},{9,11},{10,... | collective-permute-start | bytes 147464 | tf_op jit(solution)/shard_map/ppermute | solution.py:675
  31.9 4.1 %collective-permute-start.9 = (bf16[96,256]{1,0:T(8,128)(2,1)S(1)}, bf16[96,256]{1,0:T(8,128)(2,1)S(1)}, u32[]{:S(2)}, u32[]{:S(2)}) collective-permute-start(bf16[96,256]{1,0:T(8,128)(2,1)S(1)} %get-tuple-element.34), channel_id=1, source_target_pairs={{0,4},{1,5},{2,6},{3,7},{4,0},{5,1},{6,2},{7,3},{8,12},{9,13},{10,... | collective-permute-start | bytes 147464 | tf_op jit(solution)/shard_map/ppermute | solution.py:675

commit v3 on v2

--- a/solution.py
+++ b/solution.py
@@ -18,6 +18,8 @@
 F32 = jnp.float32
 BF16 = jnp.bfloat16
 VMEM = pltpu.VMEM
+PAIR_TYPE = BF16
+CROSSED = 1
 
 
 def spread(block, axis, owner):
@@ -131,6 +133,10 @@
     )
 
 
+def partner(step):
+    return 2 * step + CROSSED * min(step, 1)
+
+
 def nt(first, second):
     return lax.dot_general(first, second, (((1,), (1,)), ((), ())), preferred_element_type=F32)
 
@@ -179,71 +185,111 @@
     return pl.CostEstimate(flops=flops, bytes_accessed=bytes_accessed, transcendentals=0)
 
 
-def solve_kernel(odd, right_hbm, inverse_hbm, out_ref, right_ref, inverse_ref, sems):
+def solve_step(block, my_col, right_ref, inverse, out_ref, step, copy=None):
+    @pl.when(block >= my_col)
+    def _():
+        if copy is not None:
+            copy.wait()
+        out_ref[step] = nt(right_ref[...], inverse[step]).astype(out_ref.dtype)
+
+    @pl.when(block < my_col)
+    def _():
+        out_ref[step] = jnp.zeros(out_ref.shape[1:], out_ref.dtype)
+
+
+def solve_odd_kernel(
+    right_hbm, inverse_hbm, out_ref, right_ref, even_ref, inverse_ref, odd_sems, even_sems
+):
     parts = out_ref.shape[0]
     piece = right_ref.shape[1]
     my_col = lax.axis_index("col")
-    first = pltpu.make_async_copy(right_hbm, right_ref, sems.at[parts])
-    first.start()
+    right_copy = pltpu.make_async_copy(right_hbm, right_ref, odd_sems.at[parts])
+    right_copy.start()
     copies = []
+    for odd, target, sems in ((1, inverse_ref, odd_sems), (0, even_ref, even_sems)):
+        for step in range(parts):
+            block = my_col ^ (partner(step) ^ odd)
+            rows = pl.ds(pl.multiple_of(block * piece, piece), piece)
+            copy = pltpu.make_async_copy(inverse_hbm.at[rows], target.at[step], sems.at[step])
+            pl.when(block >= my_col)(copy.start)
+            copies.append((block, copy))
+    right_copy.wait()
     for step in range(parts):
-        block = my_col ^ (2 * step + odd)
-        copy = pltpu.make_async_copy(
-            inverse_hbm.at[pl.ds(pl.multiple_of(block * piece, piece), piece)],
-            inverse_ref.at[step],
-            sems.at[step],
-        )
-        copy.start()
-        copies.append(copy)
-    first.wait()
-    right = right_ref[...]
-    for step, copy in enumerate(copies):
-        copy.wait()
-        out_ref[step] = nt(right, inverse_ref[step])
-
-
-def solve_part(right, inverse, odd, parts):
+        block, copy = copies[step]
+        solve_step(block, my_col, right_ref, inverse_ref, out_ref, step, copy)
+    for block, copy in copies[parts:]:
+        pl.when(block >= my_col)(copy.wait)
+
+
+def solve_odd(right, inverse, parts):
     lines, piece = right.shape
     return pl.pallas_call(
-        functools.partial(solve_kernel, odd),
+        solve_odd_kernel,
         in_specs=[pl.BlockSpec(memory_space=pltpu.HBM)] * 2,
+        out_specs=in_vmem(3),
+        out_shape=[
+            jax.ShapeDtypeStruct((parts, lines, piece), PAIR_TYPE),
+            jax.ShapeDtypeStruct((lines, piece), BF16),
+            jax.ShapeDtypeStruct((parts, piece, piece), BF16),
+        ],
+        scratch_shapes=[
+            VMEM((parts, piece, piece), BF16),
+            pltpu.SemaphoreType.DMA((parts + 1,)),
+            pltpu.SemaphoreType.DMA((parts,)),
+        ],
+        name="solve_odd",
+        compiler_params=grant(4),
+        cost_estimate=small_cost(
+            4 * parts * piece * piece + 4 * parts * lines * piece,
+            2 * parts * lines * piece * piece,
+        ),
+    )(right, inverse)
+
+
+def solve_even_kernel(right_ref, even_ref, out_ref):
+    my_col = lax.axis_index("col")
+    for step in range(out_ref.shape[0]):
+        solve_step(my_col ^ partner(step), my_col, right_ref, even_ref, out_ref, step)
+
+
+def solve_even(right, even):
+    lines, piece = right.shape
+    parts = even.shape[0]
+    return pl.pallas_call(
+        solve_even_kernel,
+        in_specs=in_vmem(2),
         out_specs=pl.BlockSpec(memory_space=VMEM),
         out_shape=jax.ShapeDtypeStruct((parts, lines, piece), F32),
-        scratch_shapes=[
-            VMEM((lines, piece), BF16),
-            VMEM((parts, piece, piece), BF16),
-            pltpu.SemaphoreType.DMA((parts + 1,)),
-        ],
-        name="solve_odd" if odd else "solve_even",
+        name="solve_even",
         compiler_params=grant(4),
         cost_estimate=small_cost(
             2 * parts * piece * piece + 4 * parts * lines * piece,
             2 * parts * lines * piece * piece,
         ),
-    )(right, inverse)
+    )(right, even)
 
 
 def pair_add_kernel(mine_ref, other_ref, keep_ref, *send_refs):
-    keep_ref[...] = mine_ref[0] + other_ref[0]
+    keep_ref[...] = mine_ref[0] + other_ref[0].astype(F32)
     for step, ref in enumerate(send_refs):
-        ref[...] = (mine_ref[step + 1] + other_ref[step + 1]).astype(BF16)
-
-
-def pair_add(mine, other):
+        ref[...] = (mine_ref[step + 1] + other_ref[step + 1].astype(F32)).astype(ref.dtype)
+
+
+def pair_add(mine, other, send_type):
     parts, lines, piece = mine.shape
     return pl.pallas_call(
         pair_add_kernel,
         in_specs=in_vmem(2),
         out_specs=in_vmem(parts),
         out_shape=[jax.ShapeDtypeStruct((lines, piece), F32)]
-        + [jax.ShapeDtypeStruct((lines, piece), BF16)] * (parts - 1),
+        + [jax.ShapeDtypeStruct((lines, piece), send_type)] * (parts - 1),
         name="pair_add",
         compiler_params=grant(4),
         cost_estimate=small_cost(3 * mine.size * 4),
     )(mine, other)
 
 
-def gather_add_kernel(head, first_ref, panel_ref, mask_ref, *refs):
+def gather_add_kernel(head, first_ref, mask_ref, *refs):
     *others, solved_ref, head_ref = refs
     total = first_ref[...]
     for ref in others:
@@ -251,135 +297,114 @@
     keep = jnp.concatenate([mask_ref[...]] * (total.shape[1] // LANES), axis=1)
     rounded = jnp.where(keep > 0.0, total, 0.0).astype(BF16)
     solved_ref[...] = rounded
-    head_ref[:head] = rounded[:head]
-    head_ref[head:] = panel_ref[:head]
-
-
-def gather_add(first, panel, mask, others, head):
+    head_ref[...] = rounded[:head]
+
+
+def gather_add(first, mask, others, head):
     return pl.pallas_call(
         functools.partial(gather_add_kernel, head),
-        in_specs=in_vmem(3 + len(others)),
+        in_specs=in_vmem(2 + len(others)),
         out_specs=in_vmem(2),
         out_shape=[
             jax.ShapeDtypeStruct(first.shape, BF16),
-            jax.ShapeDtypeStruct((2 * head, first.shape[1]), BF16),
+            jax.ShapeDtypeStruct((head, first.shape[1]), BF16),
         ],
         name="gather_add",
         compiler_params=grant(4),
         cost_estimate=small_cost(first.size * 10),
-    )(first, panel, mask, *others)
-
-
-def bundle_kernel(*refs):
-    *pieces, out_ref = refs
-    for step, ref in enumerate(pieces):
-        out_ref[step] = ref[...]
-
-
-def bundle(pieces):
-    count = len(pieces)
-    return pl.pallas_call(
-        bundle_kernel,
-        in_specs=in_vmem(count),
-        out_specs=pl.BlockSpec(memory_space=VMEM),
-        out_shape=jax.ShapeDtypeStruct((count,) + pieces[0].shape, BF16),
-        name="bundle",
-        compiler_params=grant(4),
-        cost_estimate=small_cost(count * pieces[0].size * 4),
-    )(*pieces)
-
-
-def both_halves(value):
-    return jnp.concatenate(split(value), axis=1)
-
-
-def from_halves(value):
-    half = value.shape[1] // 2
-    return value[:, :half].astype(F32) + value[:, half:].astype(F32)
-
-
-def core_kernel(rows_total, cols_total, width, own_ref, panel_ref, *refs):
+    )(first, mask, *others)
+
+
+def column_tiles(rows_total, cols_total, width, own_ref, others):
+    my_row = lax.axis_index("row")
+    for shift in range(rows_total):
+        source = own_ref if shift == 0 else others[shift - 1]
+        for index in range(cols_total // rows_total):
+            lines = source[index * width : (index + 1) * width, :]
+            yield index * rows_total + (my_row ^ shift), lines
+
+
+def message_kernel(rows_total, cols_total, width, own_ref, *refs):
     others = refs[: rows_total - 1]
-    even_ref, even_panel_ref, odd_ref, solved_stage, panel_stage = refs[rows_total - 1 :]
-    my_row, my_col = lax.axis_index("row"), lax.axis_index("col")
-    half = cols_total // 2
-    per_row = cols_total // rows_total
-    head = per_row * width
-    for shift in range(rows_total):
-        from_row = my_row ^ shift
-        for index in range(per_row):
-            relative = my_col ^ (index * rows_total + from_row)
-            place = (relative & 1) * half + lax.shift_right_logical(relative, 1)
-            lines = slice(index * width, (index + 1) * width)
-            if shift == 0:
-                solved_stage[place] = own_ref[lines, :]
-                panel_stage[place] = panel_ref[lines, :]
-            else:
-                source = others[shift - 1]
-                solved_stage[place] = source[lines, :]
-                panel_stage[place] = source[head + index * width : head + (index + 1) * width, :]
-    piece = own_ref.shape[1]
-    own = own_ref[...]
-    odd_core = nt(solved_stage[half:].reshape(half * width, piece), own)
-    for step in range(half):
-        odd_ref[step, :width] = both_halves(odd_core[step * width : (step + 1) * width])
-        odd_ref[step, width:] = panel_stage[half + step]
-    even_ref[...] = nt(solved_stage[:half].reshape(half * width, piece), own).reshape(
-        even_ref.shape
-    )
-    even_panel_ref[...] = panel_stage[:half]
-
-
-def core_parts(own, panel, others, rows_total, cols_total, width):
+    *message_refs, stage = refs[rows_total - 1 :]
+    my_col = lax.axis_index("col")
+    lines = own_ref.shape[0]
+    for tile, value in column_tiles(rows_total, cols_total, width, own_ref, others):
+        stage[tile] = value
+    for step, ref in enumerate(message_refs):
+        target = my_col ^ partner(step)
+        ref[:width] = stage[target]
+        ref[width : width + lines] = own_ref[...]
+        ref[width + lines :] = stage[target ^ 1]
+
+
+def messages(own, others, rows_total, cols_total, width):
     lines, piece = own.shape
     half = cols_total // 2
     return pl.pallas_call(
+        functools.partial(message_kernel, rows_total, cols_total, width),
+        in_specs=in_vmem(rows_total),
+        out_specs=in_vmem(half),
+        out_shape=[jax.ShapeDtypeStruct((lines + 2 * width, piece), BF16)] * half,
+        scratch_shapes=[VMEM((cols_total, width, piece), BF16)],
+        name="messages",
+        compiler_params=grant(4),
+        cost_estimate=small_cost(half * (lines + 2 * width) * piece * 4),
+    )(own, *others)
+
+
+def bundle_kernel(width, *refs):
+    *pieces, here_ref, there_ref = refs
+    for step, ref in enumerate(pieces):
+        here_ref[step] = ref[: here_ref.shape[1]]
+        there_ref[step] = ref[width:]
+
+
+def bundle(pieces, width):
+    count = len(pieces)
+    lines, piece = pieces[0].shape
+    shape = jax.ShapeDtypeStruct((count, lines - width, piece), BF16)
+    return pl.pallas_call(
+        functools.partial(bundle_kernel, width),
+        in_specs=in_vmem(count),
+        out_specs=in_vmem(2),
+        out_shape=[shape, shape],
+        name="bundle",
+        compiler_params=grant(4),
+        cost_estimate=small_cost(count * pieces[0].size * 6),
+    )(*pieces)
+
+
+def core_kernel(rows_total, cols_total, width, own_ref, *refs):
+    others = refs[: rows_total - 1]
+    even_ref, odd_ref, stage = refs[rows_total - 1 :]
+    my_col = lax.axis_index("col")
+    half = cols_total // 2
+    for tile, value in column_tiles(rows_total, cols_total, width, own_ref, others):
+        relative = my_col ^ tile
+        step = lax.shift_right_logical(relative, 1)
+        given = (relative & 1) ^ (jnp.minimum(step, 1) * CROSSED)
+        stage[given * half + step] = value
+    piece = own_ref.shape[1]
+    own = own_ref[...]
+    odd_ref[...] = nt(stage[half:].reshape(half * width, piece), own).reshape(odd_ref.shape)
+    even_ref[...] = nt(stage[:half].reshape(half * width, piece), own).reshape(even_ref.shape)
+
+
+def core_parts(own, others, rows_total, cols_total, width):
+    lines, piece = own.shape
+    half = cols_total // 2
+    shape = jax.ShapeDtypeStruct((half, width, lines), F32)
+    return pl.pallas_call(
         functools.partial(core_kernel, rows_total, cols_total, width),
-        in_specs=in_vmem(1 + rows_total),
-        out_specs=in_vmem(3),
-        out_shape=[
-            jax.ShapeDtypeStruct((half, width, lines), F32),
-            jax.ShapeDtypeStruct((half, width, piece), BF16),
-            jax.ShapeDtypeStruct((half, 2 * width, piece), BF16),
-        ],
-        scratch_shapes=[VMEM((cols_total, width, piece), BF16)] * 2,
+        in_specs=in_vmem(rows_total),
+        out_specs=in_vmem(2),
+        out_shape=[shape, shape],
+        scratch_shapes=[VMEM((cols_total, width, piece), BF16)],
         name="core_parts",
         compiler_params=grant(4),
         cost_estimate=small_cost(400000, 2 * lines * piece * cols_total * width),
-    )(own, panel, *others)
-
-
-def core_add_kernel(mine_ref, panel_ref, other_ref, keep_ref, keep_panel_ref, *send_refs):
-    width = mine_ref.shape[1]
-    for step in range(mine_ref.shape[0]):
-        total = mine_ref[step] + from_halves(other_ref[step, :width])
-        if step == 0:
-            keep_ref[...] = total
-            keep_panel_ref[:width] = panel_ref[0]
-            keep_panel_ref[width:] = other_ref[0, width:]
-        else:
-            ref = send_refs[step - 1]
-            ref[:width] = both_halves(total)
-            ref[width : 2 * width] = panel_ref[step]
-            ref[2 * width :] = other_ref[step, width:]
-
-
-def core_add(mine, panel, other):
-    half, width, lines = mine.shape
-    piece = panel.shape[2]
-    return pl.pallas_call(
-        core_add_kernel,
-        in_specs=in_vmem(3),
-        out_specs=in_vmem(1 + half),
-        out_shape=[
-            jax.ShapeDtypeStruct((width, lines), F32),
-            jax.ShapeDtypeStruct((2 * width, piece), BF16),
-        ]
-        + [jax.ShapeDtypeStruct((3 * width, piece), BF16)] * (half - 1),
-        name="core_add",
-        compiler_params=grant(4),
-        cost_estimate=small_cost(1000000),
-    )(mine, panel, other)
+    )(own, *others)
 
 
 def piece_spot(relative, piece):
@@ -397,40 +422,69 @@
     return (lane // width) == (line // width)
 
 
+def panel_piece(even_ref, odd_ref, relative, width):
+    step = relative // 2
+    if relative != partner(step):
+        lines = odd_ref.shape[1] - width
+        return odd_ref[step, :lines], odd_ref[step, lines:]
+    return even_ref[step, width:], even_ref[step, :width]
+
+
+def panel_wide(even_ref, odd_ref, width):
+    parts = [panel_piece(even_ref, odd_ref, k, width) for k in range(2 * even_ref.shape[0])]
+    return [jnp.concatenate(side, axis=1) for side in zip(*parts)]
+
+
 def gram_kernel(width, *refs):
     left_ref, right_ref, sketch_ref, even_ref, odd_ref, keep_line_ref, keep_lane_ref = refs[:7]
-    row_high_ref, row_low_ref, right_gram_ref, sketch_right_ref = refs[7:]
-    half, lines, piece = even_ref.shape
-    count = 2 * half
+    (
+        row_high_ref,
+        row_low_ref,
+        right_gram_ref,
+        sketch_right_ref,
+        column_right_ref,
+        column_column_ref,
+        sketch_column_ref,
+    ) = refs[7:]
+    lines = left_ref.shape[0]
+    piece = even_ref.shape[2]
+    count = 2 * even_ref.shape[0]
     same = same_tile(lines, width)
-    panel = jnp.concatenate(
-        [(odd_ref if k & 1 else even_ref)[k // 2] for k in range(count)], axis=1
-    )
+    panel, column = panel_wide(even_ref, odd_ref, width)
     left = pieces_wide(left_ref, count, piece)
     for i, one in enumerate((left, panel)):
         for j, two in enumerate((left, panel)):
             high, low = split(jnp.where(same, nt(one, two), 0.0))
             row_high_ref[i * lines : (i + 1) * lines, j * lines : (j + 1) * lines] = high
             row_low_ref[i * lines : (i + 1) * lines, j * lines : (j + 1) * lines] = low
-    right = right_ref[...]
+    right = pieces_wide(right_ref, count, piece)
+    sketch = pieces_wide(sketch_ref, count, piece)
     keep_line = keep_line_ref[...] > 0.0
     keep_lane = keep_lane_ref[:1] > 0.0
     right_gram_ref[...] = jnp.where(same & keep_line & keep_lane, nt(right, right), 0.0)
-    sketch_right_ref[...] = jnp.where(keep_lane, nt(sketch_ref[...], right), 0.0)
+    sketch_right_ref[...] = jnp.where(keep_lane, nt(sketch, right), 0.0)
+    column_right_ref[...] = jnp.where(keep_lane, nt(column, right), 0.0)
+    column_column_ref[...] = nt(column, column)
+    sketch_column_ref[...] = nt(sketch, column)
 
 
 def grams(left, right, sketch, even, odd, keep_line, keep_lane, width):
     lines, order = left.shape
     square = jax.ShapeDtypeStruct((2 * lines, 2 * lines), BF16)
+    flat = jax.ShapeDtypeStruct((width, lines), F32)
+    small = jax.ShapeDtypeStruct((width, width), F32)
     return pl.pallas_call(
         functools.partial(gram_kernel, width),
         in_specs=in_vmem(7),
-        out_specs=in_vmem(4),
+        out_specs=in_vmem(7),
         out_shape=[
             square,
             square,
             jax.ShapeDtypeStruct((lines, lines), F32),
-            jax.ShapeDtypeStruct((sketch.shape[0], lines), F32),
+            flat,
+            flat,
+            small,
+            small,
         ],
         name="grams",
         compiler_params=grant(16),
@@ -502,16 +556,17 @@
 
 
 def finish_kernel(half, width, rows_total, *refs):
-    core_ref, column_ref = refs[:2]
-    core_refs = refs[2 : half + 1]
+    core_refs = refs[:half]
     (
         row_high_ref,
         row_low_ref,
         right_gram_ref,
         sketch_right_ref,
+        column_right_ref,
+        column_column_ref,
+        sketch_column_ref,
         left_ref,
         right_ref,
-        sketch_ref,
         even_ref,
         odd_ref,
         keep_lane_ref,
@@ -520,7 +575,7 @@
         out_left_ref,
         out_right_ref,
         sems,
-    ) = refs[half + 1 :]
+    ) = refs[half:]
     my_row, my_col = lax.axis_index("row"), lax.axis_index("col")
     lines, order = left_ref.shape
     tiles = lines // width
@@ -536,12 +591,6 @@
 
     def blocks(value):
         return jnp.concatenate([stacked(value[:, :lines]), stacked(value[:, lines:])], axis=1)
-
-    def column_piece(relative):
-        step, side = divmod(relative, 2)
-        if step == 0:
-            return column_ref[side * width : (side + 1) * width]
-        return core_refs[step - 1][(1 + side) * width : (2 + side) * width]
 
     keep_lane = keep_lane_ref[:1] > 0.0
     lane_row = lax.broadcasted_iota(jnp.int32, (1, lines), 1)
@@ -551,18 +600,15 @@
         live = (tile * rows_total + my_row) > my_col
         live_line |= (lane_row >= low) & (lane_row < low + jnp.where(live, width, 0))
 
-    columns = jnp.concatenate([column_piece(k) for k in range(count)], axis=1)
-    sketch_column = nt(pieces_wide(sketch_ref, count, piece), columns)
     row_parts = (row_high_ref[...], row_low_ref[...])
-
-    core = core_ref[...]
-    for ref in core_refs:
-        core = core + from_halves(ref[:width])
+    core = core_refs[0][...]
+    for ref in core_refs[1:]:
+        core = core + ref[...]
     core_split = split(core)
     core_blocks = stacked(core)
     core_block_split = split(core_blocks)
 
-    first = jnp.concatenate([sketch_right_ref[...], -dot_split(nn, sketch_column, core_split)], axis=1)
+    first = jnp.concatenate([sketch_right_ref[...], -dot_split(nn, sketch_column_ref[...], core_split)], axis=1)
     ones = jnp.where(same, 1.0, 0.0).astype(BF16)
 
     def traced(one, two):
@@ -574,12 +620,9 @@
     image = dot_split(nn, first, row_parts)
     shift = traced(first, image)
     gram = dot_split(nt, first, split(blocks(image)))
-    tall = jnp.concatenate([pieces_wide(right_ref, count, piece), columns], axis=0)
-    column_wide = nt(columns, tall)
-    column_right = jnp.where(keep_lane, column_wide[:, :lines], 0.0)
     core_lines = core.T
-    cross = -diagonal(dot_split(nn, core_lines, split(column_right)))
-    inner = dot_split(nn, column_wide[:, lines:], core_split)
+    cross = -diagonal(dot_split(nn, core_lines, split(column_right_ref[...])))
+    inner = dot_split(nn, column_column_ref[...], core_split)
     corner = diagonal(dot_split(nn, core_lines, split(inner)))
     middle = jnp.concatenate(
         [
@@ -617,11 +660,10 @@
     copies = []
     for relative in range(count):
         spot = piece_spot(relative, piece)
-        rows = jnp.concatenate(
-            [left_ref[:, spot], (odd_ref if relative & 1 else even_ref)[relative // 2]], axis=0
-        )
+        panel, column = panel_piece(even_ref, odd_ref, relative, width)
+        rows = jnp.concatenate([left_ref[:, spot], panel], axis=0)
         out_left_ref[relative] = nn(left_small, rows).astype(BF16)
-        tall = jnp.concatenate([right_ref[:, spot]] + [column_piece(relative)] * tiles, axis=0)
+        tall = jnp.concatenate([right_ref[:, spot]] + [column] * tiles, axis=0)
         out_right_ref[relative] = nn(right_small, tall).astype(BF16)
         for side, (ref, hbm) in enumerate(
             ((out_left_ref, out_left_hbm), (out_right_ref, out_right_hbm))
@@ -633,12 +675,12 @@
         copy.wait()
 
 
-def finish(core, column, cores, others, rows_total, width):
-    half = len(cores) + 1
-    left, panel = others[4], others[7]
-    lines, piece = panel.shape[1:]
+def finish(cores, others, rows_total, width):
+    half = len(cores)
+    left = others[7]
+    lines, piece = left.shape[0], left.shape[1] // (2 * half)
     shape = jax.ShapeDtypeStruct(left.shape, BF16)
-    operands = (core, column, *cores, *others)
+    operands = (*cores, *others)
     return pl.pallas_call(
         functools.partial(finish_kernel, half, width, rows_total),
         in_specs=in_vmem(len(operands)),
@@ -679,7 +721,7 @@
         return lax.ppermute(block, "row", pairs)
 
     def across(blocks):
-        return [swap(block, 2 * (step + 1)) for step, block in enumerate(blocks)]
+        return [swap(block, partner(step + 1)) for step, block in enumerate(blocks)]
 
     def along(block):
         return [turn(block, shift) for shift in range(1, rows_total)]
@@ -688,29 +730,25 @@
     slab_line, slab_lane = line_mask(panel.shape[0], slab_ranks.reshape(-1))
     solve_right = pltpu.with_memory_space_constraint(solve_right, pltpu.HBM)
     inverse_factor = pltpu.with_memory_space_constraint(inverse_factor, pltpu.HBM)
-    odd = solve_part(solve_right, inverse_factor, 1, half)
+    odd, right_panel, even_blocks = solve_odd(solve_right, inverse_factor, half)
     other = swap(odd, 1)
-    even = solve_part(solve_right, inverse_factor, 0, half)
-    kept, *sends = pair_add(even, other)
+    even = solve_even(right_panel, even_blocks)
+    kept, *sends = pair_add(even, other, BF16)
     received = across(sends)
-    solved, solved_head = gather_add(kept, panel, panel_keep, received, head)
+    panel_others = along(panel[:head])
+    solved, solved_head = gather_add(kept, panel_keep, received, head)
     solved_others = along(solved_head)
-    even_panel = bundle([panel] + across([panel] * (half - 1)))
-    odd_panel = swap(even_panel, 1)
+    own_message, *sends = messages(panel, panel_others, rows_total, cols_total, width)
+    even_panel, odd_panel = bundle([own_message] + across(sends), width)
+    odd_panel = swap(odd_panel, 1)
     gram_parts = grams(
         left, right, sketch_lines, even_panel, odd_panel, slab_line, slab_lane, width
     )
-    core_even, even_column, odd_message = core_parts(
-        solved, panel, solved_others, rows_total, cols_total, width
-    )
-    other = swap(odd_message, 1)
-    core, column, *sends = core_add(core_even, even_column, other)
-    cores = across(sends)
+    core_even, core_odd = core_parts(solved, solved_others, rows_total, cols_total, width)
+    kept, *sends = pair_add(core_even, swap(core_odd, 1), F32)
     fresh_left, fresh_right = finish(
-        core,
-        column,
-        cores,
-        (*gram_parts, left, right, sketch_lines, even_panel, odd_panel, slab_lane),
+        [kept] + across(sends),
+        (*gram_parts, left, right, even_panel, odd_panel, slab_lane),
         rows_total,
         width,
     )

time: 40 us -> 45.9 us (1.15)
  waiting for transfers between devices: 12.5 us -> 17.2 us
  starting transfers between devices: 17.2 us -> 19.4 us
  Pallas kernels: 8.93 us -> 7.47 us
    ppermute x3 -> x6, starting transfers between devices: 4.45 us -> 9.83 us  [turn(): return lax.ppermute(block, 'row', pairs)]
    ppermute x12, starting transfers between devices: 12.7 us -> 9.6 us  [swap(): lax.ppermute(block, 'col', [(i, i ^ step) for i in range(cols_total)])]
    ppermute x12, waiting for transfers between devices: 6.75 us -> 9.22 us  [swap(): lax.ppermute(block, 'col', [(i, i ^ step) for i in range(cols_total)])]
    ppermute x3 -> x6, waiting for transfers between devices: 5.73 us -> 7.99 us  [turn(): return lax.ppermute(block, 'row', pairs)]
    pallas_call x4, Pallas kernels: 3.74 us -> 2.65 us  [the longest x1 1.86 us: solve_odd(): pl.pallas_call(solve_odd_kernel, in_specs=[pl.BlockSpec(memory_space=pltp...]
    pallas_call x1, Pallas kernels: 3.92 us -> 3.31 us  [finish(): pl.pallas_call(functools.partial(finish_kernel, half, width, rows_total),...]
  transfers between devices with their start and end apart: 15 -> 18, of which waited for: 8 -> 12; matrix products, arithmetic and copies ran while one was open for 1% -> 1% of each run, Pallas kernels for 8% -> 5%
where the time goes in v3:
time: 45.9 us; the launch traced here: 45.8 us
  starting transfers between devices  19.4 us (42%)
  waiting for transfers between devices  17.2 us (37%)
  Pallas kernels  7.47 us (16%)
  between operations  0.79 us (2%)
  local copies, waits for them, and re-layouts  0.72 us (2%)
    ppermute x6, starting transfers between devices, turn(): return lax.ppermute(block, 'row', pairs)  9.83 us
    ppermute x12, starting transfers between devices, swap(): lax.ppermute(block, 'col', [(i, i ^ step) for i in range(cols_total)])  9.6 us
    ppermute x12, waiting for transfers between devices, swap(): lax.ppermute(block, 'col', [(i, i ^ step) for i in range(cols_total)])  9.22 us
    ppermute x6, waiting for transfers between devices, turn(): return lax.ppermute(block, 'row', pairs)  7.99 us
    pallas_call x1, Pallas kernels, finish(): pl.pallas_call(functools.partial(finish_kernel, half, width, rows_total),...  3.31 us
    pallas_call x1, Pallas kernels, solve_odd(): pl.pallas_call(solve_odd_kernel, in_specs=[pl.BlockSpec(memory_space=pltp...  1.86 us
    pallas_call x1, Pallas kernels, grams(): pl.pallas_call(functools.partial(gram_kernel, width), in_specs=in_vmem(7)...  1.21 us
  transfers between devices with their start and end apart: 18, of which 12 were waited for; matrix products, arithmetic and copies ran while one was open for 1% of the time, Pallas kernels for 5%

profile of v3, /device:TPU:0, one launch (start us, length us, event | category | flops | bytes accessed | tf_op | source)
XLA Modules:
  0.0 45.8 jit_solution(11523062503916566237)
XLA Ops:
  0.6 0.0 copy-start
  0.6 1.9 %solve_odd.1 = (bf16[4,128,256]{2,1,0:T(8,128)(2,1)S(1)}, bf16[128,256]{1,0:T(8,128)(2,1)S(1)}, bf16[4,256,256]{2,1,0:T(8,128)(2,1)S(1)}) custom-call(bf16[128,256]{1,0:T(8,128)(2,1)} %bitcast.32, bf16[2048,256]{1,0:T(8,128)(2,1)} %inverse_hbm.1), custom_call_target="tpu_custom_call" | custom-call | flops 67108864 | bytes 1572864 | tf_op jit(solution)/shard_map/solve_odd/pallas_call | solution.py:226
  2.5 0.4 collective-permute-start
  2.9 0.0 copy-done
  2.9 2.8 %collective-permute-start.11 = (bf16[64,256]{1,0:T(8,128)(2,1)S(1)}, bf16[64,256]{1,0:T(8,128)(2,1)S(1)}, u32[]{:S(2)}, u32[]{:S(2)}) collective-permute-start(bf16[64,256]{1,0:T(8,128)(2,1)S(1)} %bitcast.33), channel_id=1, source_target_pairs={{0,8},{8,0},{16,24},{24,16},{1,9},{9,1},{17,25},{25,17},{2,10},{10... | collective-permute-start | bytes 98312 | tf_op jit(solution)/shard_map/ppermute | solution.py:721
  5.7 2.6 %collective-permute-start.12 = (bf16[64,256]{1,0:T(8,128)(2,1)S(1)}, bf16[64,256]{1,0:T(8,128)(2,1)S(1)}, u32[]{:S(2)}, u32[]{:S(2)}) collective-permute-start(bf16[64,256]{1,0:T(8,128)(2,1)S(1)} %bitcast.34), channel_id=1, source_target_pairs={{0,16},{8,24},{16,0},{24,8},{1,17},{9,25},{17,1},{25,9},{2,18},{10... | collective-permute-start | bytes 98312 | tf_op jit(solution)/shard_map/ppermute | solution.py:721
  8.3 0.0 collective-permute-start.13
  8.3 0.0 collective-permute-done.11.refs_0_
  8.3 2.8 %collective-permute-done.12.refs_1_ = bf16[64,256]{1,0:T(8,128)(2,1)S(1)} collective-permute-done((bf16[64,256]{1,0:T(8,128)(2,1)S(1)}, bf16[64,256]{1,0:T(8,128)(2,1)S(1)}, u32[]{:S(2)}, u32[]{:S(2)}) %collective-permute-start.12) | collective-permute-done | bytes 32800 | tf_op jit(solution)/shard_map/ppermute | solution.py:721
  11.1 2.9 %collective-permute-done.13.refs_2_ = bf16[64,256]{1,0:T(8,128)(2,1)S(1)} collective-permute-done((bf16[64,256]{1,0:T(8,128)(2,1)S(1)}, bf16[64,256]{1,0:T(8,128)(2,1)S(1)}, u32[]{:S(2)}, u32[]{:S(2)}) %collective-permute-start.13) | collective-permute-done | bytes 32800 | tf_op jit(solution)/shard_map/ppermute | solution.py:721
  14.1 0.1 collective-permute-start.14
  14.2 2.1 %collective-permute-start.15 = (bf16[192,256]{1,0:T(8,128)(2,1)S(1)}, bf16[192,256]{1,0:T(8,128)(2,1)S(1)}, u32[]{:S(2)}, u32[]{:S(2)}) collective-permute-start(bf16[192,256]{1,0:T(8,128)(2,1)S(1)} %get-tuple-element.49), channel_id=1, source_target_pairs={{0,5},{1,4},{2,7},{3,6},{4,1},{5,0},{6,3},{7,2},{8,13},{9,12},{10,... | collective-permute-start | bytes 294920 | tf_op jit(solution)/shard_map/ppermute | solution.py:717
  16.3 0.4 collective-permute-start.16
  16.7 0.7 %solve_even.1.mine_ref = f32[4,128,256]{2,1,0:T(8,128)S(1)} custom-call(bf16[128,256]{1,0:T(8,128)(2,1)S(1)} %get-tuple-element.32.right_ref, bf16[4,256,256]{2,1,0:T(8,128)(2,1)S(1)} %get-tuple-element.33.even_ref), custom_call_target="tpu_custom_call" | custom-call | flops 67108864 | bytes 1048576 | tf_op jit(solution)/shard_map/solve_even/pallas_call | solution.py:258
  17.4 1.7 %collective-permute-done.14.refs_1_ = bf16[192,256]{1,0:T(8,128)(2,1)S(1)} collective-permute-done((bf16[192,256]{1,0:T(8,128)(2,1)S(1)}, bf16[192,256]{1,0:T(8,128)(2,1)S(1)}, u32[]{:S(2)}, u32[]{:S(2)}) %collective-permute-start.14) | collective-permute-done | bytes 98336 | tf_op jit(solution)/shard_map/ppermute | solution.py:717
  19.1 0.0 collective-permute-done.15.refs_2_
  19.1 2.8 %collective-permute-done.16.refs_3_ = bf16[192,256]{1,0:T(8,128)(2,1)S(1)} collective-permute-done((bf16[192,256]{1,0:T(8,128)(2,1)S(1)}, bf16[192,256]{1,0:T(8,128)(2,1)S(1)}, u32[]{:S(2)}, u32[]{:S(2)}) %collective-permute-start.16) | collective-permute-done | bytes 98336 | tf_op jit(solution)/shard_map/ppermute | solution.py:717
  21.9 0.1 collective-permute-start.17
  22.0 0.0 collective-permute-done.other_ref
  22.0 0.0 copy-start.4
  22.0 0.0 copy-start.2
  22.0 0.1 pair_add.2
  22.1 0.0 copy-start.1
  22.1 1.2 %collective-permute-start.1 = (bf16[128,256]{1,0:T(8,128)(2,1)S(1)}, bf16[128,256]{1,0:T(8,128)(2,1)S(1)}, u32[]{:S(2)}, u32[]{:S(2)}) collective-permute-start(bf16[128,256]{1,0:T(8,128)(2,1)S(1)} %get-tuple-element.36), channel_id=1, source_target_pairs={{0,3},{1,2},{2,1},{3,0},{4,7},{5,6},{6,5},{7,4},{8,11},{9,10},{10,... | collective-permute-start | bytes 196616 | tf_op jit(solution)/shard_map/ppermute | solution.py:717
  23.3 0.6 %collective-permute-start.2 = (bf16[128,256]{1,0:T(8,128)(2,1)S(1)}, bf16[128,256]{1,0:T(8,128)(2,1)S(1)}, u32[]{:S(2)}, u32[]{:S(2)}) collective-permute-start(bf16[128,256]{1,0:T(8,128)(2,1)S(1)} %get-tuple-element.37), channel_id=1, source_target_pairs={{0,5},{1,4},{2,7},{3,6},{4,1},{5,0},{6,3},{7,2},{8,13},{9,12},{10,... | collective-permute-start | bytes 196616 | tf_op jit(solution)/shard_map/ppermute | solution.py:717
  23.9 1.6 %collective-permute-start.3 = (bf16[128,256]{1,0:T(8,128)(2,1)S(1)}, bf16[128,256]{1,0:T(8,128)(2,1)S(1)}, u32[]{:S(2)}, u32[]{:S(2)}) collective-permute-start(bf16[128,256]{1,0:T(8,128)(2,1)S(1)} %get-tuple-element.38), channel_id=1, source_target_pairs={{0,7},{1,6},{2,5},{3,4},{4,3},{5,2},{6,1},{7,0},{8,15},{9,14},{10,... | collective-permute-start | bytes 196616 | tf_op jit(solution)/shard_map/ppermute | solution.py:717
  25.4 0.0 copy-done.4
  25.4 0.1 fusion
  25.5 0.1 reshape.78
  25.6 0.3 collective-permute-done.1.refs_0_
  25.9 1.5 %collective-permute-done.2.refs_1_ = bf16[128,256]{1,0:T(8,128)(2,1)S(1)} collective-permute-done((bf16[128,256]{1,0:T(8,128)(2,1)S(1)}, bf16[128,256]{1,0:T(8,128)(2,1)S(1)}, u32[]{:S(2)}, u32[]{:S(2)}) %collective-permute-start.2) | collective-permute-done | bytes 65568 | tf_op jit(solution)/shard_map/ppermute | solution.py:717
  27.5 1.0 %collective-permute-done.3.refs_2_ = bf16[128,256]{1,0:T(8,128)(2,1)S(1)} collective-permute-done((bf16[128,256]{1,0:T(8,128)(2,1)S(1)}, bf16[128,256]{1,0:T(8,128)(2,1)S(1)}, u32[]{:S(2)}, u32[]{:S(2)}) %collective-permute-start.3) | collective-permute-done | bytes 65568 | tf_op jit(solution)/shard_map/ppermute | solution.py:717
  28.5 0.1 broadcast_in_dim.6.mask_ref
  28.6 0.1 gather_add.1
  28.6 0.1 collective-permute-start.4
  28.7 0.9 %collective-permute-start.5 = (bf16[64,256]{1,0:T(8,128)(2,1)S(1)}, bf16[64,256]{1,0:T(8,128)(2,1)S(1)}, u32[]{:S(2)}, u32[]{:S(2)}) collective-permute-start(bf16[64,256]{1,0:T(8,128)(2,1)S(1)} %get-tuple-element.40), channel_id=1, source_target_pairs={{0,16},{8,24},{16,0},{24,8},{1,17},{9,25},{17,1},{25,9},{2,18},{10... | collective-permute-start | bytes 98312 | tf_op jit(solution)/shard_map/ppermute | solution.py:721
  29.7 3.4 %collective-permute-start.6 = (bf16[64,256]{1,0:T(8,128)(2,1)S(1)}, bf16[64,256]{1,0:T(8,128)(2,1)S(1)}, u32[]{:S(2)}, u32[]{:S(2)}) collective-permute-start(bf16[64,256]{1,0:T(8,128)(2,1)S(1)} %get-tuple-element.40), channel_id=1, source_target_pairs={{0,24},{8,16},{16,8},{24,0},{1,25},{9,17},{17,9},{25,1},{2,26},{10... | collective-permute-start | bytes 98312 | tf_op jit(solution)/shard_map/ppermute | solution.py:721
  33.1 0.0 collective-permute-done.4.refs_0_
  33.1 0.7 %collective-permute-done.5.refs_1_ = bf16[64,256]{1,0:T(8,128)(2,1)S(1)} collective-permute-done((bf16[64,256]{1,0:T(8,128)(2,1)S(1)}, bf16[64,256]{1,0:T(8,128)(2,1)S(1)}, u32[]{:S(2)}, u32[]{:S(2)}) %collective-permute-start.5) | collective-permute-done | bytes 32800 | tf_op jit(solution)/shard_map/ppermute | solution.py:721
  33.8 1.6 %collective-permute-done.6.refs_2_ = bf16[64,256]{1,0:T(8,128)(2,1)S(1)} collective-permute-done((bf16[64,256]{1,0:T(8,128)(2,1)S(1)}, bf16[64,256]{1,0:T(8,128)(2,1)S(1)}, u32[]{:S(2)}, u32[]{:S(2)}) %collective-permute-start.6) | collective-permute-done | bytes 32800 | tf_op jit(solution)/shard_map/ppermute | solution.py:721
  35.4 0.0 copy-start.5
  35.4 0.2 core_parts.1
  35.6 0.0 copy-start.3
  35.6 0.1 collective-permute-start.7
  35.7 0.4 copy-done.5
  36.0 0.1 fusion.1
  36.1 0.1 reshape.79
  36.2 0.7 %collective-permute-done.7.other_ref = f32[4,32,128]{2,1,0:T(8,128)S(1)} collective-permute-done((f32[4,32,128]{2,1,0:T(8,128)S(1)}, f32[4,32,128]{2,1,0:T(8,128)S(1)}, u32[]{:S(2)}, u32[]{:S(2)}) %collective-permute-start.7) | collective-permute-done | bytes 65568 | tf_op jit(solution)/shard_map/ppermute | solution.py:717
  36.9 1.4 %collective-permute-start.10 = (f32[32,128]{1,0:T(8,128)S(1)}, f32[32,128]{1,0:T(8,128)S(1)}, u32[]{:S(2)}, u32[]{:S(2)}) collective-permute-start(f32[32,128]{1,0:T(8,128)S(1)} %get-tuple-element.46), channel_id=1, source_target_pairs={{0,7},{1,6},{2,5},{3,4},{4,3},{5,2},{6,1},{7,0},{8,15},{9,14},{10,... | collective-permute-start | bytes 49160 | tf_op jit(solution)/shard_map/ppermute | solution.py:717
  38.3 1.0 %collective-permute-start.8 = (f32[32,128]{1,0:T(8,128)S(1)}, f32[32,128]{1,0:T(8,128)S(1)}, u32[]{:S(2)}, u32[]{:S(2)}) collective-permute-start(f32[32,128]{1,0:T(8,128)S(1)} %get-tuple-element.44), channel_id=1, source_target_pairs={{0,3},{1,2},{2,1},{3,0},{4,7},{5,6},{6,5},{7,4},{8,11},{9,10},{10,... | collective-permute-start | bytes 49160 | tf_op jit(solution)/shard_map/ppermute | solution.py:717
  39.3 0.7 %collective-permute-start.9 = (f32[32,128]{1,0:T(8,128)S(1)}, f32[32,128]{1,0:T(8,128)S(1)}, u32[]{:S(2)}, u32[]{:S(2)}) collective-permute-start(f32[32,128]{1,0:T(8,128)S(1)} %get-tuple-element.45), channel_id=1, source_target_pairs={{0,5},{1,4},{2,7},{3,6},{4,1},{5,0},{6,3},{7,2},{8,13},{9,12},{10,... | collective-permute-start | bytes 49160 | tf_op jit(solution)/shard_map/ppermute | solution.py:717
  39.9 0.0 collective-permute-done.17.refs_4_.refs_14_
  40.0 0.1 broadcast_in_dim.7.refs_5_
  40.0 0.0 copy-done.2
  40.0 0.0 copy-done.1
  40.0 0.0 copy-done.3
  40.1 1.2 %grams.1 = (bf16[256,256]{1,0:T(8,128)(2,1)S(1)}, bf16[256,256]{1,0:T(8,128)(2,1)S(1)}, f32[128,128]{1,0:T(8,128)S(1)}, f32[32,128]{1,0:T(8,128)S(1)}, f32[32,12...) custom-call(bf16[128,2048]{1,0:T(8,128)(2,1)S(1)} %bitcast.27, bf16[128,2048]{1,0:T(8,128)(2,1)S(1)} %bitcast.29, ...), custom_call_target="tpu_custom_call" | custom-call | flops 536870912 | bytes 2000000 | tf_op jit(solution)/shard_map/grams/pallas_call | solution.py:476
  41.3 0.0 collective-permute-done.10.refs_3_
  41.3 0.2 collective-permute-done.8.refs_1_
  41.5 1.0 %collective-permute-done.9.refs_2_ = f32[32,128]{1,0:T(8,128)S(1)} collective-permute-done((f32[32,128]{1,0:T(8,128)S(1)}, f32[32,128]{1,0:T(8,128)S(1)}, u32[]{:S(2)}, u32[]{:S(2)}) %collective-permute-start.9) | collective-permute-done | bytes 16416 | tf_op jit(solution)/shard_map/ppermute | solution.py:717
  42.4 3.3 %finish.1 = (bf16[128,2048]{1,0:T(8,128)(2,1)}, bf16[128,2048]{1,0:T(8,128)(2,1)}) custom-call(f32[32,128]{1,0:T(8,128)S(1)} %get-tuple-element.43.refs_0_, f32[32,128]{1,0:T(8,128)S(1)} %collective-permute-done.8.refs_1_, f32[32,128]{1,0:T(8,128)S(1)} %collective-permute-done.9.refs_2_, f32[32,128]{1,0:T(8,128)S(1)} %collective-permute-done.10.refs_3_, ...), custom_call_target="tpu_custom_call" | custom-call | flops 1000000000 | bytes 5000000 | tf_op jit(solution)/shard_map/finish/pallas_call | solution.py:684
  (5 shorter events, 0.1 us)
Async XLA Ops:
  0.6 2.3 %copy-start = (bf16[4,256,32]{1,2,0:T(8,128)(2,1)S(1)}, bf16[4,256,32]{1,2,0:T(8,128)(2,1)}, u32[]{:S(2)}) copy-start(bf16[4,256,32]{1,2,0:T(8,128)(2,1)} %param.11) | copy-start | bytes 196612
  2.5 19.5 %collective-permute-start = (bf16[4,128,256]{2,1,0:T(8,128)(2,1)S(1)}, bf16[4,128,256]{2,1,0:T(8,128)(2,1)S(1)}, u32[]{:S(2)}, u32[]{:S(2)}) collective-permute-start(bf16[4,128,256]{2,1,0:T(8,128)(2,1)S(1)} %get-tuple-element.34), channel_id=1, source_target_pairs={{0,1},{1,0},{2,3},{3,2},{4,5},{5,4},{6,7},{7,6},{8,9},{9,8},{10,11... | collective-permute-start | bytes 786440 | tf_op jit(solution)/shard_map/ppermute | solution.py:717
  2.9 5.4 %collective-permute-start.11 = (bf16[64,256]{1,0:T(8,128)(2,1)S(1)}, bf16[64,256]{1,0:T(8,128)(2,1)S(1)}, u32[]{:S(2)}, u32[]{:S(2)}) collective-permute-start(bf16[64,256]{1,0:T(8,128)(2,1)S(1)} %bitcast.33), channel_id=1, source_target_pairs={{0,8},{8,0},{16,24},{24,16},{1,9},{9,1},{17,25},{25,17},{2,10},{10... | collective-permute-start | bytes 98312 | tf_op jit(solution)/shard_map/ppermute | solution.py:721
  5.7 5.4 %collective-permute-start.12 = (bf16[64,256]{1,0:T(8,128)(2,1)S(1)}, bf16[64,256]{1,0:T(8,128)(2,1)S(1)}, u32[]{:S(2)}, u32[]{:S(2)}) collective-permute-start(bf16[64,256]{1,0:T(8,128)(2,1)S(1)} %bitcast.34), channel_id=1, source_target_pairs={{0,16},{8,24},{16,0},{24,8},{1,17},{9,25},{17,1},{25,9},{2,18},{10... | collective-permute-start | bytes 98312 | tf_op jit(solution)/shard_map/ppermute | solution.py:721
  8.3 5.7 %collective-permute-start.13 = (bf16[64,256]{1,0:T(8,128)(2,1)S(1)}, bf16[64,256]{1,0:T(8,128)(2,1)S(1)}, u32[]{:S(2)}, u32[]{:S(2)}) collective-permute-start(bf16[64,256]{1,0:T(8,128)(2,1)S(1)} %bitcast.35), channel_id=1, source_target_pairs={{0,24},{8,16},{16,8},{24,0},{1,25},{9,17},{17,9},{25,1},{2,26},{10... | collective-permute-start | bytes 98312 | tf_op jit(solution)/shard_map/ppermute | solution.py:721
  14.1 5.0 %collective-permute-start.14 = (bf16[192,256]{1,0:T(8,128)(2,1)S(1)}, bf16[192,256]{1,0:T(8,128)(2,1)S(1)}, u32[]{:S(2)}, u32[]{:S(2)}) collective-permute-start(bf16[192,256]{1,0:T(8,128)(2,1)S(1)} %get-tuple-element.48), channel_id=1, source_target_pairs={{0,3},{1,2},{2,1},{3,0},{4,7},{5,6},{6,5},{7,4},{8,11},{9,10},{10,... | collective-permute-start | bytes 294920 | tf_op jit(solution)/shard_map/ppermute | solution.py:717
  14.2 4.9 %collective-permute-start.15 = (bf16[192,256]{1,0:T(8,128)(2,1)S(1)}, bf16[192,256]{1,0:T(8,128)(2,1)S(1)}, u32[]{:S(2)}, u32[]{:S(2)}) collective-permute-start(bf16[192,256]{1,0:T(8,128)(2,1)S(1)} %get-tuple-element.49), channel_id=1, source_target_pairs={{0,5},{1,4},{2,7},{3,6},{4,1},{5,0},{6,3},{7,2},{8,13},{9,12},{10,... | collective-permute-start | bytes 294920 | tf_op jit(solution)/shard_map/ppermute | solution.py:717
  16.3 5.6 %collective-permute-start.16 = (bf16[192,256]{1,0:T(8,128)(2,1)S(1)}, bf16[192,256]{1,0:T(8,128)(2,1)S(1)}, u32[]{:S(2)}, u32[]{:S(2)}) collective-permute-start(bf16[192,256]{1,0:T(8,128)(2,1)S(1)} %get-tuple-element.50), channel_id=1, source_target_pairs={{0,7},{1,6},{2,5},{3,4},{4,3},{5,2},{6,1},{7,0},{8,15},{9,14},{10,... | collective-permute-start | bytes 294920 | tf_op jit(solution)/shard_map/ppermute | solution.py:717
  21.9 18.0 %collective-permute-start.17 = (bf16[4,160,256]{2,1,0:T(8,128)(2,1)S(1)}, bf16[4,160,256]{2,1,0:T(8,128)(2,1)S(1)}, u32[]{:S(2)}, u32[]{:S(2)}) collective-permute-start(bf16[4,160,256]{2,1,0:T(8,128)(2,1)S(1)} %get-tuple-element.52), channel_id=1, source_target_pairs={{0,1},{1,0},{2,3},{3,2},{4,5},{5,4},{6,7},{7,6},{8,9},{9,8},{10,11... | collective-permute-start | bytes 983048 | tf_op jit(solution)/shard_map/ppermute | solution.py:717
  22.0 3.4 %copy-start.4 = (s32[4]{0:T(128)S(1)}, s32[4]{0:T(128)}, u32[]{:S(2)}) copy-start(s32[4]{0:T(128)} %param.13) | copy-start | bytes 52
  22.0 18.0 %copy-start.2 = (bf16[4,1,2048,32]{2,3,1,0:T(8,128)(2,1)S(1)}, bf16[4,1,2048,32]{2,3,1,0:T(8,128)(2,1)}, u32[]{:S(2)}) copy-start(bf16[4,1,2048,32]{2,3,1,0:T(8,128)(2,1)} %param.9) | copy-start | bytes 1572868
  22.1 17.9 %copy-start.1 = (bf16[4,1,2048,32]{2,3,1,0:T(8,128)(2,1)S(1)}, bf16[4,1,2048,32]{2,3,1,0:T(8,128)(2,1)}, u32[]{:S(2)}) copy-start(bf16[4,1,2048,32]{2,3,1,0:T(8,128)(2,1)} %param.8) | copy-start | bytes 1572868
  22.1 3.8 %collective-permute-start.1 = (bf16[128,256]{1,0:T(8,128)(2,1)S(1)}, bf16[128,256]{1,0:T(8,128)(2,1)S(1)}, u32[]{:S(2)}, u32[]{:S(2)}) collective-permute-start(bf16[128,256]{1,0:T(8,128)(2,1)S(1)} %get-tuple-element.36), channel_id=1, source_target_pairs={{0,3},{1,2},{2,1},{3,0},{4,7},{5,6},{6,5},{7,4},{8,11},{9,10},{10,... | collective-permute-start | bytes 196616 | tf_op jit(solution)/shard_map/ppermute | solution.py:717
  23.3 4.2 %collective-permute-start.2 = (bf16[128,256]{1,0:T(8,128)(2,1)S(1)}, bf16[128,256]{1,0:T(8,128)(2,1)S(1)}, u32[]{:S(2)}, u32[]{:S(2)}) collective-permute-start(bf16[128,256]{1,0:T(8,128)(2,1)S(1)} %get-tuple-element.37), channel_id=1, source_target_pairs={{0,5},{1,4},{2,7},{3,6},{4,1},{5,0},{6,3},{7,2},{8,13},{9,12},{10,... | collective-permute-start | bytes 196616 | tf_op jit(solution)/shard_map/ppermute | solution.py:717
  23.9 4.6 %collective-permute-start.3 = (bf16[128,256]{1,0:T(8,128)(2,1)S(1)}, bf16[128,256]{1,0:T(8,128)(2,1)S(1)}, u32[]{:S(2)}, u32[]{:S(2)}) collective-permute-start(bf16[128,256]{1,0:T(8,128)(2,1)S(1)} %get-tuple-element.38), channel_id=1, source_target_pairs={{0,7},{1,6},{2,5},{3,4},{4,3},{5,2},{6,1},{7,0},{8,15},{9,14},{10,... | collective-permute-start | bytes 196616 | tf_op jit(solution)/shard_map/ppermute | solution.py:717
  28.6 4.5 %collective-permute-start.4 = (bf16[64,256]{1,0:T(8,128)(2,1)S(1)}, bf16[64,256]{1,0:T(8,128)(2,1)S(1)}, u32[]{:S(2)}, u32[]{:S(2)}) collective-permute-start(bf16[64,256]{1,0:T(8,128)(2,1)S(1)} %get-tuple-element.40), channel_id=1, source_target_pairs={{0,8},{8,0},{16,24},{24,16},{1,9},{9,1},{17,25},{25,17},{2,10},{10... | collective-permute-start | bytes 98312 | tf_op jit(solution)/shard_map/ppermute | solution.py:721
  28.7 5.1 %collective-permute-start.5 = (bf16[64,256]{1,0:T(8,128)(2,1)S(1)}, bf16[64,256]{1,0:T(8,128)(2,1)S(1)}, u32[]{:S(2)}, u32[]{:S(2)}) collective-permute-start(bf16[64,256]{1,0:T(8,128)(2,1)S(1)} %get-tuple-element.40), channel_id=1, source_target_pairs={{0,16},{8,24},{16,0},{24,8},{1,17},{9,25},{17,1},{25,9},{2,18},{10... | collective-permute-start | bytes 98312 | tf_op jit(solution)/shard_map/ppermute | solution.py:721
  29.7 5.7 %collective-permute-start.6 = (bf16[64,256]{1,0:T(8,128)(2,1)S(1)}, bf16[64,256]{1,0:T(8,128)(2,1)S(1)}, u32[]{:S(2)}, u32[]{:S(2)}) collective-permute-start(bf16[64,256]{1,0:T(8,128)(2,1)S(1)} %get-tuple-element.40), channel_id=1, source_target_pairs={{0,24},{8,16},{16,8},{24,0},{1,25},{9,17},{17,9},{25,1},{2,26},{10... | collective-permute-start | bytes 98312 | tf_op jit(solution)/shard_map/ppermute | solution.py:721
  35.4 0.7 %copy-start.5 = (s32[4,1]{0,1:T(1,128)S(1)}, s32[4,1]{0,1:T(1,128)}, u32[]{:S(2)}) copy-start(s32[4,1]{0,1:T(1,128)} %param.10) | copy-start | bytes 52
  35.6 4.5 %copy-start.3 = (bf16[2048,32]{0,1:T(8,128)(2,1)S(1)}, bf16[2048,32]{0,1:T(8,128)(2,1)}, u32[]{:S(2)}) copy-start(bf16[2048,32]{0,1:T(8,128)(2,1)} %param.15) | copy-start | bytes 393220
  35.6 1.3 %collective-permute-start.7 = (f32[4,32,128]{2,1,0:T(8,128)S(1)}, f32[4,32,128]{2,1,0:T(8,128)S(1)}, u32[]{:S(2)}, u32[]{:S(2)}) collective-permute-start(f32[4,32,128]{2,1,0:T(8,128)S(1)} %get-tuple-element.42), channel_id=1, source_target_pairs={{0,1},{1,0},{2,3},{3,2},{4,5},{5,4},{6,7},{7,6},{8,9},{9,8},{10,11... | collective-permute-start | bytes 196616 | tf_op jit(solution)/shard_map/ppermute | solution.py:717
  36.9 4.4 %collective-permute-start.10 = (f32[32,128]{1,0:T(8,128)S(1)}, f32[32,128]{1,0:T(8,128)S(1)}, u32[]{:S(2)}, u32[]{:S(2)}) collective-permute-start(f32[32,128]{1,0:T(8,128)S(1)} %get-tuple-element.46), channel_id=1, source_target_pairs={{0,7},{1,6},{2,5},{3,4},{4,3},{5,2},{6,1},{7,0},{8,15},{9,14},{10,... | collective-permute-start | bytes 49160 | tf_op jit(solution)/shard_map/ppermute | solution.py:717
  38.3 3.2 %collective-permute-start.8 = (f32[32,128]{1,0:T(8,128)S(1)}, f32[32,128]{1,0:T(8,128)S(1)}, u32[]{:S(2)}, u32[]{:S(2)}) collective-permute-start(f32[32,128]{1,0:T(8,128)S(1)} %get-tuple-element.44), channel_id=1, source_target_pairs={{0,3},{1,2},{2,1},{3,0},{4,7},{5,6},{6,5},{7,4},{8,11},{9,10},{10,... | collective-permute-start | bytes 49160 | tf_op jit(solution)/shard_map/ppermute | solution.py:717
  39.3 3.2 %collective-permute-start.9 = (f32[32,128]{1,0:T(8,128)S(1)}, f32[32,128]{1,0:T(8,128)S(1)}, u32[]{:S(2)}, u32[]{:S(2)}) collective-permute-start(f32[32,128]{1,0:T(8,128)S(1)} %get-tuple-element.45), channel_id=1, source_target_pairs={{0,5},{1,4},{2,7},{3,6},{4,1},{5,0},{6,3},{7,2},{8,13},{9,12},{10,... | collective-permute-start | bytes 49160 | tf_op jit(solution)/shard_map/ppermute | solution.py:717

commit v4 on v3

--- a/solution.py
+++ b/solution.py
@@ -412,10 +412,6 @@
     return pl.ds(pl.multiple_of(block * piece, LANES), piece)
 
 
-def pieces_wide(ref, count, piece):
-    return jnp.concatenate([ref[:, piece_spot(k, piece)] for k in range(count)], axis=1)
-
-
 def same_tile(lines, width):
     lane = lax.broadcasted_iota(jnp.int32, (lines, lines), 1)
     line = lax.broadcasted_iota(jnp.int32, (lines, lines), 0)
@@ -430,66 +426,95 @@
     return even_ref[step, width:], even_ref[step, :width]
 
 
-def panel_wide(even_ref, odd_ref, width):
-    parts = [panel_piece(even_ref, odd_ref, k, width) for k in range(2 * even_ref.shape[0])]
-    return [jnp.concatenate(side, axis=1) for side in zip(*parts)]
-
-
-def gram_kernel(width, *refs):
-    left_ref, right_ref, sketch_ref, even_ref, odd_ref, keep_line_ref, keep_lane_ref = refs[:7]
-    (
-        row_high_ref,
-        row_low_ref,
-        right_gram_ref,
-        sketch_right_ref,
-        column_right_ref,
-        column_column_ref,
-        sketch_column_ref,
-    ) = refs[7:]
-    lines = left_ref.shape[0]
-    piece = even_ref.shape[2]
-    count = 2 * even_ref.shape[0]
-    same = same_tile(lines, width)
-    panel, column = panel_wide(even_ref, odd_ref, width)
-    left = pieces_wide(left_ref, count, piece)
-    for i, one in enumerate((left, panel)):
-        for j, two in enumerate((left, panel)):
-            high, low = split(jnp.where(same, nt(one, two), 0.0))
-            row_high_ref[i * lines : (i + 1) * lines, j * lines : (j + 1) * lines] = high
-            row_low_ref[i * lines : (i + 1) * lines, j * lines : (j + 1) * lines] = low
-    right = pieces_wide(right_ref, count, piece)
-    sketch = pieces_wide(sketch_ref, count, piece)
+def partial_grams(given, left_ref, right_ref, sketch_ref, panel_ref, width):
+    count, lines, piece = panel_ref.shape
+    lines = lines - width
+    relatives = [partner(step) ^ given for step in range(count)]
+    if given:
+        panel = jnp.concatenate([panel_ref[k, :lines] for k in range(count)], axis=1)
+        column = jnp.concatenate([panel_ref[k, lines:] for k in range(count)], axis=1)
+    else:
+        panel = jnp.concatenate([panel_ref[k, width:] for k in range(count)], axis=1)
+        column = jnp.concatenate([panel_ref[k, :width] for k in range(count)], axis=1)
+    left, right, sketch = (
+        jnp.concatenate([ref[:, piece_spot(k, piece)] for k in relatives], axis=1)
+        for ref in (left_ref, right_ref, sketch_ref)
+    )
+    return (
+        nt(left, panel),
+        nt(panel, panel),
+        nt(column, right),
+        nt(column, column),
+        nt(sketch, column),
+    )
+
+
+def early_gram_kernel(width, *refs):
+    left_ref, right_ref, sketch_ref, even_ref, keep_line_ref, keep_lane_ref = refs[:6]
+    left_high_ref, left_low_ref, right_gram_ref, sketch_right_ref, *sum_refs = refs[6:]
+    sums = partial_grams(0, left_ref, right_ref, sketch_ref, even_ref, width)
+    for ref, value in zip(sum_refs, sums):
+        ref[...] = value
+    same = same_tile(left_ref.shape[0], width)
+    left, right = left_ref[...], right_ref[...]
+    left_high_ref[...], left_low_ref[...] = split(jnp.where(same, nt(left, left), 0.0))
     keep_line = keep_line_ref[...] > 0.0
     keep_lane = keep_lane_ref[:1] > 0.0
     right_gram_ref[...] = jnp.where(same & keep_line & keep_lane, nt(right, right), 0.0)
-    sketch_right_ref[...] = jnp.where(keep_lane, nt(sketch, right), 0.0)
-    column_right_ref[...] = jnp.where(keep_lane, nt(column, right), 0.0)
-    column_column_ref[...] = nt(column, column)
-    sketch_column_ref[...] = nt(sketch, column)
-
-
-def grams(left, right, sketch, even, odd, keep_line, keep_lane, width):
+    sketch_right_ref[...] = jnp.where(keep_lane, nt(sketch_ref[...], right), 0.0)
+
+
+def early_grams(left, right, sketch, even, keep_line, keep_lane, width):
     lines, order = left.shape
-    square = jax.ShapeDtypeStruct((2 * lines, 2 * lines), BF16)
+    rounded = jax.ShapeDtypeStruct((lines, lines), BF16)
+    square = jax.ShapeDtypeStruct((lines, lines), F32)
     flat = jax.ShapeDtypeStruct((width, lines), F32)
     small = jax.ShapeDtypeStruct((width, width), F32)
-    return pl.pallas_call(
-        functools.partial(gram_kernel, width),
-        in_specs=in_vmem(7),
+    outs = [rounded, rounded, square, flat, square, square, flat, small, small]
+    return pl.pallas_call(
+        functools.partial(early_gram_kernel, width),
+        in_specs=in_vmem(6),
+        out_specs=in_vmem(len(outs)),
+        out_shape=outs,
+        name="early_grams",
+        compiler_params=grant(16),
+        cost_estimate=small_cost(1000000, 2 * order * lines * lines * 5),
+    )(left, right, sketch, even, keep_line, keep_lane)
+
+
+def late_gram_kernel(width, *refs):
+    left_ref, right_ref, sketch_ref, odd_ref, keep_lane_ref, *sum_refs = refs[:10]
+    side_high_ref, side_low_ref, turned_high_ref, turned_low_ref, *out_refs = refs[10:]
+    lines = left_ref.shape[0]
+    same = same_tile(lines, width)
+    sums = partial_grams(1, left_ref, right_ref, sketch_ref, odd_ref, width)
+    cross, own, column_right, column_column, sketch_column = (
+        ref[...] + value for ref, value in zip(sum_refs, sums)
+    )
+    cross = jnp.where(same, cross, 0.0)
+    side_high_ref[:lines], side_low_ref[:lines] = split(cross)
+    turned_high_ref[...], turned_low_ref[...] = split(cross.T)
+    side_high_ref[lines:], side_low_ref[lines:] = split(jnp.where(same, own, 0.0))
+    column_right = jnp.where(keep_lane_ref[:1] > 0.0, column_right, 0.0)
+    for ref, value in zip(out_refs, (column_right, column_column, sketch_column)):
+        ref[...] = value
+
+
+def late_grams(left, right, sketch, odd, keep_lane, sums, width):
+    lines, order = left.shape
+    square = jax.ShapeDtypeStruct((lines, lines), BF16)
+    tall = jax.ShapeDtypeStruct((2 * lines, lines), BF16)
+    flat = jax.ShapeDtypeStruct((width, lines), F32)
+    small = jax.ShapeDtypeStruct((width, width), F32)
+    return pl.pallas_call(
+        functools.partial(late_gram_kernel, width),
+        in_specs=in_vmem(10),
         out_specs=in_vmem(7),
-        out_shape=[
-            square,
-            square,
-            jax.ShapeDtypeStruct((lines, lines), F32),
-            flat,
-            flat,
-            small,
-            small,
-        ],
-        name="grams",
+        out_shape=[tall, tall, square, square, flat, small, small],
+        name="late_grams",
         compiler_params=grant(16),
-        cost_estimate=small_cost(2000000, 2 * order * lines * lines * 8),
-    )(left, right, sketch, even, odd, keep_line, keep_lane)
+        cost_estimate=small_cost(1000000, 2 * order * lines * lines * 2),
+    )(left, right, sketch, odd, keep_lane, *sums)
 
 
 def factor_and_apply(gram, shift, bands):
@@ -558,10 +583,14 @@
 def finish_kernel(half, width, rows_total, *refs):
     core_refs = refs[:half]
     (
-        row_high_ref,
-        row_low_ref,
+        left_high_ref,
+        left_low_ref,
         right_gram_ref,
         sketch_right_ref,
+        side_high_ref,
+        side_low_ref,
+        turned_high_ref,
+        turned_low_ref,
         column_right_ref,
         column_column_ref,
         sketch_column_ref,
@@ -600,7 +629,16 @@
         live = (tile * rows_total + my_row) > my_col
         live_line |= (lane_row >= low) & (lane_row < low + jnp.where(live, width, 0))
 
-    row_parts = (row_high_ref[...], row_low_ref[...])
+    row_parts = [
+        jnp.concatenate(
+            [jnp.concatenate([one[...], turned[...]], axis=0), side[...]],
+            axis=1,
+        )
+        for one, turned, side in (
+            (left_high_ref, turned_high_ref, side_high_ref),
+            (left_low_ref, turned_low_ref, side_low_ref),
+        )
+    ]
     core = core_refs[0][...]
     for ref in core_refs[1:]:
         core = core + ref[...]
@@ -657,7 +695,6 @@
         ],
         axis=1,
     ).astype(BF16)
-    copies = []
     for relative in range(count):
         spot = piece_spot(relative, piece)
         panel, column = panel_piece(even_ref, odd_ref, relative, width)
@@ -668,16 +705,14 @@
         for side, (ref, hbm) in enumerate(
             ((out_left_ref, out_left_hbm), (out_right_ref, out_right_hbm))
         ):
-            copy = pltpu.make_async_copy(ref.at[relative], hbm.at[:, spot], sems.at[relative, side])
-            copy.start()
-            copies.append(copy)
-    for copy in copies:
-        copy.wait()
+            pltpu.make_async_copy(ref.at[relative], hbm.at[:, spot], sems.at[side]).start()
+    for side, hbm in enumerate((out_left_hbm, out_right_hbm)):
+        pltpu.make_async_copy(hbm, hbm, sems.at[side]).wait()
 
 
 def finish(cores, others, rows_total, width):
     half = len(cores)
-    left = others[7]
+    left = others[11]
     lines, piece = left.shape[0], left.shape[1] // (2 * half)
     shape = jax.ShapeDtypeStruct(left.shape, BF16)
     operands = (*cores, *others)
@@ -689,7 +724,7 @@
         scratch_shapes=[
             VMEM((2 * half, lines, piece), BF16),
             VMEM((2 * half, lines, piece), BF16),
-            pltpu.SemaphoreType.DMA((2 * half, 2)),
+            pltpu.SemaphoreType.DMA((2,)),
         ],
         name="finish",
         compiler_params=grant(16),
@@ -741,14 +776,14 @@
     own_message, *sends = messages(panel, panel_others, rows_total, cols_total, width)
     even_panel, odd_panel = bundle([own_message] + across(sends), width)
     odd_panel = swap(odd_panel, 1)
-    gram_parts = grams(
-        left, right, sketch_lines, even_panel, odd_panel, slab_line, slab_lane, width
-    )
+    early = early_grams(left, right, sketch_lines, even_panel, slab_line, slab_lane, width)
+    slab_parts, sums = early[:4], early[4:]
+    panel_parts = late_grams(left, right, sketch_lines, odd_panel, slab_lane, sums, width)
     core_even, core_odd = core_parts(solved, solved_others, rows_total, cols_total, width)
     kept, *sends = pair_add(core_even, swap(core_odd, 1), F32)
     fresh_left, fresh_right = finish(
         [kept] + across(sends),
-        (*gram_parts, left, right, even_panel, odd_panel, slab_lane),
+        (*slab_parts, *panel_parts, left, right, even_panel, odd_panel, slab_lane),
         rows_total,
         width,
     )

time: 45.9 us -> 46.2 us (level)
    pallas_call x1 -> x2, Pallas kernels: 1.21 us -> 1.22 us  [the longest x1 0.82 us: early_grams(): pl.pallas_call(functools.partial(early_gram_kernel, width), in_specs=in_v...]
  transfers between devices with their start and end apart: 18 -> 18, of which waited for: 12 -> 11; matrix products, arithmetic and copies ran while one was open for 1% -> 1% of each run, Pallas kernels for 5% -> 5%
where the time goes in v4:
time: 46.2 us; the launch traced here: 46.1 us
  starting transfers between devices  19.4 us (42%)
  waiting for transfers between devices  17.6 us (38%)
  Pallas kernels  7.35 us (16%)
  between operations  0.81 us (2%)
  local copies, waits for them, and re-layouts  0.72 us (2%)
    ppermute x6, starting transfers between devices, turn(): return lax.ppermute(block, 'row', pairs)  9.83 us
    ppermute x12, waiting for transfers between devices, swap(): lax.ppermute(block, 'col', [(i, i ^ step) for i in range(cols_total)])  9.64 us
    ppermute x12, starting transfers between devices, swap(): lax.ppermute(block, 'col', [(i, i ^ step) for i in range(cols_total)])  9.6 us
    ppermute x6, waiting for transfers between devices, turn(): return lax.ppermute(block, 'row', pairs)  7.99 us
    pallas_call x1, Pallas kernels, finish(): pl.pallas_call(functools.partial(finish_kernel, half, width, rows_total),...  3.19 us
    pallas_call x1, Pallas kernels, solve_odd(): pl.pallas_call(solve_odd_kernel, in_specs=[pl.BlockSpec(memory_space=pltp...  1.86 us
  transfers between devices with their start and end apart: 18, of which 11 were waited for; matrix products, arithmetic and copies ran while one was open for 1% of the time, Pallas kernels for 5%

profile of v4, /device:TPU:0, one launch (start us, length us, event | category | flops | bytes accessed | tf_op | source)
XLA Modules:
  0.0 46.1 jit_solution(12036825124273927009)
XLA Ops:
  0.6 0.0 copy-start.3
  0.6 1.9 %solve_odd.1 = (bf16[4,128,256]{2,1,0:T(8,128)(2,1)S(1)}, bf16[128,256]{1,0:T(8,128)(2,1)S(1)}, bf16[4,256,256]{2,1,0:T(8,128)(2,1)S(1)}) custom-call(bf16[128,256]{1,0:T(8,128)(2,1)} %bitcast.35, bf16[2048,256]{1,0:T(8,128)(2,1)} %inverse_hbm.1), custom_call_target="tpu_custom_call" | custom-call | flops 67108864 | bytes 1572864 | tf_op jit(solution)/shard_map/solve_odd/pallas_call | solution.py:226
  2.5 0.4 collective-permute-start
  2.9 0.0 copy-done.3
  2.9 2.8 %collective-permute-start.11 = (bf16[64,256]{1,0:T(8,128)(2,1)S(1)}, bf16[64,256]{1,0:T(8,128)(2,1)S(1)}, u32[]{:S(2)}, u32[]{:S(2)}) collective-permute-start(bf16[64,256]{1,0:T(8,128)(2,1)S(1)} %bitcast.36), channel_id=1, source_target_pairs={{0,8},{8,0},{16,24},{24,16},{1,9},{9,1},{17,25},{25,17},{2,10},{10... | collective-permute-start | bytes 98312 | tf_op jit(solution)/shard_map/ppermute | solution.py:756
  5.7 2.6 %collective-permute-start.12 = (bf16[64,256]{1,0:T(8,128)(2,1)S(1)}, bf16[64,256]{1,0:T(8,128)(2,1)S(1)}, u32[]{:S(2)}, u32[]{:S(2)}) collective-permute-start(bf16[64,256]{1,0:T(8,128)(2,1)S(1)} %bitcast.37), channel_id=1, source_target_pairs={{0,16},{8,24},{16,0},{24,8},{1,17},{9,25},{17,1},{25,9},{2,18},{10... | collective-permute-start | bytes 98312 | tf_op jit(solution)/shard_map/ppermute | solution.py:756
  8.3 0.0 collective-permute-start.13
  8.3 0.0 collective-permute-done.11.refs_0_
  8.3 2.8 %collective-permute-done.12.refs_1_ = bf16[64,256]{1,0:T(8,128)(2,1)S(1)} collective-permute-done((bf16[64,256]{1,0:T(8,128)(2,1)S(1)}, bf16[64,256]{1,0:T(8,128)(2,1)S(1)}, u32[]{:S(2)}, u32[]{:S(2)}) %collective-permute-start.12) | collective-permute-done | bytes 32800 | tf_op jit(solution)/shard_map/ppermute | solution.py:756
  11.1 2.9 %collective-permute-done.13.refs_2_ = bf16[64,256]{1,0:T(8,128)(2,1)S(1)} collective-permute-done((bf16[64,256]{1,0:T(8,128)(2,1)S(1)}, bf16[64,256]{1,0:T(8,128)(2,1)S(1)}, u32[]{:S(2)}, u32[]{:S(2)}) %collective-permute-start.13) | collective-permute-done | bytes 32800 | tf_op jit(solution)/shard_map/ppermute | solution.py:756
  14.1 0.1 collective-permute-start.14
  14.2 2.1 %collective-permute-start.15 = (bf16[192,256]{1,0:T(8,128)(2,1)S(1)}, bf16[192,256]{1,0:T(8,128)(2,1)S(1)}, u32[]{:S(2)}, u32[]{:S(2)}) collective-permute-start(bf16[192,256]{1,0:T(8,128)(2,1)S(1)} %get-tuple-element.58), channel_id=1, source_target_pairs={{0,5},{1,4},{2,7},{3,6},{4,1},{5,0},{6,3},{7,2},{8,13},{9,12},{10,... | collective-permute-start | bytes 294920 | tf_op jit(solution)/shard_map/ppermute | solution.py:752
  16.3 0.4 collective-permute-start.16
  16.7 0.7 %solve_even.1.mine_ref = f32[4,128,256]{2,1,0:T(8,128)S(1)} custom-call(bf16[128,256]{1,0:T(8,128)(2,1)S(1)} %get-tuple-element.41.right_ref, bf16[4,256,256]{2,1,0:T(8,128)(2,1)S(1)} %get-tuple-element.42.even_ref), custom_call_target="tpu_custom_call" | custom-call | flops 67108864 | bytes 1048576 | tf_op jit(solution)/shard_map/solve_even/pallas_call | solution.py:258
  17.4 1.7 %collective-permute-done.14.refs_1_ = bf16[192,256]{1,0:T(8,128)(2,1)S(1)} collective-permute-done((bf16[192,256]{1,0:T(8,128)(2,1)S(1)}, bf16[192,256]{1,0:T(8,128)(2,1)S(1)}, u32[]{:S(2)}, u32[]{:S(2)}) %collective-permute-start.14) | collective-permute-done | bytes 98336 | tf_op jit(solution)/shard_map/ppermute | solution.py:752
  19.1 0.0 collective-permute-done.15.refs_2_
  19.1 2.8 %collective-permute-done.16.refs_3_ = bf16[192,256]{1,0:T(8,128)(2,1)S(1)} collective-permute-done((bf16[192,256]{1,0:T(8,128)(2,1)S(1)}, bf16[192,256]{1,0:T(8,128)(2,1)S(1)}, u32[]{:S(2)}, u32[]{:S(2)}) %collective-permute-start.16) | collective-permute-done | bytes 98336 | tf_op jit(solution)/shard_map/ppermute | solution.py:752
  21.9 0.1 collective-permute-start.17
  22.0 0.0 collective-permute-done.other_ref
  22.0 0.0 copy-start.4
  22.0 0.0 copy-start.1
  22.0 0.1 pair_add.2
  22.1 0.0 copy-start
  22.1 1.2 %collective-permute-start.1 = (bf16[128,256]{1,0:T(8,128)(2,1)S(1)}, bf16[128,256]{1,0:T(8,128)(2,1)S(1)}, u32[]{:S(2)}, u32[]{:S(2)}) collective-permute-start(bf16[128,256]{1,0:T(8,128)(2,1)S(1)} %get-tuple-element.45), channel_id=1, source_target_pairs={{0,3},{1,2},{2,1},{3,0},{4,7},{5,6},{6,5},{7,4},{8,11},{9,10},{10,... | collective-permute-start | bytes 196616 | tf_op jit(solution)/shard_map/ppermute | solution.py:752
  23.3 0.6 %collective-permute-start.2 = (bf16[128,256]{1,0:T(8,128)(2,1)S(1)}, bf16[128,256]{1,0:T(8,128)(2,1)S(1)}, u32[]{:S(2)}, u32[]{:S(2)}) collective-permute-start(bf16[128,256]{1,0:T(8,128)(2,1)S(1)} %get-tuple-element.46), channel_id=1, source_target_pairs={{0,5},{1,4},{2,7},{3,6},{4,1},{5,0},{6,3},{7,2},{8,13},{9,12},{10,... | collective-permute-start | bytes 196616 | tf_op jit(solution)/shard_map/ppermute | solution.py:752
  23.9 1.6 %collective-permute-start.3 = (bf16[128,256]{1,0:T(8,128)(2,1)S(1)}, bf16[128,256]{1,0:T(8,128)(2,1)S(1)}, u32[]{:S(2)}, u32[]{:S(2)}) collective-permute-start(bf16[128,256]{1,0:T(8,128)(2,1)S(1)} %get-tuple-element.47), channel_id=1, source_target_pairs={{0,7},{1,6},{2,5},{3,4},{4,3},{5,2},{6,1},{7,0},{8,15},{9,14},{10,... | collective-permute-start | bytes 196616 | tf_op jit(solution)/shard_map/ppermute | solution.py:752
  25.4 0.0 copy-done.4
  25.4 0.1 fusion
  25.5 0.1 reshape.78
  25.6 0.3 collective-permute-done.1.refs_0_
  25.9 1.5 %collective-permute-done.2.refs_1_ = bf16[128,256]{1,0:T(8,128)(2,1)S(1)} collective-permute-done((bf16[128,256]{1,0:T(8,128)(2,1)S(1)}, bf16[128,256]{1,0:T(8,128)(2,1)S(1)}, u32[]{:S(2)}, u32[]{:S(2)}) %collective-permute-start.2) | collective-permute-done | bytes 65568 | tf_op jit(solution)/shard_map/ppermute | solution.py:752
  27.5 1.0 %collective-permute-done.3.refs_2_ = bf16[128,256]{1,0:T(8,128)(2,1)S(1)} collective-permute-done((bf16[128,256]{1,0:T(8,128)(2,1)S(1)}, bf16[128,256]{1,0:T(8,128)(2,1)S(1)}, u32[]{:S(2)}, u32[]{:S(2)}) %collective-permute-start.3) | collective-permute-done | bytes 65568 | tf_op jit(solution)/shard_map/ppermute | solution.py:752
  28.5 0.1 broadcast_in_dim.6.mask_ref
  28.6 0.1 collective-permute-start.4
  28.7 0.9 %collective-permute-start.5 = (bf16[64,256]{1,0:T(8,128)(2,1)S(1)}, bf16[64,256]{1,0:T(8,128)(2,1)S(1)}, u32[]{:S(2)}, u32[]{:S(2)}) collective-permute-start(bf16[64,256]{1,0:T(8,128)(2,1)S(1)} %get-tuple-element.49), channel_id=1, source_target_pairs={{0,16},{8,24},{16,0},{24,8},{1,17},{9,25},{17,1},{25,9},{2,18},{10... | collective-permute-start | bytes 98312 | tf_op jit(solution)/shard_map/ppermute | solution.py:756
  29.7 3.4 %collective-permute-start.6 = (bf16[64,256]{1,0:T(8,128)(2,1)S(1)}, bf16[64,256]{1,0:T(8,128)(2,1)S(1)}, u32[]{:S(2)}, u32[]{:S(2)}) collective-permute-start(bf16[64,256]{1,0:T(8,128)(2,1)S(1)} %get-tuple-element.49), channel_id=1, source_target_pairs={{0,24},{8,16},{16,8},{24,0},{1,25},{9,17},{17,9},{25,1},{2,26},{10... | collective-permute-start | bytes 98312 | tf_op jit(solution)/shard_map/ppermute | solution.py:756
  33.1 0.0 collective-permute-done.4.refs_0_
  33.1 0.7 %collective-permute-done.5.refs_1_ = bf16[64,256]{1,0:T(8,128)(2,1)S(1)} collective-permute-done((bf16[64,256]{1,0:T(8,128)(2,1)S(1)}, bf16[64,256]{1,0:T(8,128)(2,1)S(1)}, u32[]{:S(2)}, u32[]{:S(2)}) %collective-permute-start.5) | collective-permute-done | bytes 32800 | tf_op jit(solution)/shard_map/ppermute | solution.py:756
  33.8 1.6 %collective-permute-done.6.refs_2_ = bf16[64,256]{1,0:T(8,128)(2,1)S(1)} collective-permute-done((bf16[64,256]{1,0:T(8,128)(2,1)S(1)}, bf16[64,256]{1,0:T(8,128)(2,1)S(1)}, u32[]{:S(2)}, u32[]{:S(2)}) %collective-permute-start.6) | collective-permute-done | bytes 32800 | tf_op jit(solution)/shard_map/ppermute | solution.py:756
  35.4 0.0 copy-start.5
  35.4 0.2 core_parts.1
  35.6 0.0 copy-start.2
  35.6 0.1 collective-permute-start.7
  35.7 0.4 copy-done.5
  36.0 0.1 fusion.1
  36.1 0.1 reshape.79
  36.2 0.7 %collective-permute-done.7.other_ref = f32[4,32,128]{2,1,0:T(8,128)S(1)} collective-permute-done((f32[4,32,128]{2,1,0:T(8,128)S(1)}, f32[4,32,128]{2,1,0:T(8,128)S(1)}, u32[]{:S(2)}, u32[]{:S(2)}) %collective-permute-start.7) | collective-permute-done | bytes 65568 | tf_op jit(solution)/shard_map/ppermute | solution.py:752
  36.9 1.0 %collective-permute-start.8 = (f32[32,128]{1,0:T(8,128)S(1)}, f32[32,128]{1,0:T(8,128)S(1)}, u32[]{:S(2)}, u32[]{:S(2)}) collective-permute-start(f32[32,128]{1,0:T(8,128)S(1)} %get-tuple-element.53), channel_id=1, source_target_pairs={{0,3},{1,2},{2,1},{3,0},{4,7},{5,6},{6,5},{7,4},{8,11},{9,10},{10,... | collective-permute-start | bytes 49160 | tf_op jit(solution)/shard_map/ppermute | solution.py:752
  37.9 0.9 %collective-permute-start.9 = (f32[32,128]{1,0:T(8,128)S(1)}, f32[32,128]{1,0:T(8,128)S(1)}, u32[]{:S(2)}, u32[]{:S(2)}) collective-permute-start(f32[32,128]{1,0:T(8,128)S(1)} %get-tuple-element.54), channel_id=1, source_target_pairs={{0,5},{1,4},{2,7},{3,6},{4,1},{5,0},{6,3},{7,2},{8,13},{9,12},{10,... | collective-permute-start | bytes 49160 | tf_op jit(solution)/shard_map/ppermute | solution.py:752
  38.8 1.1 %collective-permute-start.10 = (f32[32,128]{1,0:T(8,128)S(1)}, f32[32,128]{1,0:T(8,128)S(1)}, u32[]{:S(2)}, u32[]{:S(2)}) collective-permute-start(f32[32,128]{1,0:T(8,128)S(1)} %get-tuple-element.55), channel_id=1, source_target_pairs={{0,7},{1,6},{2,5},{3,4},{4,3},{5,2},{6,1},{7,0},{8,15},{9,14},{10,... | collective-permute-start | bytes 49160 | tf_op jit(solution)/shard_map/ppermute | solution.py:752
  39.9 0.1 broadcast_in_dim.7.refs_4_
  40.0 0.0 copy-done.1
  40.0 0.0 copy-done
  40.0 0.0 copy-done.2
  40.1 0.8 %early_grams.1 = (bf16[128,128]{1,0:T(8,128)(2,1)S(1)}, bf16[128,128]{1,0:T(8,128)(2,1)S(1)}, f32[128,128]{1,0:T(8,128)S(1)}, f32[32,128]{1,0:T(8,128)S(1)}, f32...) custom-call(bf16[128,2048]{1,0:T(8,128)(2,1)S(1)} %bitcast.25, ...), custom_call_target="tpu_custom_call" | custom-call | flops 335544320 | bytes 1000000 | tf_op jit(solution)/shard_map/early_grams/pallas_call | solution.py:474
  40.9 0.0 collective-permute-done.17.refs_3_.refs_18_
  40.9 0.4 late_grams.1
  41.3 0.0 collective-permute-done.8.refs_1_
  41.3 0.0 collective-permute-done.9.refs_2_
  41.3 1.6 %collective-permute-done.10.refs_3_ = f32[32,128]{1,0:T(8,128)S(1)} collective-permute-done((f32[32,128]{1,0:T(8,128)S(1)}, f32[32,128]{1,0:T(8,128)S(1)}, u32[]{:S(2)}, u32[]{:S(2)}) %collective-permute-start.10) | collective-permute-done | bytes 16416 | tf_op jit(solution)/shard_map/ppermute | solution.py:752
  42.9 3.2 %finish.1 = (bf16[128,2048]{1,0:T(8,128)(2,1)}, bf16[128,2048]{1,0:T(8,128)(2,1)}) custom-call(f32[32,128]{1,0:T(8,128)S(1)} %get-tuple-element.52.refs_0_, f32[32,128]{1,0:T(8,128)S(1)} %collective-permute-done.8.refs_1_, f32[32,128]{1,0:T(8,128)S(1)} %collective-permute-done.9.refs_2_, f32[32,128]{1,0:T(8,128)S(1)} %collective-permute-done.10.refs_3_, ...), custom_call_target="tpu_custom_call" | custom-call | flops 1000000000 | bytes 5000000 | tf_op jit(solution)/shard_map/finish/pallas_call | solution.py:719
  (6 shorter events, 0.1 us)
Async XLA Ops:
  0.6 2.3 %copy-start.3 = (bf16[4,256,32]{1,2,0:T(8,128)(2,1)S(1)}, bf16[4,256,32]{1,2,0:T(8,128)(2,1)}, u32[]{:S(2)}) copy-start(bf16[4,256,32]{1,2,0:T(8,128)(2,1)} %param.11) | copy-start | bytes 196612
  2.5 19.5 %collective-permute-start = (bf16[4,128,256]{2,1,0:T(8,128)(2,1)S(1)}, bf16[4,128,256]{2,1,0:T(8,128)(2,1)S(1)}, u32[]{:S(2)}, u32[]{:S(2)}) collective-permute-start(bf16[4,128,256]{2,1,0:T(8,128)(2,1)S(1)} %get-tuple-element.43), channel_id=1, source_target_pairs={{0,1},{1,0},{2,3},{3,2},{4,5},{5,4},{6,7},{7,6},{8,9},{9,8},{10,11... | collective-permute-start | bytes 786440 | tf_op jit(solution)/shard_map/ppermute | solution.py:752
  2.9 5.4 %collective-permute-start.11 = (bf16[64,256]{1,0:T(8,128)(2,1)S(1)}, bf16[64,256]{1,0:T(8,128)(2,1)S(1)}, u32[]{:S(2)}, u32[]{:S(2)}) collective-permute-start(bf16[64,256]{1,0:T(8,128)(2,1)S(1)} %bitcast.36), channel_id=1, source_target_pairs={{0,8},{8,0},{16,24},{24,16},{1,9},{9,1},{17,25},{25,17},{2,10},{10... | collective-permute-start | bytes 98312 | tf_op jit(solution)/shard_map/ppermute | solution.py:756
  5.7 5.4 %collective-permute-start.12 = (bf16[64,256]{1,0:T(8,128)(2,1)S(1)}, bf16[64,256]{1,0:T(8,128)(2,1)S(1)}, u32[]{:S(2)}, u32[]{:S(2)}) collective-permute-start(bf16[64,256]{1,0:T(8,128)(2,1)S(1)} %bitcast.37), channel_id=1, source_target_pairs={{0,16},{8,24},{16,0},{24,8},{1,17},{9,25},{17,1},{25,9},{2,18},{10... | collective-permute-start | bytes 98312 | tf_op jit(solution)/shard_map/ppermute | solution.py:756
  8.3 5.7 %collective-permute-start.13 = (bf16[64,256]{1,0:T(8,128)(2,1)S(1)}, bf16[64,256]{1,0:T(8,128)(2,1)S(1)}, u32[]{:S(2)}, u32[]{:S(2)}) collective-permute-start(bf16[64,256]{1,0:T(8,128)(2,1)S(1)} %bitcast.38), channel_id=1, source_target_pairs={{0,24},{8,16},{16,8},{24,0},{1,25},{9,17},{17,9},{25,1},{2,26},{10... | collective-permute-start | bytes 98312 | tf_op jit(solution)/shard_map/ppermute | solution.py:756
  14.1 5.0 %collective-permute-start.14 = (bf16[192,256]{1,0:T(8,128)(2,1)S(1)}, bf16[192,256]{1,0:T(8,128)(2,1)S(1)}, u32[]{:S(2)}, u32[]{:S(2)}) collective-permute-start(bf16[192,256]{1,0:T(8,128)(2,1)S(1)} %get-tuple-element.57), channel_id=1, source_target_pairs={{0,3},{1,2},{2,1},{3,0},{4,7},{5,6},{6,5},{7,4},{8,11},{9,10},{10,... | collective-permute-start | bytes 294920 | tf_op jit(solution)/shard_map/ppermute | solution.py:752
  14.2 4.9 %collective-permute-start.15 = (bf16[192,256]{1,0:T(8,128)(2,1)S(1)}, bf16[192,256]{1,0:T(8,128)(2,1)S(1)}, u32[]{:S(2)}, u32[]{:S(2)}) collective-permute-start(bf16[192,256]{1,0:T(8,128)(2,1)S(1)} %get-tuple-element.58), channel_id=1, source_target_pairs={{0,5},{1,4},{2,7},{3,6},{4,1},{5,0},{6,3},{7,2},{8,13},{9,12},{10,... | collective-permute-start | bytes 294920 | tf_op jit(solution)/shard_map/ppermute | solution.py:752
  16.3 5.6 %collective-permute-start.16 = (bf16[192,256]{1,0:T(8,128)(2,1)S(1)}, bf16[192,256]{1,0:T(8,128)(2,1)S(1)}, u32[]{:S(2)}, u32[]{:S(2)}) collective-permute-start(bf16[192,256]{1,0:T(8,128)(2,1)S(1)} %get-tuple-element.59), channel_id=1, source_target_pairs={{0,7},{1,6},{2,5},{3,4},{4,3},{5,2},{6,1},{7,0},{8,15},{9,14},{10,... | collective-permute-start | bytes 294920 | tf_op jit(solution)/shard_map/ppermute | solution.py:752
  21.9 19.0 %collective-permute-start.17 = (bf16[4,160,256]{2,1,0:T(8,128)(2,1)S(1)}, bf16[4,160,256]{2,1,0:T(8,128)(2,1)S(1)}, u32[]{:S(2)}, u32[]{:S(2)}) collective-permute-start(bf16[4,160,256]{2,1,0:T(8,128)(2,1)S(1)} %get-tuple-element.65), channel_id=1, source_target_pairs={{0,1},{1,0},{2,3},{3,2},{4,5},{5,4},{6,7},{7,6},{8,9},{9,8},{10,11... | collective-permute-start | bytes 983048 | tf_op jit(solution)/shard_map/ppermute | solution.py:752
  22.0 3.4 %copy-start.4 = (s32[4]{0:T(128)S(1)}, s32[4]{0:T(128)}, u32[]{:S(2)}) copy-start(s32[4]{0:T(128)} %param.13) | copy-start | bytes 52
  22.0 18.0 %copy-start.1 = (bf16[4,1,2048,32]{2,3,1,0:T(8,128)(2,1)S(1)}, bf16[4,1,2048,32]{2,3,1,0:T(8,128)(2,1)}, u32[]{:S(2)}) copy-start(bf16[4,1,2048,32]{2,3,1,0:T(8,128)(2,1)} %param.9) | copy-start | bytes 1572868
  22.1 17.9 %copy-start = (bf16[4,1,2048,32]{2,3,1,0:T(8,128)(2,1)S(1)}, bf16[4,1,2048,32]{2,3,1,0:T(8,128)(2,1)}, u32[]{:S(2)}) copy-start(bf16[4,1,2048,32]{2,3,1,0:T(8,128)(2,1)} %param.8) | copy-start | bytes 1572868
  22.1 3.8 %collective-permute-start.1 = (bf16[128,256]{1,0:T(8,128)(2,1)S(1)}, bf16[128,256]{1,0:T(8,128)(2,1)S(1)}, u32[]{:S(2)}, u32[]{:S(2)}) collective-permute-start(bf16[128,256]{1,0:T(8,128)(2,1)S(1)} %get-tuple-element.45), channel_id=1, source_target_pairs={{0,3},{1,2},{2,1},{3,0},{4,7},{5,6},{6,5},{7,4},{8,11},{9,10},{10,... | collective-permute-start | bytes 196616 | tf_op jit(solution)/shard_map/ppermute | solution.py:752
  23.3 4.2 %collective-permute-start.2 = (bf16[128,256]{1,0:T(8,128)(2,1)S(1)}, bf16[128,256]{1,0:T(8,128)(2,1)S(1)}, u32[]{:S(2)}, u32[]{:S(2)}) collective-permute-start(bf16[128,256]{1,0:T(8,128)(2,1)S(1)} %get-tuple-element.46), channel_id=1, source_target_pairs={{0,5},{1,4},{2,7},{3,6},{4,1},{5,0},{6,3},{7,2},{8,13},{9,12},{10,... | collective-permute-start | bytes 196616 | tf_op jit(solution)/shard_map/ppermute | solution.py:752
  23.9 4.6 %collective-permute-start.3 = (bf16[128,256]{1,0:T(8,128)(2,1)S(1)}, bf16[128,256]{1,0:T(8,128)(2,1)S(1)}, u32[]{:S(2)}, u32[]{:S(2)}) collective-permute-start(bf16[128,256]{1,0:T(8,128)(2,1)S(1)} %get-tuple-element.47), channel_id=1, source_target_pairs={{0,7},{1,6},{2,5},{3,4},{4,3},{5,2},{6,1},{7,0},{8,15},{9,14},{10,... | collective-permute-start | bytes 196616 | tf_op jit(solution)/shard_map/ppermute | solution.py:752
  28.6 4.5 %collective-permute-start.4 = (bf16[64,256]{1,0:T(8,128)(2,1)S(1)}, bf16[64,256]{1,0:T(8,128)(2,1)S(1)}, u32[]{:S(2)}, u32[]{:S(2)}) collective-permute-start(bf16[64,256]{1,0:T(8,128)(2,1)S(1)} %get-tuple-element.49), channel_id=1, source_target_pairs={{0,8},{8,0},{16,24},{24,16},{1,9},{9,1},{17,25},{25,17},{2,10},{10... | collective-permute-start | bytes 98312 | tf_op jit(solution)/shard_map/ppermute | solution.py:756
  28.7 5.1 %collective-permute-start.5 = (bf16[64,256]{1,0:T(8,128)(2,1)S(1)}, bf16[64,256]{1,0:T(8,128)(2,1)S(1)}, u32[]{:S(2)}, u32[]{:S(2)}) collective-permute-start(bf16[64,256]{1,0:T(8,128)(2,1)S(1)} %get-tuple-element.49), channel_id=1, source_target_pairs={{0,16},{8,24},{16,0},{24,8},{1,17},{9,25},{17,1},{25,9},{2,18},{10... | collective-permute-start | bytes 98312 | tf_op jit(solution)/shard_map/ppermute | solution.py:756
  29.7 5.7 %collective-permute-start.6 = (bf16[64,256]{1,0:T(8,128)(2,1)S(1)}, bf16[64,256]{1,0:T(8,128)(2,1)S(1)}, u32[]{:S(2)}, u32[]{:S(2)}) collective-permute-start(bf16[64,256]{1,0:T(8,128)(2,1)S(1)} %get-tuple-element.49), channel_id=1, source_target_pairs={{0,24},{8,16},{16,8},{24,0},{1,25},{9,17},{17,9},{25,1},{2,26},{10... | collective-permute-start | bytes 98312 | tf_op jit(solution)/shard_map/ppermute | solution.py:756
  35.4 0.7 %copy-start.5 = (s32[4,1]{0,1:T(1,128)S(1)}, s32[4,1]{0,1:T(1,128)}, u32[]{:S(2)}) copy-start(s32[4,1]{0,1:T(1,128)} %param.10) | copy-start | bytes 52
  35.6 4.5 %copy-start.2 = (bf16[2048,32]{0,1:T(8,128)(2,1)S(1)}, bf16[2048,32]{0,1:T(8,128)(2,1)}, u32[]{:S(2)}) copy-start(bf16[2048,32]{0,1:T(8,128)(2,1)} %param.15) | copy-start | bytes 393220
  35.6 1.3 %collective-permute-start.7 = (f32[4,32,128]{2,1,0:T(8,128)S(1)}, f32[4,32,128]{2,1,0:T(8,128)S(1)}, u32[]{:S(2)}, u32[]{:S(2)}) collective-permute-start(f32[4,32,128]{2,1,0:T(8,128)S(1)} %get-tuple-element.51), channel_id=1, source_target_pairs={{0,1},{1,0},{2,3},{3,2},{4,5},{5,4},{6,7},{7,6},{8,9},{9,8},{10,11... | collective-permute-start | bytes 196616 | tf_op jit(solution)/shard_map/ppermute | solution.py:752
  36.9 4.4 %collective-permute-start.8 = (f32[32,128]{1,0:T(8,128)S(1)}, f32[32,128]{1,0:T(8,128)S(1)}, u32[]{:S(2)}, u32[]{:S(2)}) collective-permute-start(f32[32,128]{1,0:T(8,128)S(1)} %get-tuple-element.53), channel_id=1, source_target_pairs={{0,3},{1,2},{2,1},{3,0},{4,7},{5,6},{6,5},{7,4},{8,11},{9,10},{10,... | collective-permute-start | bytes 49160 | tf_op jit(solution)/shard_map/ppermute | solution.py:752
  37.9 3.4 %collective-permute-start.9 = (f32[32,128]{1,0:T(8,128)S(1)}, f32[32,128]{1,0:T(8,128)S(1)}, u32[]{:S(2)}, u32[]{:S(2)}) collective-permute-start(f32[32,128]{1,0:T(8,128)S(1)} %get-tuple-element.54), channel_id=1, source_target_pairs={{0,5},{1,4},{2,7},{3,6},{4,1},{5,0},{6,3},{7,2},{8,13},{9,12},{10,... | collective-permute-start | bytes 49160 | tf_op jit(solution)/shard_map/ppermute | solution.py:752
  38.8 4.1 %collective-permute-start.10 = (f32[32,128]{1,0:T(8,128)S(1)}, f32[32,128]{1,0:T(8,128)S(1)}, u32[]{:S(2)}, u32[]{:S(2)}) collective-permute-start(f32[32,128]{1,0:T(8,128)S(1)} %get-tuple-element.55), channel_id=1, source_target_pairs={{0,7},{1,6},{2,5},{3,4},{4,3},{5,2},{6,1},{7,0},{8,15},{9,14},{10,... | collective-permute-start | bytes 49160 | tf_op jit(solution)/shard_map/ppermute | solution.py:752

commit v5 on v4

--- a/solution.py
+++ b/solution.py
@@ -20,6 +20,7 @@
 VMEM = pltpu.VMEM
 PAIR_TYPE = BF16
 CROSSED = 1
+FLIPPED = 1
 
 
 def spread(block, axis, owner):
@@ -137,6 +138,14 @@
     return 2 * step + CROSSED * min(step, 1)
 
 
+def flip(row):
+    return row & FLIPPED
+
+
+def owned_block():
+    return lax.axis_index("col") ^ flip(lax.axis_index("row"))
+
+
 def nt(first, second):
     return lax.dot_general(first, second, (((1,), (1,)), ((), ())), preferred_element_type=F32)
 
@@ -185,30 +194,35 @@
     return pl.CostEstimate(flops=flops, bytes_accessed=bytes_accessed, transcendentals=0)
 
 
-def solve_step(block, my_col, right_ref, inverse, out_ref, step, copy=None):
+def solve_step(block, my_col, right_ref, inverse, out_ref, step, copy=None, spare=None):
     @pl.when(block >= my_col)
     def _():
         if copy is not None:
             copy.wait()
-        out_ref[step] = nt(right_ref[...], inverse[step]).astype(out_ref.dtype)
+        value = nt(right_ref[...], inverse[step])
+        out_ref[step] = value.astype(out_ref.dtype)
+        if spare is not None and step == 0:
+            out_ref[spare] = (value - out_ref[step].astype(F32)).astype(out_ref.dtype)
 
     @pl.when(block < my_col)
     def _():
         out_ref[step] = jnp.zeros(out_ref.shape[1:], out_ref.dtype)
+        if spare is not None and step == 0:
+            out_ref[spare] = jnp.zeros(out_ref.shape[1:], out_ref.dtype)
 
 
 def solve_odd_kernel(
     right_hbm, inverse_hbm, out_ref, right_ref, even_ref, inverse_ref, odd_sems, even_sems
 ):
-    parts = out_ref.shape[0]
+    parts = inverse_ref.shape[0]
     piece = right_ref.shape[1]
-    my_col = lax.axis_index("col")
+    my_col, owned = lax.axis_index("col"), owned_block()
     right_copy = pltpu.make_async_copy(right_hbm, right_ref, odd_sems.at[parts])
     right_copy.start()
     copies = []
     for odd, target, sems in ((1, inverse_ref, odd_sems), (0, even_ref, even_sems)):
         for step in range(parts):
-            block = my_col ^ (partner(step) ^ odd)
+            block = owned ^ (partner(step) ^ odd)
             rows = pl.ds(pl.multiple_of(block * piece, piece), piece)
             copy = pltpu.make_async_copy(inverse_hbm.at[rows], target.at[step], sems.at[step])
             pl.when(block >= my_col)(copy.start)
@@ -216,7 +230,7 @@
     right_copy.wait()
     for step in range(parts):
         block, copy = copies[step]
-        solve_step(block, my_col, right_ref, inverse_ref, out_ref, step, copy)
+        solve_step(block, my_col, right_ref, inverse_ref, out_ref, step, copy, parts)
     for block, copy in copies[parts:]:
         pl.when(block >= my_col)(copy.wait)
 
@@ -228,7 +242,7 @@
         in_specs=[pl.BlockSpec(memory_space=pltpu.HBM)] * 2,
         out_specs=in_vmem(3),
         out_shape=[
-            jax.ShapeDtypeStruct((parts, lines, piece), PAIR_TYPE),
+            jax.ShapeDtypeStruct((parts + 1, lines, piece), PAIR_TYPE),
             jax.ShapeDtypeStruct((lines, piece), BF16),
             jax.ShapeDtypeStruct((parts, piece, piece), BF16),
         ],
@@ -249,7 +263,7 @@
 def solve_even_kernel(right_ref, even_ref, out_ref):
     my_col = lax.axis_index("col")
     for step in range(out_ref.shape[0]):
-        solve_step(my_col ^ partner(step), my_col, right_ref, even_ref, out_ref, step)
+        solve_step(owned_block() ^ partner(step), my_col, right_ref, even_ref, out_ref, step)
 
 
 def solve_even(right, even):
@@ -270,7 +284,10 @@
 
 
 def pair_add_kernel(mine_ref, other_ref, keep_ref, *send_refs):
-    keep_ref[...] = mine_ref[0] + other_ref[0].astype(F32)
+    total = mine_ref[0] + other_ref[0].astype(F32)
+    if other_ref.shape[0] > mine_ref.shape[0]:
+        total = total + other_ref[mine_ref.shape[0]].astype(F32)
+    keep_ref[...] = total
     for step, ref in enumerate(send_refs):
         ref[...] = (mine_ref[step + 1] + other_ref[step + 1].astype(F32)).astype(ref.dtype)
 
@@ -295,9 +312,9 @@
     for ref in others:
         total = total + ref[...].astype(F32)
     keep = jnp.concatenate([mask_ref[...]] * (total.shape[1] // LANES), axis=1)
-    rounded = jnp.where(keep > 0.0, total, 0.0).astype(BF16)
-    solved_ref[...] = rounded
-    head_ref[...] = rounded[:head]
+    halves = wide(jnp.where(keep > 0.0, total, 0.0))
+    solved_ref[...] = halves
+    head_ref[...] = halves[:head]
 
 
 def gather_add(first, mask, others, head):
@@ -306,7 +323,7 @@
         in_specs=in_vmem(2 + len(others)),
         out_specs=in_vmem(2),
         out_shape=[
-            jax.ShapeDtypeStruct(first.shape, BF16),
+            jax.ShapeDtypeStruct((2 * first.shape[0], first.shape[1]), BF16),
             jax.ShapeDtypeStruct((head, first.shape[1]), BF16),
         ],
         name="gather_add",
@@ -386,13 +403,15 @@
         given = (relative & 1) ^ (jnp.minimum(step, 1) * CROSSED)
         stage[given * half + step] = value
     piece = own_ref.shape[1]
-    own = own_ref[...]
-    odd_ref[...] = nt(stage[half:].reshape(half * width, piece), own).reshape(odd_ref.shape)
-    even_ref[...] = nt(stage[:half].reshape(half * width, piece), own).reshape(even_ref.shape)
+    lines = odd_ref.shape[2]
+    high, low = own_ref[:lines], own_ref[lines:]
+    for ref, part in ((odd_ref, stage[half:]), (even_ref, stage[:half])):
+        part = part.reshape(half * width, piece)
+        ref[...] = (nt(part, high) + nt(part, low)).reshape(ref.shape)
 
 
 def core_parts(own, others, rows_total, cols_total, width):
-    lines, piece = own.shape
+    lines, piece = own.shape[0] // 2, own.shape[1]
     half = cols_total // 2
     shape = jax.ShapeDtypeStruct((half, width, lines), F32)
     return pl.pallas_call(
@@ -751,15 +770,20 @@
     def swap(block, step):
         return lax.ppermute(block, "col", [(i, i ^ step) for i in range(cols_total)])
 
-    def turn(block, shift):
-        pairs = [(i, i ^ shift) for i in range(rows_total)]
-        return lax.ppermute(block, "row", pairs)
+    def turn(block, shift, owners=False):
+        pairs = []
+        for row in range(rows_total):
+            other = row ^ shift
+            change = flip(row) ^ flip(other) if owners else 0
+            for col in range(cols_total):
+                pairs.append((row * cols_total + col, other * cols_total + (col ^ change)))
+        return lax.ppermute(block, ("row", "col"), pairs)
 
     def across(blocks):
         return [swap(block, partner(step + 1)) for step, block in enumerate(blocks)]
 
-    def along(block):
-        return [turn(block, shift) for shift in range(1, rows_total)]
+    def along(block, owners=False):
+        return [turn(block, shift, owners) for shift in range(1, rows_total)]
 
     panel_keep, _ = line_mask(panel.shape[0], panel_ranks)
     slab_line, slab_lane = line_mask(panel.shape[0], slab_ranks.reshape(-1))
@@ -772,7 +796,7 @@
     received = across(sends)
     panel_others = along(panel[:head])
     solved, solved_head = gather_add(kept, panel_keep, received, head)
-    solved_others = along(solved_head)
+    solved_others = along(solved_head, True)
     own_message, *sends = messages(panel, panel_others, rows_total, cols_total, width)
     even_panel, odd_panel = bundle([own_message] + across(sends), width)
     odd_panel = swap(odd_panel, 1)

time: 46.2 us -> 45.9 us (level)
    ppermute x6, starting transfers between devices: 9.83 us -> 9.27 us  [turn(): return lax.ppermute(block, ('row', 'col'), pairs)]
    ppermute x12, starting transfers between devices: 9.6 us -> 10.2 us  [swap(): lax.ppermute(block, 'col', [(i, i ^ step) for i in range(cols_total)])]
where the time goes in v5:
time: 45.9 us; the launch traced here: 45.8 us
  starting transfers between devices  19.4 us (42%)
  waiting for transfers between devices  17.6 us (38%)
  Pallas kernels  7.48 us (16%)
  between operations  0.8 us (2%)
    ppermute x12, starting transfers between devices, swap(): lax.ppermute(block, 'col', [(i, i ^ step) for i in range(cols_total)])  10.2 us
    ppermute x12, waiting for transfers between devices, swap(): lax.ppermute(block, 'col', [(i, i ^ step) for i in range(cols_total)])  9.35 us
    ppermute x6, starting transfers between devices, turn(): return lax.ppermute(block, ('row', 'col'), pairs)  9.27 us
    ppermute x6, waiting for transfers between devices, turn(): return lax.ppermute(block, ('row', 'col'), pairs)  8.23 us
    pallas_call x1, Pallas kernels, finish(): pl.pallas_call(functools.partial(finish_kernel, half, width, rows_total),...  3.19 us
    pallas_call x1, Pallas kernels, solve_odd(): pl.pallas_call(solve_odd_kernel, in_specs=[pl.BlockSpec(memory_space=pltp...  1.86 us
  transfers between devices with their start and end apart: 18, of which 11 were waited for; matrix products, arithmetic and copies ran while one was open for 1% of the time, Pallas kernels for 5%

profile of v5, /device:TPU:0, one launch (start us, length us, event | category | flops | bytes accessed | tf_op | source)
XLA Modules:
  0.0 45.8 jit_solution(16007769773446960523)
XLA Ops:
  0.6 0.0 copy-start.3
  0.6 1.9 %solve_odd.1 = (bf16[5,128,256]{2,1,0:T(8,128)(2,1)S(1)}, bf16[128,256]{1,0:T(8,128)(2,1)S(1)}, bf16[4,256,256]{2,1,0:T(8,128)(2,1)S(1)}) custom-call(bf16[128,256]{1,0:T(8,128)(2,1)} %bitcast.35, bf16[2048,256]{1,0:T(8,128)(2,1)} %inverse_hbm.1), custom_call_target="tpu_custom_call" | custom-call | flops 67108864 | bytes 1572864 | tf_op jit(solution)/shard_map/solve_odd/pallas_call | solution.py:240
  2.5 0.4 collective-permute-start
  2.9 0.0 copy-done.3
  2.9 2.8 %collective-permute-start.11 = (bf16[64,256]{1,0:T(8,128)(2,1)S(1)}, bf16[64,256]{1,0:T(8,128)(2,1)S(1)}, u32[]{:S(2)}, u32[]{:S(2)}) collective-permute-start(bf16[64,256]{1,0:T(8,128)(2,1)S(1)} %bitcast.36), channel_id=1, source_target_pairs={{0,8},{1,9},{2,10},{3,11},{4,12},{5,13},{6,14},{7,15},{8,0},{9,1},... | collective-permute-start | bytes 98312 | tf_op jit(solution)/shard_map/ppermute | solution.py:780
  5.7 2.6 %collective-permute-start.12 = (bf16[64,256]{1,0:T(8,128)(2,1)S(1)}, bf16[64,256]{1,0:T(8,128)(2,1)S(1)}, u32[]{:S(2)}, u32[]{:S(2)}) collective-permute-start(bf16[64,256]{1,0:T(8,128)(2,1)S(1)} %bitcast.37), channel_id=1, source_target_pairs={{0,16},{1,17},{2,18},{3,19},{4,20},{5,21},{6,22},{7,23},{8,24},{9,... | collective-permute-start | bytes 98312 | tf_op jit(solution)/shard_map/ppermute | solution.py:780
  8.3 0.0 collective-permute-start.13
  8.3 0.0 collective-permute-done.11.refs_0_
  8.3 2.8 %collective-permute-done.12.refs_1_ = bf16[64,256]{1,0:T(8,128)(2,1)S(1)} collective-permute-done((bf16[64,256]{1,0:T(8,128)(2,1)S(1)}, bf16[64,256]{1,0:T(8,128)(2,1)S(1)}, u32[]{:S(2)}, u32[]{:S(2)}) %collective-permute-start.12) | collective-permute-done | bytes 32800 | tf_op jit(solution)/shard_map/ppermute | solution.py:780
  11.1 2.9 %collective-permute-done.13.refs_2_ = bf16[64,256]{1,0:T(8,128)(2,1)S(1)} collective-permute-done((bf16[64,256]{1,0:T(8,128)(2,1)S(1)}, bf16[64,256]{1,0:T(8,128)(2,1)S(1)}, u32[]{:S(2)}, u32[]{:S(2)}) %collective-permute-start.13) | collective-permute-done | bytes 32800 | tf_op jit(solution)/shard_map/ppermute | solution.py:780
  14.1 0.1 collective-permute-start.14
  14.2 2.1 %collective-permute-start.15 = (bf16[192,256]{1,0:T(8,128)(2,1)S(1)}, bf16[192,256]{1,0:T(8,128)(2,1)S(1)}, u32[]{:S(2)}, u32[]{:S(2)}) collective-permute-start(bf16[192,256]{1,0:T(8,128)(2,1)S(1)} %get-tuple-element.58), channel_id=1, source_target_pairs={{0,5},{1,4},{2,7},{3,6},{4,1},{5,0},{6,3},{7,2},{8,13},{9,12},{10,... | collective-permute-start | bytes 294920 | tf_op jit(solution)/shard_map/ppermute | solution.py:771
  16.3 0.4 collective-permute-start.16
  16.7 0.8 %solve_even.1.mine_ref = f32[4,128,256]{2,1,0:T(8,128)S(1)} custom-call(bf16[128,256]{1,0:T(8,128)(2,1)S(1)} %get-tuple-element.41.right_ref, bf16[4,256,256]{2,1,0:T(8,128)(2,1)S(1)} %get-tuple-element.42.even_ref), custom_call_target="tpu_custom_call" | custom-call | flops 67108864 | bytes 1048576 | tf_op jit(solution)/shard_map/solve_even/pallas_call | solution.py:272
  17.5 1.6 %collective-permute-done.14.refs_1_ = bf16[192,256]{1,0:T(8,128)(2,1)S(1)} collective-permute-done((bf16[192,256]{1,0:T(8,128)(2,1)S(1)}, bf16[192,256]{1,0:T(8,128)(2,1)S(1)}, u32[]{:S(2)}, u32[]{:S(2)}) %collective-permute-start.14) | collective-permute-done | bytes 98336 | tf_op jit(solution)/shard_map/ppermute | solution.py:771
  19.1 0.0 collective-permute-done.15.refs_2_
  19.1 2.8 %collective-permute-done.16.refs_3_ = bf16[192,256]{1,0:T(8,128)(2,1)S(1)} collective-permute-done((bf16[192,256]{1,0:T(8,128)(2,1)S(1)}, bf16[192,256]{1,0:T(8,128)(2,1)S(1)}, u32[]{:S(2)}, u32[]{:S(2)}) %collective-permute-start.16) | collective-permute-done | bytes 98336 | tf_op jit(solution)/shard_map/ppermute | solution.py:771
  21.9 0.1 collective-permute-start.17
  22.0 0.0 collective-permute-done.other_ref
  22.0 0.0 copy-start.4
  22.0 0.0 copy-start.1
  22.0 0.1 pair_add.2
  22.1 0.0 copy-start
  22.1 1.2 %collective-permute-start.1 = (bf16[128,256]{1,0:T(8,128)(2,1)S(1)}, bf16[128,256]{1,0:T(8,128)(2,1)S(1)}, u32[]{:S(2)}, u32[]{:S(2)}) collective-permute-start(bf16[128,256]{1,0:T(8,128)(2,1)S(1)} %get-tuple-element.45), channel_id=1, source_target_pairs={{0,3},{1,2},{2,1},{3,0},{4,7},{5,6},{6,5},{7,4},{8,11},{9,10},{10,... | collective-permute-start | bytes 196616 | tf_op jit(solution)/shard_map/ppermute | solution.py:771
  23.3 0.6 %collective-permute-start.2 = (bf16[128,256]{1,0:T(8,128)(2,1)S(1)}, bf16[128,256]{1,0:T(8,128)(2,1)S(1)}, u32[]{:S(2)}, u32[]{:S(2)}) collective-permute-start(bf16[128,256]{1,0:T(8,128)(2,1)S(1)} %get-tuple-element.46), channel_id=1, source_target_pairs={{0,5},{1,4},{2,7},{3,6},{4,1},{5,0},{6,3},{7,2},{8,13},{9,12},{10,... | collective-permute-start | bytes 196616 | tf_op jit(solution)/shard_map/ppermute | solution.py:771
  23.9 1.6 %collective-permute-start.3 = (bf16[128,256]{1,0:T(8,128)(2,1)S(1)}, bf16[128,256]{1,0:T(8,128)(2,1)S(1)}, u32[]{:S(2)}, u32[]{:S(2)}) collective-permute-start(bf16[128,256]{1,0:T(8,128)(2,1)S(1)} %get-tuple-element.47), channel_id=1, source_target_pairs={{0,7},{1,6},{2,5},{3,4},{4,3},{5,2},{6,1},{7,0},{8,15},{9,14},{10,... | collective-permute-start | bytes 196616 | tf_op jit(solution)/shard_map/ppermute | solution.py:771
  25.4 0.0 copy-done.4
  25.4 0.1 fusion
  25.5 0.1 reshape.78
  25.6 0.3 collective-permute-done.1.refs_0_
  25.9 1.5 %collective-permute-done.2.refs_1_ = bf16[128,256]{1,0:T(8,128)(2,1)S(1)} collective-permute-done((bf16[128,256]{1,0:T(8,128)(2,1)S(1)}, bf16[128,256]{1,0:T(8,128)(2,1)S(1)}, u32[]{:S(2)}, u32[]{:S(2)}) %collective-permute-start.2) | collective-permute-done | bytes 65568 | tf_op jit(solution)/shard_map/ppermute | solution.py:771
  27.5 1.0 %collective-permute-done.3.refs_2_ = bf16[128,256]{1,0:T(8,128)(2,1)S(1)} collective-permute-done((bf16[128,256]{1,0:T(8,128)(2,1)S(1)}, bf16[128,256]{1,0:T(8,128)(2,1)S(1)}, u32[]{:S(2)}, u32[]{:S(2)}) %collective-permute-start.3) | collective-permute-done | bytes 65568 | tf_op jit(solution)/shard_map/ppermute | solution.py:771
  28.5 0.1 broadcast_in_dim.6.mask_ref
  28.6 0.1 gather_add.1
  28.6 0.1 collective-permute-start.4
  28.7 1.0 %collective-permute-start.5 = (bf16[64,256]{1,0:T(8,128)(2,1)S(1)}, bf16[64,256]{1,0:T(8,128)(2,1)S(1)}, u32[]{:S(2)}, u32[]{:S(2)}) collective-permute-start(bf16[64,256]{1,0:T(8,128)(2,1)S(1)} %get-tuple-element.49), channel_id=1, source_target_pairs={{0,16},{1,17},{2,18},{3,19},{4,20},{5,21},{6,22},{7,23},{8,24},{9,... | collective-permute-start | bytes 98312 | tf_op jit(solution)/shard_map/ppermute | solution.py:780
  29.8 2.8 %collective-permute-start.6 = (bf16[64,256]{1,0:T(8,128)(2,1)S(1)}, bf16[64,256]{1,0:T(8,128)(2,1)S(1)}, u32[]{:S(2)}, u32[]{:S(2)}) collective-permute-start(bf16[64,256]{1,0:T(8,128)(2,1)S(1)} %get-tuple-element.49), channel_id=1, source_target_pairs={{0,25},{1,24},{2,27},{3,26},{4,29},{5,28},{6,31},{7,30},{8,17},{9,... | collective-permute-start | bytes 98312 | tf_op jit(solution)/shard_map/ppermute | solution.py:780
  32.5 0.0 collective-permute-done.4.refs_0_
  32.5 1.8 %collective-permute-done.5.refs_1_ = bf16[64,256]{1,0:T(8,128)(2,1)S(1)} collective-permute-done((bf16[64,256]{1,0:T(8,128)(2,1)S(1)}, bf16[64,256]{1,0:T(8,128)(2,1)S(1)}, u32[]{:S(2)}, u32[]{:S(2)}) %collective-permute-start.5) | collective-permute-done | bytes 32800 | tf_op jit(solution)/shard_map/ppermute | solution.py:780
  34.3 0.8 %collective-permute-done.6.refs_2_ = bf16[64,256]{1,0:T(8,128)(2,1)S(1)} collective-permute-done((bf16[64,256]{1,0:T(8,128)(2,1)S(1)}, bf16[64,256]{1,0:T(8,128)(2,1)S(1)}, u32[]{:S(2)}, u32[]{:S(2)}) %collective-permute-start.6) | collective-permute-done | bytes 32800 | tf_op jit(solution)/shard_map/ppermute | solution.py:780
  35.1 0.0 copy-start.5
  35.1 0.2 core_parts.1
  35.3 0.0 copy-start.2
  35.3 0.4 collective-permute-start.7
  35.7 0.0 copy-done.5
  35.7 0.1 fusion.1
  35.8 0.1 reshape.79
  35.9 0.7 %collective-permute-done.7.other_ref = f32[4,32,128]{2,1,0:T(8,128)S(1)} collective-permute-done((f32[4,32,128]{2,1,0:T(8,128)S(1)}, f32[4,32,128]{2,1,0:T(8,128)S(1)}, u32[]{:S(2)}, u32[]{:S(2)}) %collective-permute-start.7) | collective-permute-done | bytes 65568 | tf_op jit(solution)/shard_map/ppermute | solution.py:771
  36.6 1.2 %collective-permute-start.8 = (f32[32,128]{1,0:T(8,128)S(1)}, f32[32,128]{1,0:T(8,128)S(1)}, u32[]{:S(2)}, u32[]{:S(2)}) collective-permute-start(f32[32,128]{1,0:T(8,128)S(1)} %get-tuple-element.53), channel_id=1, source_target_pairs={{0,3},{1,2},{2,1},{3,0},{4,7},{5,6},{6,5},{7,4},{8,11},{9,10},{10,... | collective-permute-start | bytes 49160 | tf_op jit(solution)/shard_map/ppermute | solution.py:771
  37.8 0.7 %collective-permute-start.9 = (f32[32,128]{1,0:T(8,128)S(1)}, f32[32,128]{1,0:T(8,128)S(1)}, u32[]{:S(2)}, u32[]{:S(2)}) collective-permute-start(f32[32,128]{1,0:T(8,128)S(1)} %get-tuple-element.54), channel_id=1, source_target_pairs={{0,5},{1,4},{2,7},{3,6},{4,1},{5,0},{6,3},{7,2},{8,13},{9,12},{10,... | collective-permute-start | bytes 49160 | tf_op jit(solution)/shard_map/ppermute | solution.py:771
  38.5 1.4 %collective-permute-start.10 = (f32[32,128]{1,0:T(8,128)S(1)}, f32[32,128]{1,0:T(8,128)S(1)}, u32[]{:S(2)}, u32[]{:S(2)}) collective-permute-start(f32[32,128]{1,0:T(8,128)S(1)} %get-tuple-element.55), channel_id=1, source_target_pairs={{0,7},{1,6},{2,5},{3,4},{4,3},{5,2},{6,1},{7,0},{8,15},{9,14},{10,... | collective-permute-start | bytes 49160 | tf_op jit(solution)/shard_map/ppermute | solution.py:771
  39.9 0.1 broadcast_in_dim.7.refs_4_
  40.0 0.0 copy-done.1
  40.0 0.0 copy-done
  40.0 0.0 copy-done.2
  40.0 0.8 %early_grams.1 = (bf16[128,128]{1,0:T(8,128)(2,1)S(1)}, bf16[128,128]{1,0:T(8,128)(2,1)S(1)}, f32[128,128]{1,0:T(8,128)S(1)}, f32[32,128]{1,0:T(8,128)S(1)}, f32...) custom-call(bf16[128,2048]{1,0:T(8,128)(2,1)S(1)} %bitcast.25, ...), custom_call_target="tpu_custom_call" | custom-call | flops 335544320 | bytes 1000000 | tf_op jit(solution)/shard_map/early_grams/pallas_call | solution.py:493
  40.8 0.0 collective-permute-done.17.refs_3_.refs_18_
  40.8 0.4 late_grams.1
  41.2 0.0 collective-permute-done.8.refs_1_
  41.2 0.0 collective-permute-done.9.refs_2_
  41.2 1.3 %collective-permute-done.10.refs_3_ = f32[32,128]{1,0:T(8,128)S(1)} collective-permute-done((f32[32,128]{1,0:T(8,128)S(1)}, f32[32,128]{1,0:T(8,128)S(1)}, u32[]{:S(2)}, u32[]{:S(2)}) %collective-permute-start.10) | collective-permute-done | bytes 16416 | tf_op jit(solution)/shard_map/ppermute | solution.py:771
  42.6 3.2 %finish.1 = (bf16[128,2048]{1,0:T(8,128)(2,1)}, bf16[128,2048]{1,0:T(8,128)(2,1)}) custom-call(f32[32,128]{1,0:T(8,128)S(1)} %get-tuple-element.52.refs_0_, f32[32,128]{1,0:T(8,128)S(1)} %collective-permute-done.8.refs_1_, f32[32,128]{1,0:T(8,128)S(1)} %collective-permute-done.9.refs_2_, f32[32,128]{1,0:T(8,128)S(1)} %collective-permute-done.10.refs_3_, ...), custom_call_target="tpu_custom_call" | custom-call | flops 1000000000 | bytes 5000000 | tf_op jit(solution)/shard_map/finish/pallas_call | solution.py:738
  (5 shorter events, 0.1 us)
Async XLA Ops:
  0.6 2.3 %copy-start.3 = (bf16[4,256,32]{1,2,0:T(8,128)(2,1)S(1)}, bf16[4,256,32]{1,2,0:T(8,128)(2,1)}, u32[]{:S(2)}) copy-start(bf16[4,256,32]{1,2,0:T(8,128)(2,1)} %param.11) | copy-start | bytes 196612
  2.5 19.5 %collective-permute-start = (bf16[5,128,256]{2,1,0:T(8,128)(2,1)S(1)}, bf16[5,128,256]{2,1,0:T(8,128)(2,1)S(1)}, u32[]{:S(2)}, u32[]{:S(2)}) collective-permute-start(bf16[5,128,256]{2,1,0:T(8,128)(2,1)S(1)} %get-tuple-element.43), channel_id=1, source_target_pairs={{0,1},{1,0},{2,3},{3,2},{4,5},{5,4},{6,7},{7,6},{8,9},{9,8},{10,11... | collective-permute-start | bytes 983048 | tf_op jit(solution)/shard_map/ppermute | solution.py:771
  2.9 5.4 %collective-permute-start.11 = (bf16[64,256]{1,0:T(8,128)(2,1)S(1)}, bf16[64,256]{1,0:T(8,128)(2,1)S(1)}, u32[]{:S(2)}, u32[]{:S(2)}) collective-permute-start(bf16[64,256]{1,0:T(8,128)(2,1)S(1)} %bitcast.36), channel_id=1, source_target_pairs={{0,8},{1,9},{2,10},{3,11},{4,12},{5,13},{6,14},{7,15},{8,0},{9,1},... | collective-permute-start | bytes 98312 | tf_op jit(solution)/shard_map/ppermute | solution.py:780
  5.7 5.4 %collective-permute-start.12 = (bf16[64,256]{1,0:T(8,128)(2,1)S(1)}, bf16[64,256]{1,0:T(8,128)(2,1)S(1)}, u32[]{:S(2)}, u32[]{:S(2)}) collective-permute-start(bf16[64,256]{1,0:T(8,128)(2,1)S(1)} %bitcast.37), channel_id=1, source_target_pairs={{0,16},{1,17},{2,18},{3,19},{4,20},{5,21},{6,22},{7,23},{8,24},{9,... | collective-permute-start | bytes 98312 | tf_op jit(solution)/shard_map/ppermute | solution.py:780
  8.3 5.7 %collective-permute-start.13 = (bf16[64,256]{1,0:T(8,128)(2,1)S(1)}, bf16[64,256]{1,0:T(8,128)(2,1)S(1)}, u32[]{:S(2)}, u32[]{:S(2)}) collective-permute-start(bf16[64,256]{1,0:T(8,128)(2,1)S(1)} %bitcast.38), channel_id=1, source_target_pairs={{0,24},{1,25},{2,26},{3,27},{4,28},{5,29},{6,30},{7,31},{8,16},{9,... | collective-permute-start | bytes 98312 | tf_op jit(solution)/shard_map/ppermute | solution.py:780
  14.1 5.0 %collective-permute-start.14 = (bf16[192,256]{1,0:T(8,128)(2,1)S(1)}, bf16[192,256]{1,0:T(8,128)(2,1)S(1)}, u32[]{:S(2)}, u32[]{:S(2)}) collective-permute-start(bf16[192,256]{1,0:T(8,128)(2,1)S(1)} %get-tuple-element.57), channel_id=1, source_target_pairs={{0,3},{1,2},{2,1},{3,0},{4,7},{5,6},{6,5},{7,4},{8,11},{9,10},{10,... | collective-permute-start | bytes 294920 | tf_op jit(solution)/shard_map/ppermute | solution.py:771
  14.2 4.9 %collective-permute-start.15 = (bf16[192,256]{1,0:T(8,128)(2,1)S(1)}, bf16[192,256]{1,0:T(8,128)(2,1)S(1)}, u32[]{:S(2)}, u32[]{:S(2)}) collective-permute-start(bf16[192,256]{1,0:T(8,128)(2,1)S(1)} %get-tuple-element.58), channel_id=1, source_target_pairs={{0,5},{1,4},{2,7},{3,6},{4,1},{5,0},{6,3},{7,2},{8,13},{9,12},{10,... | collective-permute-start | bytes 294920 | tf_op jit(solution)/shard_map/ppermute | solution.py:771
  16.3 5.6 %collective-permute-start.16 = (bf16[192,256]{1,0:T(8,128)(2,1)S(1)}, bf16[192,256]{1,0:T(8,128)(2,1)S(1)}, u32[]{:S(2)}, u32[]{:S(2)}) collective-permute-start(bf16[192,256]{1,0:T(8,128)(2,1)S(1)} %get-tuple-element.59), channel_id=1, source_target_pairs={{0,7},{1,6},{2,5},{3,4},{4,3},{5,2},{6,1},{7,0},{8,15},{9,14},{10,... | collective-permute-start | bytes 294920 | tf_op jit(solution)/shard_map/ppermute | solution.py:771
  21.9 18.9 %collective-permute-start.17 = (bf16[4,160,256]{2,1,0:T(8,128)(2,1)S(1)}, bf16[4,160,256]{2,1,0:T(8,128)(2,1)S(1)}, u32[]{:S(2)}, u32[]{:S(2)}) collective-permute-start(bf16[4,160,256]{2,1,0:T(8,128)(2,1)S(1)} %get-tuple-element.65), channel_id=1, source_target_pairs={{0,1},{1,0},{2,3},{3,2},{4,5},{5,4},{6,7},{7,6},{8,9},{9,8},{10,11... | collective-permute-start | bytes 983048 | tf_op jit(solution)/shard_map/ppermute | solution.py:771
  22.0 3.4 %copy-start.4 = (s32[4]{0:T(128)S(1)}, s32[4]{0:T(128)}, u32[]{:S(2)}) copy-start(s32[4]{0:T(128)} %param.13) | copy-start | bytes 52
  22.0 17.9 %copy-start.1 = (bf16[4,1,2048,32]{2,3,1,0:T(8,128)(2,1)S(1)}, bf16[4,1,2048,32]{2,3,1,0:T(8,128)(2,1)}, u32[]{:S(2)}) copy-start(bf16[4,1,2048,32]{2,3,1,0:T(8,128)(2,1)} %param.9) | copy-start | bytes 1572868
  22.1 17.9 %copy-start = (bf16[4,1,2048,32]{2,3,1,0:T(8,128)(2,1)S(1)}, bf16[4,1,2048,32]{2,3,1,0:T(8,128)(2,1)}, u32[]{:S(2)}) copy-start(bf16[4,1,2048,32]{2,3,1,0:T(8,128)(2,1)} %param.8) | copy-start | bytes 1572868
  22.1 3.8 %collective-permute-start.1 = (bf16[128,256]{1,0:T(8,128)(2,1)S(1)}, bf16[128,256]{1,0:T(8,128)(2,1)S(1)}, u32[]{:S(2)}, u32[]{:S(2)}) collective-permute-start(bf16[128,256]{1,0:T(8,128)(2,1)S(1)} %get-tuple-element.45), channel_id=1, source_target_pairs={{0,3},{1,2},{2,1},{3,0},{4,7},{5,6},{6,5},{7,4},{8,11},{9,10},{10,... | collective-permute-start | bytes 196616 | tf_op jit(solution)/shard_map/ppermute | solution.py:771
  23.3 4.2 %collective-permute-start.2 = (bf16[128,256]{1,0:T(8,128)(2,1)S(1)}, bf16[128,256]{1,0:T(8,128)(2,1)S(1)}, u32[]{:S(2)}, u32[]{:S(2)}) collective-permute-start(bf16[128,256]{1,0:T(8,128)(2,1)S(1)} %get-tuple-element.46), channel_id=1, source_target_pairs={{0,5},{1,4},{2,7},{3,6},{4,1},{5,0},{6,3},{7,2},{8,13},{9,12},{10,... | collective-permute-start | bytes 196616 | tf_op jit(solution)/shard_map/ppermute | solution.py:771
  23.9 4.6 %collective-permute-start.3 = (bf16[128,256]{1,0:T(8,128)(2,1)S(1)}, bf16[128,256]{1,0:T(8,128)(2,1)S(1)}, u32[]{:S(2)}, u32[]{:S(2)}) collective-permute-start(bf16[128,256]{1,0:T(8,128)(2,1)S(1)} %get-tuple-element.47), channel_id=1, source_target_pairs={{0,7},{1,6},{2,5},{3,4},{4,3},{5,2},{6,1},{7,0},{8,15},{9,14},{10,... | collective-permute-start | bytes 196616 | tf_op jit(solution)/shard_map/ppermute | solution.py:771
  28.6 3.9 %collective-permute-start.4 = (bf16[64,256]{1,0:T(8,128)(2,1)S(1)}, bf16[64,256]{1,0:T(8,128)(2,1)S(1)}, u32[]{:S(2)}, u32[]{:S(2)}) collective-permute-start(bf16[64,256]{1,0:T(8,128)(2,1)S(1)} %get-tuple-element.49), channel_id=1, source_target_pairs={{0,9},{1,8},{2,11},{3,10},{4,13},{5,12},{6,15},{7,14},{8,1},{9,0},... | collective-permute-start | bytes 98312 | tf_op jit(solution)/shard_map/ppermute | solution.py:780
  28.7 5.6 %collective-permute-start.5 = (bf16[64,256]{1,0:T(8,128)(2,1)S(1)}, bf16[64,256]{1,0:T(8,128)(2,1)S(1)}, u32[]{:S(2)}, u32[]{:S(2)}) collective-permute-start(bf16[64,256]{1,0:T(8,128)(2,1)S(1)} %get-tuple-element.49), channel_id=1, source_target_pairs={{0,16},{1,17},{2,18},{3,19},{4,20},{5,21},{6,22},{7,23},{8,24},{9,... | collective-permute-start | bytes 98312 | tf_op jit(solution)/shard_map/ppermute | solution.py:780
  29.8 5.3 %collective-permute-start.6 = (bf16[64,256]{1,0:T(8,128)(2,1)S(1)}, bf16[64,256]{1,0:T(8,128)(2,1)S(1)}, u32[]{:S(2)}, u32[]{:S(2)}) collective-permute-start(bf16[64,256]{1,0:T(8,128)(2,1)S(1)} %get-tuple-element.49), channel_id=1, source_target_pairs={{0,25},{1,24},{2,27},{3,26},{4,29},{5,28},{6,31},{7,30},{8,17},{9,... | collective-permute-start | bytes 98312 | tf_op jit(solution)/shard_map/ppermute | solution.py:780
  35.1 0.7 %copy-start.5 = (s32[4,1]{0,1:T(1,128)S(1)}, s32[4,1]{0,1:T(1,128)}, u32[]{:S(2)}) copy-start(s32[4,1]{0,1:T(1,128)} %param.10) | copy-start | bytes 52
  35.3 4.7 %copy-start.2 = (bf16[2048,32]{0,1:T(8,128)(2,1)S(1)}, bf16[2048,32]{0,1:T(8,128)(2,1)}, u32[]{:S(2)}) copy-start(bf16[2048,32]{0,1:T(8,128)(2,1)} %param.15) | copy-start | bytes 393220
  35.3 1.3 %collective-permute-start.7 = (f32[4,32,128]{2,1,0:T(8,128)S(1)}, f32[4,32,128]{2,1,0:T(8,128)S(1)}, u32[]{:S(2)}, u32[]{:S(2)}) collective-permute-start(f32[4,32,128]{2,1,0:T(8,128)S(1)} %get-tuple-element.51), channel_id=1, source_target_pairs={{0,1},{1,0},{2,3},{3,2},{4,5},{5,4},{6,7},{7,6},{8,9},{9,8},{10,11... | collective-permute-start | bytes 196616 | tf_op jit(solution)/shard_map/ppermute | solution.py:771
  36.6 4.6 %collective-permute-start.8 = (f32[32,128]{1,0:T(8,128)S(1)}, f32[32,128]{1,0:T(8,128)S(1)}, u32[]{:S(2)}, u32[]{:S(2)}) collective-permute-start(f32[32,128]{1,0:T(8,128)S(1)} %get-tuple-element.53), channel_id=1, source_target_pairs={{0,3},{1,2},{2,1},{3,0},{4,7},{5,6},{6,5},{7,4},{8,11},{9,10},{10,... | collective-permute-start | bytes 49160 | tf_op jit(solution)/shard_map/ppermute | solution.py:771
  37.8 3.4 %collective-permute-start.9 = (f32[32,128]{1,0:T(8,128)S(1)}, f32[32,128]{1,0:T(8,128)S(1)}, u32[]{:S(2)}, u32[]{:S(2)}) collective-permute-start(f32[32,128]{1,0:T(8,128)S(1)} %get-tuple-element.54), channel_id=1, source_target_pairs={{0,5},{1,4},{2,7},{3,6},{4,1},{5,0},{6,3},{7,2},{8,13},{9,12},{10,... | collective-permute-start | bytes 49160 | tf_op jit(solution)/shard_map/ppermute | solution.py:771
  38.5 4.1 %collective-permute-start.10 = (f32[32,128]{1,0:T(8,128)S(1)}, f32[32,128]{1,0:T(8,128)S(1)}, u32[]{:S(2)}, u32[]{:S(2)}) collective-permute-start(f32[32,128]{1,0:T(8,128)S(1)} %get-tuple-element.55), channel_id=1, source_target_pairs={{0,7},{1,6},{2,5},{3,4},{4,3},{5,2},{6,1},{7,0},{8,15},{9,14},{10,... | collective-permute-start | bytes 49160 | tf_op jit(solution)/shard_map/ppermute | solution.py:771

commit v6 on v5

--- a/solution.py
+++ b/solution.py
@@ -20,7 +20,6 @@
 VMEM = pltpu.VMEM
 PAIR_TYPE = BF16
 CROSSED = 1
-FLIPPED = 1
 
 
 def spread(block, axis, owner):
@@ -139,7 +138,7 @@
 
 
 def flip(row):
-    return row & FLIPPED
+    return (row ^ (row >> 1)) & 1
 
 
 def owned_block():
@@ -312,9 +311,9 @@
     for ref in others:
         total = total + ref[...].astype(F32)
     keep = jnp.concatenate([mask_ref[...]] * (total.shape[1] // LANES), axis=1)
-    halves = wide(jnp.where(keep > 0.0, total, 0.0))
-    solved_ref[...] = halves
-    head_ref[...] = halves[:head]
+    rounded = jnp.where(keep > 0.0, total, 0.0).astype(BF16)
+    solved_ref[...] = rounded
+    head_ref[...] = rounded[:head]
 
 
 def gather_add(first, mask, others, head):
@@ -323,7 +322,7 @@
         in_specs=in_vmem(2 + len(others)),
         out_specs=in_vmem(2),
         out_shape=[
-            jax.ShapeDtypeStruct((2 * first.shape[0], first.shape[1]), BF16),
+            jax.ShapeDtypeStruct(first.shape, BF16),
             jax.ShapeDtypeStruct((head, first.shape[1]), BF16),
         ],
         name="gather_add",
@@ -403,15 +402,13 @@
         given = (relative & 1) ^ (jnp.minimum(step, 1) * CROSSED)
         stage[given * half + step] = value
     piece = own_ref.shape[1]
-    lines = odd_ref.shape[2]
-    high, low = own_ref[:lines], own_ref[lines:]
-    for ref, part in ((odd_ref, stage[half:]), (even_ref, stage[:half])):
-        part = part.reshape(half * width, piece)
-        ref[...] = (nt(part, high) + nt(part, low)).reshape(ref.shape)
+    own = own_ref[...]
+    odd_ref[...] = nt(stage[half:].reshape(half * width, piece), own).reshape(odd_ref.shape)
+    even_ref[...] = nt(stage[:half].reshape(half * width, piece), own).reshape(even_ref.shape)
 
 
 def core_parts(own, others, rows_total, cols_total, width):
-    lines, piece = own.shape[0] // 2, own.shape[1]
+    lines, piece = own.shape
     half = cols_total // 2
     shape = jax.ShapeDtypeStruct((half, width, lines), F32)
     return pl.pallas_call(

time: 45.9 us -> 46.4 us (1.011)
    ppermute x12, starting transfers between devices: 10.2 us -> 9.6 us  [swap(): lax.ppermute(block, 'col', [(i, i ^ step) for i in range(cols_total)])]
where the time goes in v6:
time: 46.4 us; the launch traced here: 46.2 us
  starting transfers between devices  19.1 us (41%)
  waiting for transfers between devices  18 us (39%)
  Pallas kernels  7.44 us (16%)
  between operations  0.81 us (2%)
  local copies, waits for them, and re-layouts  0.72 us (2%)
    ppermute x12, starting transfers between devices, swap(): lax.ppermute(block, 'col', [(i, i ^ step) for i in range(cols_total)])  9.6 us
    ppermute x6, starting transfers between devices, turn(): return lax.ppermute(block, ('row', 'col'), pairs)  9.55 us
    ppermute x12, waiting for transfers between devices, swap(): lax.ppermute(block, 'col', [(i, i ^ step) for i in range(cols_total)])  9.52 us
    ppermute x6, waiting for transfers between devices, turn(): return lax.ppermute(block, ('row', 'col'), pairs)  8.46 us
    pallas_call x1, Pallas kernels, finish(): pl.pallas_call(functools.partial(finish_kernel, half, width, rows_total),...  3.19 us
    pallas_call x1, Pallas kernels, solve_odd(): pl.pallas_call(solve_odd_kernel, in_specs=[pl.BlockSpec(memory_space=pltp...  1.87 us
  transfers between devices with their start and end apart: 18, of which 11 were waited for; matrix products, arithmetic and copies ran while one was open for 1% of the time, Pallas kernels for 5%

profile of v6, /device:TPU:0, one launch (start us, length us, event | category | flops | bytes accessed | tf_op | source)
XLA Modules:
  0.0 46.2 jit_solution(15759166988008105936)
XLA Ops:
  0.6 0.0 copy-start.3
  0.6 1.9 %solve_odd.1 = (bf16[5,128,256]{2,1,0:T(8,128)(2,1)S(1)}, bf16[128,256]{1,0:T(8,128)(2,1)S(1)}, bf16[4,256,256]{2,1,0:T(8,128)(2,1)S(1)}) custom-call(bf16[128,256]{1,0:T(8,128)(2,1)} %bitcast.35, bf16[2048,256]{1,0:T(8,128)(2,1)} %inverse_hbm.1), custom_call_target="tpu_custom_call" | custom-call | flops 67108864 | bytes 1572864 | tf_op jit(solution)/shard_map/solve_odd/pallas_call | solution.py:239
  2.5 0.4 collective-permute-start
  2.9 0.0 copy-done.3
  2.9 2.8 %collective-permute-start.11 = (bf16[64,256]{1,0:T(8,128)(2,1)S(1)}, bf16[64,256]{1,0:T(8,128)(2,1)S(1)}, u32[]{:S(2)}, u32[]{:S(2)}) collective-permute-start(bf16[64,256]{1,0:T(8,128)(2,1)S(1)} %bitcast.36), channel_id=1, source_target_pairs={{0,8},{1,9},{2,10},{3,11},{4,12},{5,13},{6,14},{7,15},{8,0},{9,1},... | collective-permute-start | bytes 98312 | tf_op jit(solution)/shard_map/ppermute | solution.py:777
  5.7 2.6 %collective-permute-start.12 = (bf16[64,256]{1,0:T(8,128)(2,1)S(1)}, bf16[64,256]{1,0:T(8,128)(2,1)S(1)}, u32[]{:S(2)}, u32[]{:S(2)}) collective-permute-start(bf16[64,256]{1,0:T(8,128)(2,1)S(1)} %bitcast.37), channel_id=1, source_target_pairs={{0,16},{1,17},{2,18},{3,19},{4,20},{5,21},{6,22},{7,23},{8,24},{9,... | collective-permute-start | bytes 98312 | tf_op jit(solution)/shard_map/ppermute | solution.py:777
  8.3 0.0 collective-permute-start.13
  8.3 0.0 collective-permute-done.11.refs_0_
  8.3 2.8 %collective-permute-done.12.refs_1_ = bf16[64,256]{1,0:T(8,128)(2,1)S(1)} collective-permute-done((bf16[64,256]{1,0:T(8,128)(2,1)S(1)}, bf16[64,256]{1,0:T(8,128)(2,1)S(1)}, u32[]{:S(2)}, u32[]{:S(2)}) %collective-permute-start.12) | collective-permute-done | bytes 32800 | tf_op jit(solution)/shard_map/ppermute | solution.py:777
  11.1 2.9 %collective-permute-done.13.refs_2_ = bf16[64,256]{1,0:T(8,128)(2,1)S(1)} collective-permute-done((bf16[64,256]{1,0:T(8,128)(2,1)S(1)}, bf16[64,256]{1,0:T(8,128)(2,1)S(1)}, u32[]{:S(2)}, u32[]{:S(2)}) %collective-permute-start.13) | collective-permute-done | bytes 32800 | tf_op jit(solution)/shard_map/ppermute | solution.py:777
  14.1 0.1 collective-permute-start.14
  14.2 2.1 %collective-permute-start.15 = (bf16[192,256]{1,0:T(8,128)(2,1)S(1)}, bf16[192,256]{1,0:T(8,128)(2,1)S(1)}, u32[]{:S(2)}, u32[]{:S(2)}) collective-permute-start(bf16[192,256]{1,0:T(8,128)(2,1)S(1)} %get-tuple-element.58), channel_id=1, source_target_pairs={{0,5},{1,4},{2,7},{3,6},{4,1},{5,0},{6,3},{7,2},{8,13},{9,12},{10,... | collective-permute-start | bytes 294920 | tf_op jit(solution)/shard_map/ppermute | solution.py:768
  16.3 0.4 collective-permute-start.16
  16.7 0.8 %solve_even.1.mine_ref = f32[4,128,256]{2,1,0:T(8,128)S(1)} custom-call(bf16[128,256]{1,0:T(8,128)(2,1)S(1)} %get-tuple-element.41.right_ref, bf16[4,256,256]{2,1,0:T(8,128)(2,1)S(1)} %get-tuple-element.42.even_ref), custom_call_target="tpu_custom_call" | custom-call | flops 67108864 | bytes 1048576 | tf_op jit(solution)/shard_map/solve_even/pallas_call | solution.py:271
  17.5 1.6 %collective-permute-done.14.refs_1_ = bf16[192,256]{1,0:T(8,128)(2,1)S(1)} collective-permute-done((bf16[192,256]{1,0:T(8,128)(2,1)S(1)}, bf16[192,256]{1,0:T(8,128)(2,1)S(1)}, u32[]{:S(2)}, u32[]{:S(2)}) %collective-permute-start.14) | collective-permute-done | bytes 98336 | tf_op jit(solution)/shard_map/ppermute | solution.py:768
  19.1 0.0 collective-permute-done.15.refs_2_
  19.1 2.8 %collective-permute-done.16.refs_3_ = bf16[192,256]{1,0:T(8,128)(2,1)S(1)} collective-permute-done((bf16[192,256]{1,0:T(8,128)(2,1)S(1)}, bf16[192,256]{1,0:T(8,128)(2,1)S(1)}, u32[]{:S(2)}, u32[]{:S(2)}) %collective-permute-start.16) | collective-permute-done | bytes 98336 | tf_op jit(solution)/shard_map/ppermute | solution.py:768
  21.9 0.1 collective-permute-start.17
  22.0 0.0 collective-permute-done.other_ref
  22.0 0.0 copy-start.4
  22.0 0.0 copy-start.1
  22.0 0.1 pair_add.2
  22.1 0.0 copy-start
  22.1 1.2 %collective-permute-start.1 = (bf16[128,256]{1,0:T(8,128)(2,1)S(1)}, bf16[128,256]{1,0:T(8,128)(2,1)S(1)}, u32[]{:S(2)}, u32[]{:S(2)}) collective-permute-start(bf16[128,256]{1,0:T(8,128)(2,1)S(1)} %get-tuple-element.45), channel_id=1, source_target_pairs={{0,3},{1,2},{2,1},{3,0},{4,7},{5,6},{6,5},{7,4},{8,11},{9,10},{10,... | collective-permute-start | bytes 196616 | tf_op jit(solution)/shard_map/ppermute | solution.py:768
  23.3 0.6 %collective-permute-start.2 = (bf16[128,256]{1,0:T(8,128)(2,1)S(1)}, bf16[128,256]{1,0:T(8,128)(2,1)S(1)}, u32[]{:S(2)}, u32[]{:S(2)}) collective-permute-start(bf16[128,256]{1,0:T(8,128)(2,1)S(1)} %get-tuple-element.46), channel_id=1, source_target_pairs={{0,5},{1,4},{2,7},{3,6},{4,1},{5,0},{6,3},{7,2},{8,13},{9,12},{10,... | collective-permute-start | bytes 196616 | tf_op jit(solution)/shard_map/ppermute | solution.py:768
  23.9 1.6 %collective-permute-start.3 = (bf16[128,256]{1,0:T(8,128)(2,1)S(1)}, bf16[128,256]{1,0:T(8,128)(2,1)S(1)}, u32[]{:S(2)}, u32[]{:S(2)}) collective-permute-start(bf16[128,256]{1,0:T(8,128)(2,1)S(1)} %get-tuple-element.47), channel_id=1, source_target_pairs={{0,7},{1,6},{2,5},{3,4},{4,3},{5,2},{6,1},{7,0},{8,15},{9,14},{10,... | collective-permute-start | bytes 196616 | tf_op jit(solution)/shard_map/ppermute | solution.py:768
  25.4 0.0 copy-done.4
  25.4 0.1 fusion
  25.5 0.1 reshape.78
  25.6 0.3 collective-permute-done.1.refs_0_
  25.9 1.5 %collective-permute-done.2.refs_1_ = bf16[128,256]{1,0:T(8,128)(2,1)S(1)} collective-permute-done((bf16[128,256]{1,0:T(8,128)(2,1)S(1)}, bf16[128,256]{1,0:T(8,128)(2,1)S(1)}, u32[]{:S(2)}, u32[]{:S(2)}) %collective-permute-start.2) | collective-permute-done | bytes 65568 | tf_op jit(solution)/shard_map/ppermute | solution.py:768
  27.5 1.0 %collective-permute-done.3.refs_2_ = bf16[128,256]{1,0:T(8,128)(2,1)S(1)} collective-permute-done((bf16[128,256]{1,0:T(8,128)(2,1)S(1)}, bf16[128,256]{1,0:T(8,128)(2,1)S(1)}, u32[]{:S(2)}, u32[]{:S(2)}) %collective-permute-start.3) | collective-permute-done | bytes 65568 | tf_op jit(solution)/shard_map/ppermute | solution.py:768
  28.5 0.1 broadcast_in_dim.6.mask_ref
  28.6 0.1 collective-permute-start.4
  28.7 0.7 %collective-permute-start.5 = (bf16[64,256]{1,0:T(8,128)(2,1)S(1)}, bf16[64,256]{1,0:T(8,128)(2,1)S(1)}, u32[]{:S(2)}, u32[]{:S(2)}) collective-permute-start(bf16[64,256]{1,0:T(8,128)(2,1)S(1)} %get-tuple-element.49), channel_id=1, source_target_pairs={{0,17},{1,16},{2,19},{3,18},{4,21},{5,20},{6,23},{7,22},{8,25},{9,... | collective-permute-start | bytes 98312 | tf_op jit(solution)/shard_map/ppermute | solution.py:777
  29.4 3.4 %collective-permute-start.6 = (bf16[64,256]{1,0:T(8,128)(2,1)S(1)}, bf16[64,256]{1,0:T(8,128)(2,1)S(1)}, u32[]{:S(2)}, u32[]{:S(2)}) collective-permute-start(bf16[64,256]{1,0:T(8,128)(2,1)S(1)} %get-tuple-element.49), channel_id=1, source_target_pairs={{0,24},{1,25},{2,26},{3,27},{4,28},{5,29},{6,30},{7,31},{8,16},{9,... | collective-permute-start | bytes 98312 | tf_op jit(solution)/shard_map/ppermute | solution.py:777
  32.8 0.0 collective-permute-done.4.refs_0_
  32.8 0.2 collective-permute-done.5.refs_1_
  33.0 2.5 %collective-permute-done.6.refs_2_ = bf16[64,256]{1,0:T(8,128)(2,1)S(1)} collective-permute-done((bf16[64,256]{1,0:T(8,128)(2,1)S(1)}, bf16[64,256]{1,0:T(8,128)(2,1)S(1)}, u32[]{:S(2)}, u32[]{:S(2)}) %collective-permute-start.6) | collective-permute-done | bytes 32800 | tf_op jit(solution)/shard_map/ppermute | solution.py:777
  35.6 0.0 copy-start.5
  35.6 0.2 core_parts.1
  35.8 0.0 copy-start.2
  35.8 0.1 collective-permute-start.7
  35.8 0.4 copy-done.5
  36.2 0.1 fusion.1
  36.3 0.1 reshape.79
  36.4 0.7 %collective-permute-done.7.other_ref = f32[4,32,128]{2,1,0:T(8,128)S(1)} collective-permute-done((f32[4,32,128]{2,1,0:T(8,128)S(1)}, f32[4,32,128]{2,1,0:T(8,128)S(1)}, u32[]{:S(2)}, u32[]{:S(2)}) %collective-permute-start.7) | collective-permute-done | bytes 65568 | tf_op jit(solution)/shard_map/ppermute | solution.py:768
  37.1 1.0 %collective-permute-start.8 = (f32[32,128]{1,0:T(8,128)S(1)}, f32[32,128]{1,0:T(8,128)S(1)}, u32[]{:S(2)}, u32[]{:S(2)}) collective-permute-start(f32[32,128]{1,0:T(8,128)S(1)} %get-tuple-element.53), channel_id=1, source_target_pairs={{0,3},{1,2},{2,1},{3,0},{4,7},{5,6},{6,5},{7,4},{8,11},{9,10},{10,... | collective-permute-start | bytes 49160 | tf_op jit(solution)/shard_map/ppermute | solution.py:768
  38.1 0.9 %collective-permute-start.9 = (f32[32,128]{1,0:T(8,128)S(1)}, f32[32,128]{1,0:T(8,128)S(1)}, u32[]{:S(2)}, u32[]{:S(2)}) collective-permute-start(f32[32,128]{1,0:T(8,128)S(1)} %get-tuple-element.54), channel_id=1, source_target_pairs={{0,5},{1,4},{2,7},{3,6},{4,1},{5,0},{6,3},{7,2},{8,13},{9,12},{10,... | collective-permute-start | bytes 49160 | tf_op jit(solution)/shard_map/ppermute | solution.py:768
  39.0 1.2 %collective-permute-start.10 = (f32[32,128]{1,0:T(8,128)S(1)}, f32[32,128]{1,0:T(8,128)S(1)}, u32[]{:S(2)}, u32[]{:S(2)}) collective-permute-start(f32[32,128]{1,0:T(8,128)S(1)} %get-tuple-element.55), channel_id=1, source_target_pairs={{0,7},{1,6},{2,5},{3,4},{4,3},{5,2},{6,1},{7,0},{8,15},{9,14},{10,... | collective-permute-start | bytes 49160 | tf_op jit(solution)/shard_map/ppermute | solution.py:768
  40.1 0.1 broadcast_in_dim.7.refs_4_
  40.2 0.0 copy-done.1
  40.2 0.0 copy-done
  40.2 0.0 copy-done.2
  40.3 0.8 %early_grams.1 = (bf16[128,128]{1,0:T(8,128)(2,1)S(1)}, bf16[128,128]{1,0:T(8,128)(2,1)S(1)}, f32[128,128]{1,0:T(8,128)S(1)}, f32[32,128]{1,0:T(8,128)S(1)}, f32...) custom-call(bf16[128,2048]{1,0:T(8,128)(2,1)S(1)} %bitcast.25, ...), custom_call_target="tpu_custom_call" | custom-call | flops 335544320 | bytes 1000000 | tf_op jit(solution)/shard_map/early_grams/pallas_call | solution.py:490
  41.1 0.0 collective-permute-done.17.refs_3_.refs_18_
  41.1 0.4 late_grams.1
  41.5 0.0 collective-permute-done.8.refs_1_
  41.5 0.0 collective-permute-done.9.refs_2_
  41.5 1.5 %collective-permute-done.10.refs_3_ = f32[32,128]{1,0:T(8,128)S(1)} collective-permute-done((f32[32,128]{1,0:T(8,128)S(1)}, f32[32,128]{1,0:T(8,128)S(1)}, u32[]{:S(2)}, u32[]{:S(2)}) %collective-permute-start.10) | collective-permute-done | bytes 16416 | tf_op jit(solution)/shard_map/ppermute | solution.py:768
  43.0 3.2 %finish.1 = (bf16[128,2048]{1,0:T(8,128)(2,1)}, bf16[128,2048]{1,0:T(8,128)(2,1)}) custom-call(f32[32,128]{1,0:T(8,128)S(1)} %get-tuple-element.52.refs_0_, f32[32,128]{1,0:T(8,128)S(1)} %collective-permute-done.8.refs_1_, f32[32,128]{1,0:T(8,128)S(1)} %collective-permute-done.9.refs_2_, f32[32,128]{1,0:T(8,128)S(1)} %collective-permute-done.10.refs_3_, ...), custom_call_target="tpu_custom_call" | custom-call | flops 1000000000 | bytes 5000000 | tf_op jit(solution)/shard_map/finish/pallas_call | solution.py:735
  (6 shorter events, 0.1 us)
Async XLA Ops:
  0.6 2.3 %copy-start.3 = (bf16[4,256,32]{1,2,0:T(8,128)(2,1)S(1)}, bf16[4,256,32]{1,2,0:T(8,128)(2,1)}, u32[]{:S(2)}) copy-start(bf16[4,256,32]{1,2,0:T(8,128)(2,1)} %param.11) | copy-start | bytes 196612
  2.5 19.5 %collective-permute-start = (bf16[5,128,256]{2,1,0:T(8,128)(2,1)S(1)}, bf16[5,128,256]{2,1,0:T(8,128)(2,1)S(1)}, u32[]{:S(2)}, u32[]{:S(2)}) collective-permute-start(bf16[5,128,256]{2,1,0:T(8,128)(2,1)S(1)} %get-tuple-element.43), channel_id=1, source_target_pairs={{0,1},{1,0},{2,3},{3,2},{4,5},{5,4},{6,7},{7,6},{8,9},{9,8},{10,11... | collective-permute-start | bytes 983048 | tf_op jit(solution)/shard_map/ppermute | solution.py:768
  2.9 5.4 %collective-permute-start.11 = (bf16[64,256]{1,0:T(8,128)(2,1)S(1)}, bf16[64,256]{1,0:T(8,128)(2,1)S(1)}, u32[]{:S(2)}, u32[]{:S(2)}) collective-permute-start(bf16[64,256]{1,0:T(8,128)(2,1)S(1)} %bitcast.36), channel_id=1, source_target_pairs={{0,8},{1,9},{2,10},{3,11},{4,12},{5,13},{6,14},{7,15},{8,0},{9,1},... | collective-permute-start | bytes 98312 | tf_op jit(solution)/shard_map/ppermute | solution.py:777
  5.7 5.4 %collective-permute-start.12 = (bf16[64,256]{1,0:T(8,128)(2,1)S(1)}, bf16[64,256]{1,0:T(8,128)(2,1)S(1)}, u32[]{:S(2)}, u32[]{:S(2)}) collective-permute-start(bf16[64,256]{1,0:T(8,128)(2,1)S(1)} %bitcast.37), channel_id=1, source_target_pairs={{0,16},{1,17},{2,18},{3,19},{4,20},{5,21},{6,22},{7,23},{8,24},{9,... | collective-permute-start | bytes 98312 | tf_op jit(solution)/shard_map/ppermute | solution.py:777
  8.3 5.7 %collective-permute-start.13 = (bf16[64,256]{1,0:T(8,128)(2,1)S(1)}, bf16[64,256]{1,0:T(8,128)(2,1)S(1)}, u32[]{:S(2)}, u32[]{:S(2)}) collective-permute-start(bf16[64,256]{1,0:T(8,128)(2,1)S(1)} %bitcast.38), channel_id=1, source_target_pairs={{0,24},{1,25},{2,26},{3,27},{4,28},{5,29},{6,30},{7,31},{8,16},{9,... | collective-permute-start | bytes 98312 | tf_op jit(solution)/shard_map/ppermute | solution.py:777
  14.1 5.0 %collective-permute-start.14 = (bf16[192,256]{1,0:T(8,128)(2,1)S(1)}, bf16[192,256]{1,0:T(8,128)(2,1)S(1)}, u32[]{:S(2)}, u32[]{:S(2)}) collective-permute-start(bf16[192,256]{1,0:T(8,128)(2,1)S(1)} %get-tuple-element.57), channel_id=1, source_target_pairs={{0,3},{1,2},{2,1},{3,0},{4,7},{5,6},{6,5},{7,4},{8,11},{9,10},{10,... | collective-permute-start | bytes 294920 | tf_op jit(solution)/shard_map/ppermute | solution.py:768
  14.2 4.9 %collective-permute-start.15 = (bf16[192,256]{1,0:T(8,128)(2,1)S(1)}, bf16[192,256]{1,0:T(8,128)(2,1)S(1)}, u32[]{:S(2)}, u32[]{:S(2)}) collective-permute-start(bf16[192,256]{1,0:T(8,128)(2,1)S(1)} %get-tuple-element.58), channel_id=1, source_target_pairs={{0,5},{1,4},{2,7},{3,6},{4,1},{5,0},{6,3},{7,2},{8,13},{9,12},{10,... | collective-permute-start | bytes 294920 | tf_op jit(solution)/shard_map/ppermute | solution.py:768
  16.3 5.6 %collective-permute-start.16 = (bf16[192,256]{1,0:T(8,128)(2,1)S(1)}, bf16[192,256]{1,0:T(8,128)(2,1)S(1)}, u32[]{:S(2)}, u32[]{:S(2)}) collective-permute-start(bf16[192,256]{1,0:T(8,128)(2,1)S(1)} %get-tuple-element.59), channel_id=1, source_target_pairs={{0,7},{1,6},{2,5},{3,4},{4,3},{5,2},{6,1},{7,0},{8,15},{9,14},{10,... | collective-permute-start | bytes 294920 | tf_op jit(solution)/shard_map/ppermute | solution.py:768
  21.9 19.2 %collective-permute-start.17 = (bf16[4,160,256]{2,1,0:T(8,128)(2,1)S(1)}, bf16[4,160,256]{2,1,0:T(8,128)(2,1)S(1)}, u32[]{:S(2)}, u32[]{:S(2)}) collective-permute-start(bf16[4,160,256]{2,1,0:T(8,128)(2,1)S(1)} %get-tuple-element.65), channel_id=1, source_target_pairs={{0,1},{1,0},{2,3},{3,2},{4,5},{5,4},{6,7},{7,6},{8,9},{9,8},{10,11... | collective-permute-start | bytes 983048 | tf_op jit(solution)/shard_map/ppermute | solution.py:768
  22.0 3.4 %copy-start.4 = (s32[4]{0:T(128)S(1)}, s32[4]{0:T(128)}, u32[]{:S(2)}) copy-start(s32[4]{0:T(128)} %param.13) | copy-start | bytes 52
  22.0 18.2 %copy-start.1 = (bf16[4,1,2048,32]{2,3,1,0:T(8,128)(2,1)S(1)}, bf16[4,1,2048,32]{2,3,1,0:T(8,128)(2,1)}, u32[]{:S(2)}) copy-start(bf16[4,1,2048,32]{2,3,1,0:T(8,128)(2,1)} %param.9) | copy-start | bytes 1572868
  22.1 18.1 %copy-start = (bf16[4,1,2048,32]{2,3,1,0:T(8,128)(2,1)S(1)}, bf16[4,1,2048,32]{2,3,1,0:T(8,128)(2,1)}, u32[]{:S(2)}) copy-start(bf16[4,1,2048,32]{2,3,1,0:T(8,128)(2,1)} %param.8) | copy-start | bytes 1572868
  22.1 3.8 %collective-permute-start.1 = (bf16[128,256]{1,0:T(8,128)(2,1)S(1)}, bf16[128,256]{1,0:T(8,128)(2,1)S(1)}, u32[]{:S(2)}, u32[]{:S(2)}) collective-permute-start(bf16[128,256]{1,0:T(8,128)(2,1)S(1)} %get-tuple-element.45), channel_id=1, source_target_pairs={{0,3},{1,2},{2,1},{3,0},{4,7},{5,6},{6,5},{7,4},{8,11},{9,10},{10,... | collective-permute-start | bytes 196616 | tf_op jit(solution)/shard_map/ppermute | solution.py:768
  23.3 4.2 %collective-permute-start.2 = (bf16[128,256]{1,0:T(8,128)(2,1)S(1)}, bf16[128,256]{1,0:T(8,128)(2,1)S(1)}, u32[]{:S(2)}, u32[]{:S(2)}) collective-permute-start(bf16[128,256]{1,0:T(8,128)(2,1)S(1)} %get-tuple-element.46), channel_id=1, source_target_pairs={{0,5},{1,4},{2,7},{3,6},{4,1},{5,0},{6,3},{7,2},{8,13},{9,12},{10,... | collective-permute-start | bytes 196616 | tf_op jit(solution)/shard_map/ppermute | solution.py:768
  23.9 4.6 %collective-permute-start.3 = (bf16[128,256]{1,0:T(8,128)(2,1)S(1)}, bf16[128,256]{1,0:T(8,128)(2,1)S(1)}, u32[]{:S(2)}, u32[]{:S(2)}) collective-permute-start(bf16[128,256]{1,0:T(8,128)(2,1)S(1)} %get-tuple-element.47), channel_id=1, source_target_pairs={{0,7},{1,6},{2,5},{3,4},{4,3},{5,2},{6,1},{7,0},{8,15},{9,14},{10,... | collective-permute-start | bytes 196616 | tf_op jit(solution)/shard_map/ppermute | solution.py:768
  28.6 4.2 %collective-permute-start.4 = (bf16[64,256]{1,0:T(8,128)(2,1)S(1)}, bf16[64,256]{1,0:T(8,128)(2,1)S(1)}, u32[]{:S(2)}, u32[]{:S(2)}) collective-permute-start(bf16[64,256]{1,0:T(8,128)(2,1)S(1)} %get-tuple-element.49), channel_id=1, source_target_pairs={{0,9},{1,8},{2,11},{3,10},{4,13},{5,12},{6,15},{7,14},{8,1},{9,0},... | collective-permute-start | bytes 98312 | tf_op jit(solution)/shard_map/ppermute | solution.py:777
  28.7 4.3 %collective-permute-start.5 = (bf16[64,256]{1,0:T(8,128)(2,1)S(1)}, bf16[64,256]{1,0:T(8,128)(2,1)S(1)}, u32[]{:S(2)}, u32[]{:S(2)}) collective-permute-start(bf16[64,256]{1,0:T(8,128)(2,1)S(1)} %get-tuple-element.49), channel_id=1, source_target_pairs={{0,17},{1,16},{2,19},{3,18},{4,21},{5,20},{6,23},{7,22},{8,25},{9,... | collective-permute-start | bytes 98312 | tf_op jit(solution)/shard_map/ppermute | solution.py:777
  29.4 6.2 %collective-permute-start.6 = (bf16[64,256]{1,0:T(8,128)(2,1)S(1)}, bf16[64,256]{1,0:T(8,128)(2,1)S(1)}, u32[]{:S(2)}, u32[]{:S(2)}) collective-permute-start(bf16[64,256]{1,0:T(8,128)(2,1)S(1)} %get-tuple-element.49), channel_id=1, source_target_pairs={{0,24},{1,25},{2,26},{3,27},{4,28},{5,29},{6,30},{7,31},{8,16},{9,... | collective-permute-start | bytes 98312 | tf_op jit(solution)/shard_map/ppermute | solution.py:777
  35.6 0.7 %copy-start.5 = (s32[4,1]{0,1:T(1,128)S(1)}, s32[4,1]{0,1:T(1,128)}, u32[]{:S(2)}) copy-start(s32[4,1]{0,1:T(1,128)} %param.10) | copy-start | bytes 52
  35.8 4.5 %copy-start.2 = (bf16[2048,32]{0,1:T(8,128)(2,1)S(1)}, bf16[2048,32]{0,1:T(8,128)(2,1)}, u32[]{:S(2)}) copy-start(bf16[2048,32]{0,1:T(8,128)(2,1)} %param.15) | copy-start | bytes 393220
  35.8 1.3 %collective-permute-start.7 = (f32[4,32,128]{2,1,0:T(8,128)S(1)}, f32[4,32,128]{2,1,0:T(8,128)S(1)}, u32[]{:S(2)}, u32[]{:S(2)}) collective-permute-start(f32[4,32,128]{2,1,0:T(8,128)S(1)} %get-tuple-element.51), channel_id=1, source_target_pairs={{0,1},{1,0},{2,3},{3,2},{4,5},{5,4},{6,7},{7,6},{8,9},{9,8},{10,11... | collective-permute-start | bytes 196616 | tf_op jit(solution)/shard_map/ppermute | solution.py:768
  37.1 4.4 %collective-permute-start.8 = (f32[32,128]{1,0:T(8,128)S(1)}, f32[32,128]{1,0:T(8,128)S(1)}, u32[]{:S(2)}, u32[]{:S(2)}) collective-permute-start(f32[32,128]{1,0:T(8,128)S(1)} %get-tuple-element.53), channel_id=1, source_target_pairs={{0,3},{1,2},{2,1},{3,0},{4,7},{5,6},{6,5},{7,4},{8,11},{9,10},{10,... | collective-permute-start | bytes 49160 | tf_op jit(solution)/shard_map/ppermute | solution.py:768
  38.1 3.4 %collective-permute-start.9 = (f32[32,128]{1,0:T(8,128)S(1)}, f32[32,128]{1,0:T(8,128)S(1)}, u32[]{:S(2)}, u32[]{:S(2)}) collective-permute-start(f32[32,128]{1,0:T(8,128)S(1)} %get-tuple-element.54), channel_id=1, source_target_pairs={{0,5},{1,4},{2,7},{3,6},{4,1},{5,0},{6,3},{7,2},{8,13},{9,12},{10,... | collective-permute-start | bytes 49160 | tf_op jit(solution)/shard_map/ppermute | solution.py:768
  39.0 4.1 %collective-permute-start.10 = (f32[32,128]{1,0:T(8,128)S(1)}, f32[32,128]{1,0:T(8,128)S(1)}, u32[]{:S(2)}, u32[]{:S(2)}) collective-permute-start(f32[32,128]{1,0:T(8,128)S(1)} %get-tuple-element.55), channel_id=1, source_target_pairs={{0,7},{1,6},{2,5},{3,4},{4,3},{5,2},{6,1},{7,0},{8,15},{9,14},{10,... | collective-permute-start | bytes 49160 | tf_op jit(solution)/shard_map/ppermute | solution.py:768
